TPU v7x, 256 devices: a whole 4x4x8 slice. The times are simulated.
256 devices in a mesh: space: 16 (over z, x_lo), vel: 16 (over y, x_hi, core).
Axes of the slice: x: 4 (x_hi: 2, x_lo: 2; x = x_hi * 2 + x_lo), y: 4, z: 8, core: 2. Of those that a mesh axis runs over, the one named last changes fastest.
Arguments:
- velocity_dist: bfloat16 [32768, 4096], P('vel', 'space'), may hold values from -6 to 6
- macro_state: float32 [13, 4096], P(None, ('space', 'vel')), may hold values from -2 to 2
- collision_rate: float32 [4096], P('space'), may hold values from 0.25 to 2
- wall_flags: int32 [4096], P('space'), may hold values 0 or 1
- diffusivity: float32 [13], replicated, may hold values from 0.5 to 8
- coupling: float32 [13, 13], replicated, may hold values from -0.25 to 4.5, as said below
Outputs:
- dist_out: bfloat16 [32768, 4096], P('vel', 'space')
- macro_out: float32 [13, 4096], P(None, ('space', 'vel'))
Inputs may be any that keep to these rules, and one draw needn't show every extreme that they name: `coupling`: symmetric, with each diagonal entry larger than the sum of magnitudes of the other entries of its row.
All inputs are finite; a program needn't handle non-finite values. No bound on the sum of `wall_flags` on one device may be relied on, other than what follows from the above.
Results may differ from a plain program's by a relative error of at most 0.001.
Values sent between devices are 32-bit elements; how exact they have to be, the bound alone decides.
No kernel may reach another device: no remote copies, remote signals or barrier semaphores. Data moves between devices by JAX's collectives and lax.ppermute only.
A program may use at most 64 MiB of HBM per device.

v0:
```python
import math

import jax
import jax.numpy as jnp
from jax import lax
from jax.sharding import PartitionSpec as P

NV1 = 32
ITERS = 3
SWEEPS = 2


highest = lax.Precision.HIGHEST
speed_limit = 4.0
time_step = 0.125
shakhov_weights = (
    1.0,
    1.0,
    1.0,
    1.0,
    1.0,
    0.0,
    0.0,
    0.0,
    0.0,
    0.0,
    1.0 / 3.0,
    1.0 / 3.0,
    1.0 / 3.0,
)


def sent_to_all(x, axis):
    copies = jnp.broadcast_to(x, (lax.axis_size(axis), *x.shape))
    return lax.all_to_all(copies, axis, split_axis=0, concat_axis=0, tiled=True)


def in_order(blocks, dim):
    blocks = jnp.moveaxis(blocks, 0, dim)
    lengths = blocks.shape
    return blocks.reshape(*lengths[:dim], lengths[dim] * lengths[dim + 1], *lengths[dim + 2 :])


def gather_directly(x, axis, dim):
    blocks = sent_to_all(x, axis)
    return in_order(blocks, dim)


def padded_2(x, sides, width):
    for axis, dim in sides:
        devices, length = (lax.axis_size(axis), x.shape[dim])
        up = [(i, (i + 1) % devices) for i in range(devices - 1)]
        down = [(j, i) for i, j in up]
        last = lax.slice_in_dim(x, length - width, length, axis=dim)
        first = lax.slice_in_dim(x, 0, width, axis=dim)
        before = lax.ppermute(last, axis, up)
        after = lax.ppermute(first, axis, down)
        x = jnp.concatenate([before, x, after], axis=dim)
    return x


def of_everyone(x, axis):
    everything = sent_to_all(x, axis)
    return jnp.sum(everything, axis=0)


def velocity_table(first_row, number):
    indices = first_row + jnp.arange(number, dtype=jnp.int32)
    first_index = indices // (NV1 * NV1)
    second_index = indices // NV1 % NV1
    third_index = indices % NV1
    spacing = 2.0 * speed_limit / NV1
    speed_x = (first_index.astype(jnp.float32) + 0.5) * spacing - speed_limit
    speed_y = (second_index.astype(jnp.float32) + 0.5) * spacing - speed_limit
    speed_z = (third_index.astype(jnp.float32) + 0.5) * spacing - speed_limit
    speed_square = speed_x * speed_x + speed_y * speed_y + speed_z * speed_z
    weight = jnp.exp(-0.5 * speed_square) * (spacing**3 / (2.0 * math.pi) ** 1.5)
    return (speed_x, speed_y, speed_z, weight)


def moment_basis(speed_x, speed_y, speed_z):
    speed_square = speed_x * speed_x + speed_y * speed_y + speed_z * speed_z
    entries = [
        jnp.ones_like(speed_x),
        speed_x,
        speed_y,
        speed_z,
        (speed_square - 3.0) / math.sqrt(6.0),
        speed_x * speed_y,
        speed_x * speed_z,
        speed_y * speed_z,
        0.5 * (speed_x * speed_x - speed_y * speed_y),
        (speed_x * speed_x + speed_y * speed_y - 2.0 * speed_z * speed_z) / math.sqrt(12.0),
        speed_x * (speed_square - 5.0) / math.sqrt(10.0),
        speed_y * (speed_square - 5.0) / math.sqrt(10.0),
        speed_z * (speed_square - 5.0) / math.sqrt(10.0),
    ]
    return jnp.stack(entries)


def apply_operator(moments, padded, diffusivity, coupling):
    second_diff = 2.0 * moments - padded[:, :-2] - padded[:, 2:]
    return jnp.dot(coupling, moments, precision=highest) + diffusivity[:, None] * second_diff


def synthetic_whole(residual, diffusivity, coupling):
    result = jnp.zeros_like(residual)
    for repeat in range(SWEEPS):
        padded = jnp.pad(residual, ((0, 0), (1, 1)))
        applied = apply_operator(residual, padded, diffusivity, coupling)
        step_size = jnp.sum(residual * residual) / jnp.sum(residual * applied)
        result = result + step_size * residual
        residual = residual - step_size * applied
    return result


def per_device(velocity_dist, macro_state, collision_rate, wall_flags, diffusivity, coupling):
    local_velocities = velocity_dist.shape[0]
    cell_count = velocity_dist.shape[1]
    first_row = lax.axis_index("vel") * local_velocities
    speed_x, speed_y, speed_z, weight = velocity_table(first_row, local_velocities)
    basis_rows = moment_basis(speed_x, speed_y, speed_z)
    moment_rows = basis_rows * weight[None, :]
    equilibrium_rows = basis_rows * jnp.array(shakhov_weights, dtype=jnp.float32)[:, None]
    relax_rate = time_step * collision_rate * (1.0 + wall_flags.astype(jnp.float32))
    transport = (time_step * speed_x)[:, None]
    upwind = (speed_x > 0.0)[:, None]
    distribution = velocity_dist.astype(jnp.float32)
    current = gather_directly(macro_state, "vel", 1)
    for iteration in range(ITERS):
        equilibrium = jnp.dot(equilibrium_rows.T, current, precision=highest)
        padded = padded_2(distribution, (("space", 1),), 1)
        gradient = jnp.where(upwind, distribution - padded[:, :-2], padded[:, 2:] - distribution)
        advanced = (
            distribution - transport * gradient + relax_rate[None, :] * (equilibrium - distribution)
        )
        partial_value = jnp.dot(moment_rows, advanced, precision=highest)
        shares = of_everyone(partial_value, "vel")
        whole_residual = gather_directly(shares - current, "space", 1)
        whole_correction = synthetic_whole(whole_residual, diffusivity, coupling)
        spread = lax.dynamic_slice_in_dim(
            whole_correction, lax.axis_index("space") * cell_count, cell_count, 1
        )
        current = shares + spread
        distribution = advanced + jnp.dot(basis_rows.T, spread, precision=highest)
    share_width = cell_count // lax.axis_size("vel")
    final_owned = lax.dynamic_slice_in_dim(
        current, lax.axis_index("vel") * share_width, share_width, 1
    )
    return (distribution.astype(jnp.bfloat16), final_owned)


def solution(mesh):
    placed = (P("vel", "space"), P(None, ("space", "vel")), P("space"), P("space"), P(), P())
    return jax.shard_map(
        per_device,
        mesh=mesh,
        in_specs=placed,
        out_specs=(P("vel", "space"), P(None, ("space", "vel"))),
        check_vma=False,
    )
```

profile of v0, /device:TPU:2, one launch (start us, length us, event | category | flops | bytes accessed | tf_op | source)
XLA Modules:
  0.0 178.5 jit_solution(97320134992492643)
XLA Ops:
  2.1 6.1 %all-to-all-start = ((f32[16,1,208]{2,1,0:T(1,128)}), f32[16,1,208]{2,1,0:T(1,128)S(1)}, u32[]{:S(2)}, u32[]{:S(2)}) async-start(f32[16,1,208]{2,1,0:T(1,128)} %reshape.305), calls=%async_computation | async-start | bytes 32768 | tf_op jit(solution)/shard_map/all_to_all | solution.py:35
  8.3 1.5 copy.29
  9.8 4.7 %collective-permute-start = (f32[2048,1]{0,1:T(1,128)S(1)}, f32[2048,1]{0,1:T(1,128)S(1)}, u32[]{:S(2)}, u32[]{:S(2)}) collective-permute-start(f32[2048,1]{0,1:T(1,128)S(1)} %get-tuple-element.20), channel_id=1, source_target_pairs={{0,16},{16,32},{32,48},{48,64},{64,80},{80,96},{96,112},{112,128},... | collective-permute-start | bytes 24584 | tf_op jit(solution)/shard_map/ppermute | solution.py:56
  14.5 1.9 %collective-permute-start.1 = (f32[2048,1]{0,1:T(1,128)S(1)}, f32[2048,1]{0,1:T(1,128)S(1)}, u32[]{:S(2)}, u32[]{:S(2)}) collective-permute-start(f32[2048,1]{0,1:T(1,128)S(1)} %get-tuple-element.21), channel_id=1, source_target_pairs={{16,0},{32,16},{48,32},{64,48},{80,64},{96,80},{112,96},{128,112},... | collective-permute-start | bytes 24584 | tf_op jit(solution)/shard_map/ppermute | solution.py:57
  17.5 1.6 convert_element_type.160
  20.9 5.5 %fusion.12 = f32[2048,256]{0,1:T(8,128)S(1)} fusion(f32[2048,256]{0,1:T(8,128)} %convert_element_type.160, f32[13,256]{1,0:T(8,128)S(1)} %reshape.301, f32[2048,1]{0,1:T(1,128)S(1)} %collective-permute-done.1, f32[2048,1]{0,1:T(1,128)S(1)} %collective-permute-done, f32[256]{0:T(256)S(1)} %add_multiply_fusion.1, f32[2048]{0:T(1024)S(1)} %get-tuple-element.29, ...), kind=kOutput, calls=%fused_computation.24 | convolution fusion | flops 87058432 | bytes 4341812 | tf_op jit(solution)/shard_map/dot_general | solution.py:131
  26.5 1.7 fusion.38
  28.2 15.9 %all_to_all.35 = f32[16,13,256]{2,1,0:T(8,128)S(1)} all-to-all(f32[16,13,256]{2,1,0:T(8,128)S(1)} %broadcast_in_dim.50), channel_id=1, replica_groups=mesh['space'=16,'vel'=16] {'vel'}, dimensions={0} | all-to-all | bytes 425984 | tf_op jit(solution)/shard_map/all_to_all | solution.py:35
  45.0 11.7 %all-to-all-start.2 = ((f32[16,13,256]{2,1,0:T(8,128)}), f32[16,13,256]{2,1,0:T(8,128)S(1)}, u32[]{:S(2)}, u32[]{:S(2)}) async-start(f32[16,13,256]{2,1,0:T(8,128)} %broadcast_in_dim.51), calls=%async_computation.2 | async-start | bytes 524288 | tf_op jit(solution)/shard_map/all_to_all | solution.py:35
  56.6 10.3 %all-to-all-done.2 = f32[16,13,256]{2,1,0:T(8,128)S(1)} async-done(((f32[16,13,256]{2,1,0:T(8,128)}), f32[16,13,256]{2,1,0:T(8,128)S(1)}, u32[]{:S(2)}, u32[]{:S(2)}) %all-to-all-start.2) | async-done | bytes 213024 | tf_op jit(solution)/shard_map/all_to_all | solution.py:35
  67.2 1.0 multiply_reduce_fusion.7
  73.3 1.9 %convolution_add_fusion.2 = f32[2048,256]{0,1:T(8,128)S(1)} fusion(f32[2048,256]{0,1:T(8,128)S(1)} %fusion.12, f32[13,2048]{1,0:T(8,128)S(1)} %stack.2, f32[13,4096]{1,0:T(8,128)S(1)} %get-tuple-element.15, s32[]{:T(128)S(6)} %select_n.225, f32[13,4096]{1,0:T(8,128)S(1)} %bitcast.79, f32[]{:T(128)S(6)} %div.101, f32[]{:T(128)S(6)} %div.100), kind=kOutput, calls=%fused_computation.21 | convolution fusion | flops 82323200 | bytes 4358156 | tf_op jit(solution)/shard_map/dot_general | solution.py:145
  75.2 3.6 %collective-permute-start.2 = (f32[2048,1]{0,1:T(1,128)S(1)}, f32[2048,1]{0,1:T(1,128)S(1)}, u32[]{:S(2)}, u32[]{:S(2)}) collective-permute-start(f32[2048,1]{0,1:T(1,128)S(1)} %get-tuple-element.18), channel_id=1, source_target_pairs={{0,16},{16,32},{32,48},{48,64},{64,80},{80,96},{96,112},{112,128},... | collective-permute-start | bytes 24584 | tf_op jit(solution)/shard_map/ppermute | solution.py:56
  78.8 2.5 %collective-permute-start.3 = (f32[2048,1]{0,1:T(1,128)S(1)}, f32[2048,1]{0,1:T(1,128)S(1)}, u32[]{:S(2)}, u32[]{:S(2)}) collective-permute-start(f32[2048,1]{0,1:T(1,128)S(1)} %get-tuple-element.19), channel_id=1, source_target_pairs={{16,0},{32,16},{48,32},{64,48},{80,64},{96,80},{112,96},{128,112},... | collective-permute-start | bytes 24584 | tf_op jit(solution)/shard_map/ppermute | solution.py:57
  81.3 4.0 %collective-permute-done.3 = f32[2048,1]{0,1:T(1,128)S(1)} collective-permute-done((f32[2048,1]{0,1:T(1,128)S(1)}, f32[2048,1]{0,1:T(1,128)S(1)}, u32[]{:S(2)}, u32[]{:S(2)}) %collective-permute-start.3) | collective-permute-done | bytes 8224 | tf_op jit(solution)/shard_map/ppermute | solution.py:57
  85.2 2.6 %fusion.13 = f32[2048,256]{0,1:T(8,128)S(1)} fusion(f32[2048,256]{0,1:T(8,128)S(1)} %convolution_add_fusion.2, f32[13,256]{1,0:T(8,128)S(1)} %fusion.92, f32[2048,1]{0,1:T(1,128)S(1)} %collective-permute-done.3, f32[2048,1]{0,1:T(1,128)S(1)} %collective-permute-done.2, f32[256]{0:T(256)S(1)} %add_multiply_fusion.1, f32[2048]{0:T(1024)S(1)} %get-tuple-element.29, ...), kind=kOutput, calls=%fused_computation.25 | convolution fusion | flops 87058432 | bytes 4341812 | tf_op jit(solution)/shard_map/dot_general | solution.py:131
  87.8 1.7 fusion.36
  89.6 12.1 %all_to_all.36 = f32[16,13,256]{2,1,0:T(8,128)S(1)} all-to-all(f32[16,13,256]{2,1,0:T(8,128)S(1)} %broadcast_in_dim.52), channel_id=1, replica_groups=mesh['space'=16,'vel'=16] {'vel'}, dimensions={0} | all-to-all | bytes 425984 | tf_op jit(solution)/shard_map/all_to_all | solution.py:35
  101.8 15.2 %all_to_all.37 = f32[16,13,256]{2,1,0:T(8,128)S(1)} all-to-all(f32[16,13,256]{2,1,0:T(8,128)S(1)} %broadcast_in_dim.53), channel_id=1, replica_groups=mesh['space'=16,'vel'=16] {'space'}, dimensions={0} | all-to-all | bytes 425984 | tf_op jit(solution)/shard_map/all_to_all | solution.py:35
  117.3 1.0 multiply_reduce_fusion.4
  123.3 1.9 %convolution_add_fusion.1 = f32[2048,256]{0,1:T(8,128)S(1)} fusion(f32[2048,256]{0,1:T(8,128)S(1)} %fusion.13, f32[13,2048]{1,0:T(8,128)S(1)} %stack.2, f32[13,4096]{1,0:T(8,128)S(1)} %get-tuple-element.13, s32[]{:T(128)S(6)} %select_n.225, f32[13,4096]{1,0:T(8,128)S(1)} %bitcast.83, f32[]{:T(128)S(6)} %div.103, f32[]{:T(128)S(6)} %div.102), kind=kOutput, calls=%fused_computation.18 | convolution fusion | flops 82323200 | bytes 4358156 | tf_op jit(solution)/shard_map/dot_general | solution.py:145
  125.3 3.5 %collective-permute-start.4 = (f32[2048,1]{0,1:T(1,128)S(1)}, f32[2048,1]{0,1:T(1,128)S(1)}, u32[]{:S(2)}, u32[]{:S(2)}) collective-permute-start(f32[2048,1]{0,1:T(1,128)S(1)} %get-tuple-element.16), channel_id=1, source_target_pairs={{0,16},{16,32},{32,48},{48,64},{64,80},{80,96},{96,112},{112,128},... | collective-permute-start | bytes 24584 | tf_op jit(solution)/shard_map/ppermute | solution.py:56
  128.8 2.3 %collective-permute-start.5 = (f32[2048,1]{0,1:T(1,128)S(1)}, f32[2048,1]{0,1:T(1,128)S(1)}, u32[]{:S(2)}, u32[]{:S(2)}) collective-permute-start(f32[2048,1]{0,1:T(1,128)S(1)} %get-tuple-element.17), channel_id=1, source_target_pairs={{16,0},{32,16},{48,32},{64,48},{80,64},{96,80},{112,96},{128,112},... | collective-permute-start | bytes 24584 | tf_op jit(solution)/shard_map/ppermute | solution.py:57
  131.2 4.1 %collective-permute-done.5 = f32[2048,1]{0,1:T(1,128)S(1)} collective-permute-done((f32[2048,1]{0,1:T(1,128)S(1)}, f32[2048,1]{0,1:T(1,128)S(1)}, u32[]{:S(2)}, u32[]{:S(2)}) %collective-permute-start.5) | collective-permute-done | bytes 8224 | tf_op jit(solution)/shard_map/ppermute | solution.py:57
  135.3 2.6 %fusion.14 = f32[2048,256]{0,1:T(8,128)S(1)} fusion(f32[2048,256]{0,1:T(8,128)S(1)} %convolution_add_fusion.1, f32[13,256]{1,0:T(8,128)S(1)} %fusion.94, f32[2048,1]{0,1:T(1,128)S(1)} %collective-permute-done.5, f32[2048,1]{0,1:T(1,128)S(1)} %collective-permute-done.4, f32[256]{0:T(256)S(1)} %add_multiply_fusion.1, f32[2048]{0:T(1024)S(1)} %get-tuple-element.29, ...), kind=kOutput, calls=%fused_computation.26 | convolution fusion | flops 87058432 | bytes 4341812 | tf_op jit(solution)/shard_map/dot_general | solution.py:131
  137.9 1.7 fusion.34
  139.6 12.1 %all_to_all.38 = f32[16,13,256]{2,1,0:T(8,128)S(1)} all-to-all(f32[16,13,256]{2,1,0:T(8,128)S(1)} %broadcast_in_dim.54), channel_id=1, replica_groups=mesh['space'=16,'vel'=16] {'vel'}, dimensions={0} | all-to-all | bytes 425984 | tf_op jit(solution)/shard_map/all_to_all | solution.py:35
  152.5 5.4 %all-to-all-start.6 = ((f32[16,13,256]{2,1,0:T(8,128)}), f32[16,13,256]{2,1,0:T(8,128)S(1)}, u32[]{:S(2)}, u32[]{:S(2)}) async-start(f32[16,13,256]{2,1,0:T(8,128)} %broadcast_in_dim.55), calls=%async_computation.6 | async-start | bytes 524288 | tf_op jit(solution)/shard_map/all_to_all | solution.py:35
  158.0 10.3 %all-to-all-done.6 = f32[16,13,256]{2,1,0:T(8,128)S(1)} async-done(((f32[16,13,256]{2,1,0:T(8,128)}), f32[16,13,256]{2,1,0:T(8,128)S(1)}, u32[]{:S(2)}, u32[]{:S(2)}) %all-to-all-start.6) | async-done | bytes 213024 | tf_op jit(solution)/shard_map/all_to_all | solution.py:35
  168.6 1.0 multiply_reduce_fusion.1
  174.6 1.9 %fusion.15 = bf16[2048,256]{0,1:T(8,128)(2,1)S(1)} fusion(f32[2048,256]{0,1:T(8,128)S(1)} %fusion.14, f32[13,2048]{1,0:T(8,128)S(1)} %stack.2, f32[13,256]{1,0:T(8,128)S(1)} %fusion.49), kind=kOutput, calls=%fused_computation.27 | convolution fusion | flops 82837504 | bytes 3265536 | tf_op jit(solution)/shard_map/dot_general | solution.py:145
  177.2 1.3 copy.39
  (70 shorter events, 14.7 us)
Async XLA Ops:
  0.6 66.6 %copy-start = (f32[13,13]{1,0:T(8,128)S(1)}, f32[13,13]{1,0:T(8,128)}, u32[]{:S(2)}) copy-start(f32[13,13]{1,0:T(8,128)} %param.12) | copy-start | bytes 2032
  0.6 16.8 %copy-start.1 = (s32[256]{0:T(256)S(1)}, s32[256]{0:T(256)}, u32[]{:S(2)}) copy-start(s32[256]{0:T(256)} %param.10) | copy-start | bytes 3076
  0.7 16.8 %copy-start.2 = (f32[256]{0:T(256)S(1)}, f32[256]{0:T(256)}, u32[]{:S(2)}) copy-start(f32[256]{0:T(256)} %param.9) | copy-start | bytes 3076
  2.1 17.1 %all-to-all-start = ((f32[16,1,208]{2,1,0:T(1,128)}), f32[16,1,208]{2,1,0:T(1,128)S(1)}, u32[]{:S(2)}, u32[]{:S(2)}) async-start(f32[16,1,208]{2,1,0:T(1,128)} %reshape.305), calls=%async_computation | async-start | bytes 32768 | tf_op jit(solution)/shard_map/all_to_all | solution.py:35
  9.8 11.2 %copy-start.4 = (f32[13]{0:T(128)S(1)}, f32[13]{0:T(128)}, u32[]{:S(2)}) copy-start(f32[13]{0:T(128)} %constant.105.clone) | copy-start | bytes 160
  9.8 10.9 %collective-permute-start = (f32[2048,1]{0,1:T(1,128)S(1)}, f32[2048,1]{0,1:T(1,128)S(1)}, u32[]{:S(2)}, u32[]{:S(2)}) collective-permute-start(f32[2048,1]{0,1:T(1,128)S(1)} %get-tuple-element.20), channel_id=1, source_target_pairs={{0,16},{16,32},{32,48},{48,64},{64,80},{80,96},{96,112},{112,128},... | collective-permute-start | bytes 24584 | tf_op jit(solution)/shard_map/ppermute | solution.py:56
  14.5 6.4 %collective-permute-start.1 = (f32[2048,1]{0,1:T(1,128)S(1)}, f32[2048,1]{0,1:T(1,128)S(1)}, u32[]{:S(2)}, u32[]{:S(2)}) collective-permute-start(f32[2048,1]{0,1:T(1,128)S(1)} %get-tuple-element.21), channel_id=1, source_target_pairs={{16,0},{32,16},{48,32},{64,48},{80,64},{96,80},{112,96},{128,112},... | collective-permute-start | bytes 24584 | tf_op jit(solution)/shard_map/ppermute | solution.py:57
  28.2 39.0 %copy-start.3 = (f32[13]{0:T(128)S(1)}, f32[13]{0:T(128)}, u32[]{:S(2)}) copy-start(f32[13]{0:T(128)} %param.11) | copy-start | bytes 160
  45.0 21.9 %all-to-all-start.2 = ((f32[16,13,256]{2,1,0:T(8,128)}), f32[16,13,256]{2,1,0:T(8,128)S(1)}, u32[]{:S(2)}, u32[]{:S(2)}) async-start(f32[16,13,256]{2,1,0:T(8,128)} %broadcast_in_dim.51), calls=%async_computation.2 | async-start | bytes 524288 | tf_op jit(solution)/shard_map/all_to_all | solution.py:35
  75.2 6.1 %collective-permute-start.2 = (f32[2048,1]{0,1:T(1,128)S(1)}, f32[2048,1]{0,1:T(1,128)S(1)}, u32[]{:S(2)}, u32[]{:S(2)}) collective-permute-start(f32[2048,1]{0,1:T(1,128)S(1)} %get-tuple-element.18), channel_id=1, source_target_pairs={{0,16},{16,32},{32,48},{48,64},{64,80},{80,96},{96,112},{112,128},... | collective-permute-start | bytes 24584 | tf_op jit(solution)/shard_map/ppermute | solution.py:56
  78.8 6.4 %collective-permute-start.3 = (f32[2048,1]{0,1:T(1,128)S(1)}, f32[2048,1]{0,1:T(1,128)S(1)}, u32[]{:S(2)}, u32[]{:S(2)}) collective-permute-start(f32[2048,1]{0,1:T(1,128)S(1)} %get-tuple-element.19), channel_id=1, source_target_pairs={{16,0},{32,16},{48,32},{64,48},{80,64},{96,80},{112,96},{128,112},... | collective-permute-start | bytes 24584 | tf_op jit(solution)/shard_map/ppermute | solution.py:57
  125.3 5.9 %collective-permute-start.4 = (f32[2048,1]{0,1:T(1,128)S(1)}, f32[2048,1]{0,1:T(1,128)S(1)}, u32[]{:S(2)}, u32[]{:S(2)}) collective-permute-start(f32[2048,1]{0,1:T(1,128)S(1)} %get-tuple-element.16), channel_id=1, source_target_pairs={{0,16},{16,32},{32,48},{48,64},{64,80},{80,96},{96,112},{112,128},... | collective-permute-start | bytes 24584 | tf_op jit(solution)/shard_map/ppermute | solution.py:56
  128.8 6.4 %collective-permute-start.5 = (f32[2048,1]{0,1:T(1,128)S(1)}, f32[2048,1]{0,1:T(1,128)S(1)}, u32[]{:S(2)}, u32[]{:S(2)}) collective-permute-start(f32[2048,1]{0,1:T(1,128)S(1)} %get-tuple-element.17), channel_id=1, source_target_pairs={{16,0},{32,16},{48,32},{64,48},{80,64},{96,80},{112,96},{128,112},... | collective-permute-start | bytes 24584 | tf_op jit(solution)/shard_map/ppermute | solution.py:57
  152.5 15.7 %all-to-all-start.6 = ((f32[16,13,256]{2,1,0:T(8,128)}), f32[16,13,256]{2,1,0:T(8,128)S(1)}, u32[]{:S(2)}, u32[]{:S(2)}) async-start(f32[16,13,256]{2,1,0:T(8,128)} %broadcast_in_dim.55), calls=%async_computation.6 | async-start | bytes 524288 | tf_op jit(solution)/shard_map/all_to_all | solution.py:35
where the time goes:
time: 180 us; the launch traced here: 179 us
  blocking collectives  55.4 us (31%)
  starting transfers between devices  41.7 us (23%)
  waiting for transfers between devices  28.8 us (16%)
  matrix products  27.7 us (15%)
  between operations  9.11 us (5%)
  other arithmetic  8.09 us (4%)
  local copies, waits for them, and re-layouts  7.73 us (4%)
    all_to_all x4, blocking collectives, sent_to_all(): return lax.all_to_all(copies, axis, split_axis=0, concat_axis=0, tiled=True)  55.4 us
    all_to_all x3, starting transfers between devices, sent_to_all(): return lax.all_to_all(copies, axis, split_axis=0, concat_axis=0, tiled=True)  23.2 us
    all_to_all x3, waiting for transfers between devices, sent_to_all(): return lax.all_to_all(copies, axis, split_axis=0, concat_axis=0, tiled=True)  20.5 us
    ppermute x3, starting transfers between devices, padded_2(): before = lax.ppermute(last, axis, up)  11.8 us
    dot_general x3, matrix products, per_device(): equilibrium = jnp.dot(equilibrium_rows.T, current, precision=highest)  10.7 us
    ppermute x3, waiting for transfers between devices, padded_2(): after = lax.ppermute(first, axis, down)  8.26 us
    ppermute x3, starting transfers between devices, padded_2(): after = lax.ppermute(first, axis, down)  6.67 us
    dot_general x6, matrix products, apply_operator(): jnp.dot(coupling, moments, precision=highest)  6.08 us
  transfers between devices with their start and end apart: 9, of which 5 were waited for; matrix products, arithmetic and copies ran while one was open for 3% of the time, Pallas kernels for 0%

commit v1 on v0

v1 whole, which is shorter than its diff:
```python
import math

import jax
import jax.numpy as jnp
import numpy as np
from jax import lax
from jax.experimental import pallas as pl
from jax.experimental.pallas import tpu as pltpu
from jax.sharding import PartitionSpec as P

NV1 = 32
K = 13
time_step = 0.125
spacing = 8.0 / NV1
CELLS = 256
WIDE = 384
PEERS = 16
ROWS = 2048
BLOCK = 1024
bf16 = jnp.bfloat16
f32 = jnp.float32


def parts_of(x, number):
    rest = np.asarray(x, np.float64)
    out = []
    for _ in range(number):
        piece = rest.astype(np.float32).astype(bf16)
        out.append(piece)
        rest = rest - piece.astype(np.float64)
    return out


def grid_constants():
    v = (np.arange(NV1) + 0.5) * spacing - 4.0
    w = np.exp(-0.5 * v * v) * spacing / math.sqrt(2.0 * math.pi)
    vy, vz = np.repeat(v, NV1), np.tile(v, NV1)
    wyz = np.repeat(w, NV1) * np.tile(w, NV1)
    one = np.ones_like(vy)
    yz = vy * vy + vz * vz
    phi = np.stack([one, vy, vz, vy * vz, vy * vy, vz * vz, vy * yz, vz * yz])
    cmat = np.zeros((NV1, K, 8))
    for i, x in enumerate(v):
        c = cmat[i]
        c[0, 0] = 1.0
        c[1, 0] = x
        c[2, 1] = 1.0
        c[3, 2] = 1.0
        c[4, 0] = (x * x - 3.0) / math.sqrt(6.0)
        c[4, 4] = c[4, 5] = 1.0 / math.sqrt(6.0)
        c[5, 1] = x
        c[6, 2] = x
        c[7, 3] = 1.0
        c[8, 0] = 0.5 * x * x
        c[8, 4] = -0.5
        c[9, 0] = x * x / math.sqrt(12.0)
        c[9, 4] = 1.0 / math.sqrt(12.0)
        c[9, 5] = -2.0 / math.sqrt(12.0)
        c[10, 0] = x * (x * x - 5.0) / math.sqrt(10.0)
        c[10, 4] = c[10, 5] = x / math.sqrt(10.0)
        c[11, 1] = (x * x - 5.0) / math.sqrt(10.0)
        c[11, 6] = 1.0 / math.sqrt(10.0)
        c[12, 2] = (x * x - 5.0) / math.sqrt(10.0)
        c[12, 7] = 1.0 / math.sqrt(10.0)
    a = time_step * np.abs(v)
    plus = v > 0.0
    proj = phi * wyz
    groups = [np.ones(NV1)]
    for power in (1, 2, 3):
        groups += [a**power * plus, a**power * ~plus]
    big = np.zeros((7 * 16, 8 * NV1))
    for g, factor in enumerate(groups):
        for i in range(NV1):
            big[16 * g : 16 * g + K, 8 * i : 8 * i + 8] = factor[i] * w[i] * cmat[i]
    gram2 = proj @ phi.T
    shakhov = np.array([1.0] * 5 + [0.0] * 5 + [1.0 / 3.0] * 3)

    def between(factor):
        out = np.zeros((16, 16))
        for i in range(NV1):
            out[:K, :K] += factor[i] * w[i] * cmat[i] @ gram2 @ cmat[i].T
        return out

    c16 = np.zeros(16)
    c16[:K] = shakhov
    g, gp, gm, g2p, g2m = (between(groups[k]) for k in (0, 1, 2, 3, 4))
    mats = [g, gp, gm, g * c16, gp * c16, gm * c16, g2p, g2m, g2p * c16, g2m * c16]
    mats = six_terms(np.concatenate(mats, axis=0))
    big3 = np.concatenate(parts_of(big, 3), axis=0)
    p3 = np.concatenate(parts_of(proj, 3) + [np.zeros((8, BLOCK), bf16)], axis=0)
    ph, pm = parts_of(phi.T, 2)
    phi_k = np.concatenate([ph, ph, pm, np.zeros((BLOCK, 104), bf16)], axis=1)
    own = np.zeros((PEERS, 16, 16))
    speed = np.zeros((PEERS, 16, 128), np.float32)
    for j in range(PEERS):
        for u in range(2):
            own[j, 8 * u : 8 * u + 8, :K] = cmat[2 * j + u].T
            speed[j, 8 * u : 8 * u + 8] = a[2 * j + u]
    own = six_terms(own)
    return big3, mats, p3, phi_k, own, speed, shakhov


def six_terms(x):
    h, m, low = parts_of(x, 3)
    return np.concatenate([h, h, h, m, m, low], axis=-1)


BASES = (1, 3, 9)


def pair_table():
    entries = []
    for stage, size in enumerate(BASES):
        for quantity in range(4):
            for i in range(size):
                for j in range(i, size):
                    entries.append((stage, quantity, i, j))
    return entries


PAIRS = pair_table()


def pair_arrays():
    kind = np.full((8, 128), -1, np.int32)
    left = np.zeros((8, 128), np.int32)
    right = np.zeros((8, 128), np.int32)
    twice = np.zeros((8, 128), np.float32)
    for n, (stage, quantity, i, j) in enumerate(PAIRS):
        at = (n // 128, n % 128)
        kind[at] = 4 * stage + quantity
        left[at], right[at] = i, j
        twice[at] = 1.0 if i == j else 2.0
    return kind, left, right, twice


def lanes_of(shape):
    return lax.broadcasted_iota(jnp.int32, shape, len(shape) - 1)


def rows_of(shape):
    return lax.broadcasted_iota(jnp.int32, shape, 0)


def stack6(f):
    h = f.astype(bf16)
    rest = f - h.astype(f32)
    m = rest.astype(bf16)
    low = (rest - m.astype(f32)).astype(bf16)
    return jnp.concatenate([h, m, low, h, m, h], axis=0)


def relax_of(rate, flags):
    return (time_step * rate) * (1.0 + flags.astype(f32))


def shift_up(x):
    return pltpu.roll(x, 1, 1)


def shift_down(x):
    return pltpu.roll(x, x.shape[1] - 1, 1)


def diff_up(x):
    return x - shift_up(x)


def diff_down(x):
    return x - shift_down(x)


def sums_kernel(place, dist, p3, owned, rate, flags, sums, up, down, edge):
    positive = place[1] >= PEERS // 2
    parts = []
    for u in range(2):
        y = jnp.dot(p3[...], dist[pl.ds(u * BLOCK, BLOCK), :], preferred_element_type=f32)
        parts.append(y[0:8] + y[8:16] + y[16:24])
    w = jnp.concatenate(parts, axis=0)
    sums[...] = w
    lane = lanes_of((16, 128))
    row = rows_of((16, 128))
    mine = owned[...]
    relax = relax_of(rate[...], flags[...])
    r_first = jnp.broadcast_to(pltpu.roll(relax[:, 0:128], 48, 1), (16, 128))
    r_last = jnp.broadcast_to(pltpu.roll(relax[:, 128:256], 48, 1), (16, 128))
    zero = jnp.zeros((16, 128), f32)
    up[...] = (
        jnp.where(lane >= 120, w[:, 128:256], zero)
        + pltpu.roll(mine, 16, 1)
        + jnp.where((row == K) & (lane >= 32) & (lane < 48), r_last, zero)
    )
    down[...] = (
        jnp.where(lane < 8, w[:, 0:128], zero)
        + pltpu.roll(mine, 32, 1)
        + jnp.where((row == K) & (lane >= 48) & (lane < 64), r_first, zero)
    )
    e_lane = lanes_of((16, CELLS))
    e_row = rows_of((16, CELLS))
    first = jnp.where(positive, CELLS - 8, 0)
    pick = jnp.where((e_lane == e_row + first) & (e_row < 8), 1.0, 0.0).astype(bf16)
    for u in range(2):
        e = lax.dot_general(
            pick,
            dist[pl.ds(u * BLOCK, BLOCK), :],
            (((1,), (1,)), ((), ())),
            preferred_element_type=f32,
        )
        edge[:, pl.ds(u * BLOCK, BLOCK)] = e[0:8]


def pack_kernel(sums, up, down, owned, out):
    third = up[...] + down[...] + owned[...]
    whole = jnp.concatenate([sums[...], third], axis=1)
    for j in range(PEERS):
        out[j] = whole


N_FIELDS = 28


def fields_kernel(n_space, place, got, rate, flags, big3, mats, diffusivity, fields, relax_out, partial, table):
    slab = place[0]
    lane = lanes_of((1, WIDE))
    right = (lane >= CELLS) & (lane < CELLS + 8)
    left = lane >= WIDE - 8
    own = lane < CELLS
    inside = own | (right & (slab < n_space - 1)) | (left & (slab > 0))
    mask = jnp.where(inside, 1.0, 0.0)

    w = got[...].reshape(PEERS * 16, WIDE)
    w = jnp.where(own | right | left, w, 0.0)
    wh = w.astype(bf16)
    w_rest = w - wh.astype(f32)
    wm = w_rest.astype(bf16)
    wl = (w_rest - wm.astype(f32)).astype(bf16)
    y = jnp.dot(big3[...], wh, preferred_element_type=f32)
    z = jnp.dot(big3[0:224], wm, preferred_element_type=f32)
    t = jnp.dot(big3[0:112], wl, preferred_element_type=f32)
    mu = ((y[224:336] + z[112:224]) + (y[112:224] + z[0:112])) + t + y[0:112]
    mu = [mu[16 * g : 16 * g + 16] for g in range(7)]

    lane1 = lanes_of((16, 128))
    row1 = rows_of((16, 128))
    zero = jnp.zeros((16, 128), f32)
    halves = [zero, zero]
    for j in range(PEERS):
        tile = got[j, :, 2 * 128 : 3 * 128]
        amount = (16 * j - 16) % 128
        moved = pltpu.roll(tile, amount, 1) if amount else tile
        begin = 16 * (j % 8)
        halves[j // 8] = jnp.where((lane1 >= begin) & (lane1 < begin + 16), moved, halves[j // 8])
    from_first = pltpu.roll(got[0, :, 2 * 128 : 3 * 128], 80, 1)
    from_last = pltpu.roll(got[PEERS - 1, :, 2 * 128 : 3 * 128], 80, 1)
    ends = jnp.where(lane1 < 8, from_first, jnp.where(lane1 >= 120, from_last, zero))
    start = jnp.concatenate([halves[0], halves[1], ends], axis=1)
    start = jnp.where(rows_of((16, WIDE)) < K, start, 0.0)
    relax_own = relax_of(rate[...], flags[...])
    relax_ends = jnp.where((lane1 < 8) | (lane1 >= 120), from_first, zero)[K : K + 1]
    relax1 = jnp.concatenate([relax_own, relax_ends], axis=1)
    relax_out[...] = jnp.broadcast_to(relax1, (8, WIDE))
    r = jnp.broadcast_to(relax1, (16, WIDE))
    keep = 1.0 - r
    mask = jnp.broadcast_to(mask, (16, WIDE))
    diffusion = jnp.concatenate([diffusivity[...]] * 3, axis=1)

    def advance(base, ups, downs):
        new = keep * base - diff_up(ups[0]) - diff_down(downs[0])
        new_ups = [keep * ups[n] - diff_up(ups[n + 1]) for n in range(len(ups) - 1)]
        new_downs = [keep * downs[n] - diff_down(downs[n + 1]) for n in range(len(downs) - 1)]
        return new, new_ups, new_downs

    ups, downs = [mu[1], mu[3], mu[5]], [mu[2], mu[4], mu[6]]
    s1, ups, downs = advance(mu[0], ups, downs)
    s2, ups, downs = advance(s1, ups, downs)
    s3, _, _ = advance(s2, ups, downs)

    def times(first, last, inputs):
        stacked = stack6(jnp.concatenate(inputs, axis=1) if len(inputs) > 1 else inputs[0])
        y = jnp.dot(mats[16 * first : 16 * last], stacked, preferred_element_type=f32)
        out = []
        for n in range(len(inputs)):
            cut = y[:, n * WIDE : (n + 1) * WIDE]
            out.append([cut[16 * g : 16 * g + 16] for g in range(last - first)])
        return out

    def applied(f, coupled):
        return mask * (coupled + diffusion * (2.0 * f - shift_up(f) - shift_down(f)))

    def streamed(g, gp, gm):
        return keep * g - diff_up(gp) - diff_down(gm)

    def streamed_twice(k1, gp, gm, g2p, g2m):
        return keep * k1 - diff_up(keep * gp - diff_up(g2p)) - diff_down(keep * gm - diff_down(g2m))

    ((gc, gcp, gcm, _, _, g2cp, g2cm),) = times(4, 11, [start])
    relaxed = r * gc
    shares = mask * (s1 + relaxed)
    res = mask * (shares - start)
    k1_start = streamed(relaxed, r * gcp, r * gcm)
    k2_start = streamed_twice(k1_start, r * gcp, r * gcm, r * g2cp, r * g2cm)

    def parts(f, ys):
        out = [applied(f, ys[0])]
        k1 = streamed(ys[1], ys[2], ys[3])
        rg = r * ys[4]
        held = rg - f
        out += [mask * (k1 + held), held]
        if len(ys) > 5:
            out.append(streamed_twice(k1, ys[2], ys[3], ys[7], ys[8]))
            out.append(streamed(rg, r * ys[5], r * ys[6]) + held)
        return out

    y_shares, y_res = times(0, 9, [shares, res])
    rg = r * y_shares[4]
    held_shares = rg - shares
    n_shares = streamed(rg, r * y_shares[5], r * y_shares[6]) + held_shares
    p0 = mask * (s2 + k1_start + held_shares)
    e, p1, _, k2_res, n_res = parts(res, y_res)

    y_e, y_p0, y_p1 = times(0, 9, [e, p0, p1])
    ee, p2, _, k2_e, n_e = parts(e, y_e)
    ap0, q3, held_p0 = parts(p0, y_p0[:5])
    ap1, q4, held_p1 = parts(p1, y_p1[:5])
    q0 = mask * (s3 + k2_start + n_shares + held_p0)
    q1 = mask * (k2_res + n_res + held_p1)

    y_p2, y_ap0, y_ap1, y_q0, y_q1, y_q3, y_q4 = times(0, 5, [p2, ap0, ap1, q0, q1, q3, q4])
    ap2, q5, held_p2 = parts(p2, y_p2)
    aap0, q6, _ = parts(ap0, y_ap0)
    aap1, q7, _ = parts(ap1, y_ap1)
    q2 = mask * (k2_e + n_e + held_p2)
    aq0, aq1, aq3, aq4 = (applied(f, y[0]) for f, y in ((q0, y_q0), (q1, y_q1), (q3, y_q3), (q4, y_q4)))

    (y_ap2,) = times(0, 5, [ap2])
    aap2, q8, _ = parts(ap2, y_ap2)
    first = [q2, q5, q6, q7, aq0, aq1, aq3, aq4]
    aq2, aq5, aq6, aq7, aaq0, aaq1, aaq3, aaq4 = (applied(f, y[0]) for f, y in zip(first, times(0, 1, first)))
    second = [q8, aq2, aq5, aq6, aq7]
    aq8, aaq2, aaq5, aaq6, aaq7 = (applied(f, y[0]) for f, y in zip(second, times(0, 1, second)))
    ((y_aq8,),) = times(0, 1, [aq8])
    aaq8 = applied(aq8, y_aq8)

    q = [q0, q1, q2, q3, q4, q5, q6, q7, q8]
    aq = [aq0, aq1, aq2, aq3, aq4, aq5, aq6, aq7, aq8]
    aaq = [aaq0, aaq1, aaq2, aaq3, aaq4, aaq5, aaq6, aaq7, aaq8]
    for n, f in enumerate([start, shares, res, e, p0, p1, p2, ap0, ap1, ap2] + q + aq):
        fields[n] = f

    plain = [[res], [p0, p1, p2], q]
    once = [[e], [ap0, ap1, ap2], aq]
    again = [[ee], [aap0, aap1, aap2], aaq]
    table[...] = jnp.zeros((256, 128), f32)
    for n, (stage, quantity, i, j) in enumerate(PAIRS):
        a, b = ((plain, plain), (plain, once), (once, once), (once, again))[quantity]
        product = a[stage][i][:, 0:CELLS] * b[stage][j][:, 0:CELLS]
        folded = (product[0:8, 0:128] + product[0:8, 128:256]) + (product[8:16, 0:128] + product[8:16, 128:256])
        table[n : n + 1, :] = jnp.sum(folded, axis=0, keepdims=True)
    ones = jnp.ones((8, 128), f32)
    tops = [
        lax.dot_general(
            ones,
            table[128 * n : 128 * n + 128, :],
            (((1,), (1,)), ((), ())),
            precision=lax.Precision.HIGHEST,
            preferred_element_type=f32,
        )
        for n in range(2)
    ]
    row8 = rows_of((8, 128))
    line = jnp.where(row8 == 0, tops[0], jnp.where(row8 == 1, tops[1], 0.0))
    for j in range(n_space):
        partial[j] = line


UPDATE_ROWS = 256


def update_kernel(
    n_space,
    place,
    partial,
    fields,
    relax_in,
    kind,
    left,
    right,
    twice,
    coupling,
    diffusivity,
    own6,
    speed,
    shakhov,
    dist,
    phi_k,
    halo,
    out,
    macro,
    bands_h,
    bands_l,
    mixed,
    band_ends,
):
    step = pl.program_id(0)
    positive = place[1] >= PEERS // 2

    @pl.when(step == 0)
    def _():
        total = partial[0]
        for j in range(1, n_space):
            total = total + partial[j]
        total = total * twice[...]
        cpl = coupling[...]
        lane16 = lanes_of((16, 128))
        row16 = rows_of((16, 128))
        size = jnp.sum(jnp.abs(cpl), axis=1, keepdims=True)
        middle = jnp.sum(jnp.where(lane16 == row16, cpl, 0.0), axis=1, keepdims=True)
        real = row16[:, 0:1] < K
        most = jnp.max(jnp.where(real, size + 4.0 * diffusivity[:, 0:1], 0.0), axis=0, keepdims=True)
        least = jnp.min(jnp.where(real, 2.0 * middle - size, 1e30), axis=0, keepdims=True)
        low_step, high_step = 1.0 / most, 1.0 / least

        def summed(weighted, which):
            picked = jnp.where(kind[...] == which, weighted, 0.0)
            return jnp.sum(jnp.sum(picked, axis=0, keepdims=True), axis=1, keepdims=True)

        def clipped(x):
            return jnp.minimum(jnp.maximum(x, low_step), high_step)

        def weights_of(stage, weighted):
            rr, ra, aa, aaa = (summed(weighted, 4 * stage + n) for n in range(4))
            s1 = clipped(rr / ra)
            rr2 = rr - 2.0 * s1 * ra + s1 * s1 * aa
            ra2 = ra - 2.0 * s1 * aa + s1 * s1 * aaa
            s2 = clipped(rr2 / ra2)
            return s1 + s2, -s1 * s2

        li, ri = left[...], right[...]

        def choose(index, zero, one, two):
            return jnp.where(index == 0, zero, jnp.where(index == 1, one, two))

        a1, b1 = weights_of(0, total)
        a2, b2 = weights_of(1, total * choose(li, 1.0, a1, b1) * choose(ri, 1.0, a1, b1))

        def both(index):
            outer = (index >= 3).astype(jnp.int32) + (index >= 6).astype(jnp.int32)
            return choose(outer, 1.0, a2, b2) * choose(index - 3 * outer, 1.0, a1, b1)

        a3, b3 = weights_of(2, total * both(li) * both(ri))

        start, shares, res, e = (fields[n] for n in range(4))
        corr1 = a1 * res + b1 * e
        cur1 = shares + corr1
        res2 = fields[4] + a1 * fields[5] + b1 * fields[6]
        e2 = fields[7] + a1 * fields[8] + b1 * fields[9]
        corr2 = a2 * res2 + b2 * e2
        cur2 = res2 + cur1 + corr2

        def third(at):
            rows = [fields[at + 3 * n] + a1 * fields[at + 3 * n + 1] + b1 * fields[at + 3 * n + 2] for n in range(3)]
            return rows[0] + a2 * rows[1] + b2 * rows[2]

        res3, e3 = third(10), third(19)
        corr3 = a3 * res3 + b3 * e3
        cur3 = res3 + cur2 + corr3
        mine = pltpu.roll(cur3[:, 0:CELLS], lax.rem(CELLS - 16 * place[1], CELLS), 1)
        macro[...] = mine[0:K, 0:16]

        r = jnp.broadcast_to(relax_in[0:1, :], (16, WIDE))
        scaled = shakhov[:, 0:1] * r
        f1 = scaled * start + corr1
        f2 = scaled * cur1 + corr2
        f3 = scaled * cur2 + corr3
        y = jnp.dot(own6[place[1]], stack6(jnp.concatenate([f1, f2, f3], axis=1)), preferred_element_type=f32)
        y1, y2, y3 = (y[:, n * WIDE : (n + 1) * WIDE] for n in range(3))
        a = speed[place[1]][:, 0:1]

        def before(x):
            return jnp.where(positive, shift_up(x), shift_down(x))

        stay = 1.0 - r - a

        def moved(x):
            return stay * x + a * before(x)

        h = (moved(moved(y1) + y2) + y3)[:, 0:CELLS]
        hh = h.astype(bf16).astype(f32)
        hm = (h - hh).astype(bf16).astype(f32)

        once = before(stay)
        two = before(once)
        t0 = stay * stay * stay
        t1 = a * (stay * (stay + once) + once * once)
        t2 = a * a * (stay + once + two)
        t3 = jnp.broadcast_to(a * a * a, (16, WIDE))
        towards = jnp.where(positive, 1, -1)
        at = rows_of((CELLS, CELLS))
        to = lanes_of((CELLS, CELLS))
        at8 = rows_of((8, CELLS))
        to8 = lanes_of((8, CELLS))
        at8 = jnp.where(positive, at8 - 8, at8 + CELLS)
        for u in range(2):
            ts = [x[8 * u : 8 * u + 1, 0:CELLS] for x in (t0, t1, t2, t3)]

            def band(source, target):
                shape = source.shape
                back = (target - source) * towards
                value = jnp.zeros(shape, f32)
                for n, x in enumerate(ts):
                    value = jnp.where(back == n, jnp.broadcast_to(x, shape), value)
                return value

            b = band(at, to)
            bh = b.astype(bf16)
            bands_h[u] = bh
            bands_l[u] = (b - bh.astype(f32)).astype(bf16)
            b8 = band(at8, to8)
            b8h = b8.astype(bf16).astype(f32)
            band_ends[u] = jnp.concatenate([b8h, b8 - b8h], axis=0).astype(bf16)
            hu, mu = hh[8 * u : 8 * u + 8], hm[8 * u : 8 * u + 8]
            mixed[u] = jnp.concatenate([hu, mu, hu, jnp.zeros((104, CELLS), f32)], axis=0).astype(bf16)

    u = step // (BLOCK // UPDATE_ROWS)
    x = dist[...]
    value = jnp.dot(x, bands_h[u], preferred_element_type=f32)
    value += jnp.dot(x, bands_l[u], preferred_element_type=f32)
    value += jnp.dot(phi_k[...], mixed[u], preferred_element_type=f32)
    ends = halo[...]
    ends = jnp.concatenate([ends, ends], axis=0).astype(bf16)
    value += lax.dot_general(ends, band_ends[u], (((0,), (0,)), ((), ())), preferred_element_type=f32)
    out[...] = value.astype(bf16)


def vmem():
    return pl.BlockSpec(memory_space=pltpu.VMEM)


def smem():
    return pl.BlockSpec(memory_space=pltpu.SMEM)


def rounded(x):
    return lax.reduce_precision(x, 8, 7)


def make_per_device(n_space):
    big3, mats, p3, phi_k, own6, speed, shakhov = grid_constants()
    kind, left, right, twice = pair_arrays()
    shakhov16 = np.zeros((16, 128), np.float32)
    shakhov16[:K] = shakhov[:, None]

    def per_device(velocity_dist, macro_state, collision_rate, wall_flags, diffusivity, coupling):
        place = jnp.stack([lax.axis_index("space"), lax.axis_index("vel")]).astype(jnp.int32)
        rate = collision_rate.reshape(1, CELLS)
        flags = wall_flags.reshape(1, CELLS)
        owned = jnp.pad(macro_state, ((0, 3), (16, 96)))
        sums, up, down, edge = pl.pallas_call(
            sums_kernel,
            out_shape=(
                jax.ShapeDtypeStruct((16, CELLS), f32),
                jax.ShapeDtypeStruct((16, 128), f32),
                jax.ShapeDtypeStruct((16, 128), f32),
                jax.ShapeDtypeStruct((8, ROWS), f32),
            ),
            in_specs=[smem()] + [vmem()] * 5,
            out_specs=(vmem(),) * 4,
        )(place, velocity_dist, p3, owned, rate, flags)
        rising = [(i, i + 1) for i in range(n_space - 1)]
        falling = [(j, i) for i, j in rising]
        from_left = lax.ppermute(up, "space", rising)
        from_right = lax.ppermute(down, "space", falling)
        packed = pl.pallas_call(
            pack_kernel,
            out_shape=jax.ShapeDtypeStruct((PEERS, 16, WIDE), f32),
            in_specs=[vmem()] * 4,
            out_specs=vmem(),
        )(sums, from_left, from_right, owned)
        got = lax.all_to_all(packed, "vel", split_axis=0, concat_axis=0, tiled=True)
        half = PEERS // 2
        upwind = [(i * PEERS + n, j * PEERS + n) for i, j in rising for n in range(half, PEERS)]
        upwind += [(j * PEERS + n, i * PEERS + n) for i, j in rising for n in range(half)]
        halo = lax.ppermute(edge, ("space", "vel"), upwind)

        cpl = jnp.pad(coupling, ((0, 3), (0, 3)))
        h = rounded(cpl)
        m = rounded(cpl - h)
        low = rounded(cpl - h - m)
        cpl6 = jnp.concatenate([h, h, h, m, m, low], axis=1).astype(bf16)
        all_mats = jnp.concatenate([cpl6, jnp.asarray(mats)], axis=0)
        spread_diff = jnp.broadcast_to(jnp.pad(diffusivity, (0, 3))[:, None], (16, 128))
        fields, relax, partial = pl.pallas_call(
            lambda *refs: fields_kernel(n_space, *refs),
            out_shape=(
                jax.ShapeDtypeStruct((N_FIELDS, 16, WIDE), f32),
                jax.ShapeDtypeStruct((8, WIDE), f32),
                jax.ShapeDtypeStruct((n_space, 8, 128), f32),
            ),
            in_specs=[smem()] + [vmem()] * 6,
            out_specs=(vmem(),) * 3,
            scratch_shapes=[pltpu.VMEM((256, 128), f32)],
            name="fields",
        )(place, got, rate, flags, big3, all_mats, spread_diff)
        partial = lax.all_to_all(partial, "space", split_axis=0, concat_axis=0, tiled=True)

        blocks = ROWS // UPDATE_ROWS
        per_speed = BLOCK // UPDATE_ROWS
        cpl_wide = jnp.pad(coupling, ((0, 3), (0, 115)))
        return pl.pallas_call(
            lambda *refs: update_kernel(n_space, *refs),
            grid=(blocks,),
            out_shape=(
                jax.ShapeDtypeStruct((ROWS, CELLS), bf16),
                jax.ShapeDtypeStruct((K, 16), f32),
            ),
            in_specs=[smem()]
            + [vmem()] * 12
            + [
                pl.BlockSpec((UPDATE_ROWS, CELLS), lambda i: (i, 0)),
                pl.BlockSpec((UPDATE_ROWS, 128), lambda i: (i % per_speed, 0)),
                pl.BlockSpec((8, UPDATE_ROWS), lambda i: (0, i)),
            ],
            out_specs=(
                pl.BlockSpec((UPDATE_ROWS, CELLS), lambda i: (i, 0)),
                pl.BlockSpec((K, 16), lambda i: (0, 0)),
            ),
            scratch_shapes=[
                pltpu.VMEM((2, CELLS, CELLS), bf16),
                pltpu.VMEM((2, CELLS, CELLS), bf16),
                pltpu.VMEM((2, 128, CELLS), bf16),
                pltpu.VMEM((2, 16, CELLS), bf16),
            ],
            name="update",
        )(
            place,
            partial,
            fields,
            relax,
            kind,
            left,
            right,
            twice,
            cpl_wide,
            spread_diff,
            own6,
            speed,
            shakhov16,
            velocity_dist,
            phi_k,
            halo,
        )

    return per_device


def solution(mesh):
    placed = (P("vel", "space"), P(None, ("space", "vel")), P("space"), P("space"), P(), P())
    return jax.shard_map(
        make_per_device(mesh.shape["space"]),
        mesh=mesh,
        in_specs=placed,
        out_specs=(P("vel", "space"), P(None, ("space", "vel"))),
        check_vma=False,
    )
```

time: 180 us -> 66.1 us (0.37)
  blocking collectives: 55.4 us -> 0 us
  matrix products: 27.7 us -> 0 us
  starting transfers between devices: 41.7 us -> 24.3 us
  Pallas kernels: 0 us -> 15.7 us
  waiting for transfers between devices: 28.8 us -> 19.2 us
  between operations: 9.11 us -> 0.74 us
  other arithmetic: 8.09 us -> 1.25 us
  local copies, waits for them, and re-layouts: 7.73 us -> 4.07 us
    all_to_all x4 -> x0, blocking collectives: 55.4 us -> none  [sent_to_all(): return lax.all_to_all(copies, axis, split_axis=0, concat_axis=0, tiled=True)]
    dot_general x15 -> x0, matrix products: 27.7 us -> none  [the longest x3 10.7 us: per_device(): equilibrium = jnp.dot(equilibrium_rows.T, current, precision=highest)]
    pallas_call x0 -> x4, Pallas kernels: none -> 15.7 us  [the longest x1 7.97 us: per_device(): pl.pallas_call(lambda *refs: update_kernel(n_space, *refs), grid=(blocks,...]
    ppermute x6 -> x3, starting transfers between devices: 18.5 us -> 7.84 us  [the longest x1 3.78 us: per_device(): from_left = lax.ppermute(up, 'space', rising)]
    all_to_all x3 -> x2, waiting for transfers between devices: 20.5 us -> 10.2 us  [the longest x1 9.5 us: per_device(): got = lax.all_to_all(packed, 'vel', split_axis=0, concat_axis=0, tiled=True)]
    all_to_all x3 -> x2, starting transfers between devices: 23.2 us -> 16.5 us  [the longest x1 9.93 us: per_device(): lax.all_to_all(partial, 'space', split_axis=0, concat_axis=0, tiled=True)]
    reduce_sum x9 -> x0, other arithmetic: 4.08 us -> none  [the longest x6 4.01 us: synthetic_whole(): step_size = jnp.sum(residual * residual) / jnp.sum(residual * applied)]
    unnamed x20, local copies, waits for them, and re-layouts: 4.16 us -> 1.97 us
  transfers between devices with their start and end apart: 9 -> 5, of which waited for: 5 -> 4; matrix products, arithmetic and copies ran while one was open for 3% -> 2% of each run, Pallas kernels for 0% -> 0%
where the time goes in v1:
time: 66.1 us; the launch traced here: 65.4 us
  starting transfers between devices  24.3 us (37%)
  waiting for transfers between devices  19.2 us (29%)
  Pallas kernels  15.7 us (24%)
  local copies, waits for them, and re-layouts  4.07 us (6%)
  other arithmetic  1.25 us (2%)
  between operations  0.74 us (1%)
    all_to_all x1, starting transfers between devices, per_device(): lax.all_to_all(partial, 'space', split_axis=0, concat_axis=0, tiled=True)  9.93 us
    all_to_all x1, waiting for transfers between devices, per_device(): got = lax.all_to_all(packed, 'vel', split_axis=0, concat_axis=0, tiled=True)  9.5 us
    pallas_call x1, Pallas kernels, per_device(): pl.pallas_call(lambda *refs: update_kernel(n_space, *refs), grid=(blocks,...  7.97 us
    all_to_all x1, starting transfers between devices, per_device(): got = lax.all_to_all(packed, 'vel', split_axis=0, concat_axis=0, tiled=True)  6.56 us
    ppermute x1, waiting for transfers between devices, per_device(): from_right = lax.ppermute(down, 'space', falling)  4.58 us
    ppermute x1, waiting for transfers between devices, per_device(): halo = lax.ppermute(edge, ('space', 'vel'), upwind)  4.48 us
    ppermute x1, starting transfers between devices, per_device(): from_left = lax.ppermute(up, 'space', rising)  3.78 us
    pallas_call x1, Pallas kernels, per_device(): pl.pallas_call(lambda *refs: fields_kernel(n_space, *refs), out_shape=(ja...  3.77 us
  transfers between devices with their start and end apart: 5, of which 4 were waited for; matrix products, arithmetic and copies ran while one was open for 2% of the time, Pallas kernels for 0%

profile of v1, /device:TPU:2, one launch (start us, length us, event | category | flops | bytes accessed | tf_op | source)
XLA Modules:
  0.0 65.4 jit_solution(18192017346016038244)
XLA Ops:
  0.6 0.0 copy-start.7
  0.6 0.6 pad_add_fusion.place.refs_0_
  1.3 0.1 copy-done.7
  1.3 0.7 %pad.16.owned = f32[16,128]{1,0:T(8,128)} pad(f32[13,16]{1,0:T(8,128)S(1)} %copy-done.7, f32[]{:T(128)} %constant.31.clone.1), padding=0_3x16_96 | pad | bytes 9028 | tf_op jit(solution)/shard_map/jit(_pad)/pad | solution.py:557
  2.0 2.5 %shard_map.176 = (f32[16,256]{1,0:T(8,128)}, f32[16,128]{1,0:T(8,128)}, f32[16,128]{1,0:T(8,128)}, f32[8,2048]{1,0:T(8,128)}) custom-call(s32[2]{0:T(128)} %pad_add_fusion.place.refs_0_, bf16[2048,256]{1,0:T(8,128)(2,1)} %refs_13_.1, bf16[32,1024]{1,0:T(8,128)(2,1)} %constant.32.clone.p3, f32[16,128]{1,0:T(8,128)} %pad.16.owned, f32[1,256]{1,0:T(1,128)} %bitcast.4, ...), custom_call_target="tpu_custom_call" | custom-call | tf_op jit(solution)/shard_map/pallas_call | solution.py:558
  4.5 3.8 %collective-permute-start = (f32[16,128]{1,0:T(8,128)}, f32[16,128]{1,0:T(8,128)S(1)}, u32[]{:S(2)}, u32[]{:S(2)}) collective-permute-start(f32[16,128]{1,0:T(8,128)} %get-tuple-element.10), channel_id=1, source_target_pairs={{0,16},{16,32},{32,48},{48,64},{64,80},{80,96},{96,112},{112,128},... | collective-permute-start | bytes 24584 | tf_op jit(solution)/shard_map/ppermute | solution.py:571
  8.3 2.0 %collective-permute-start.1 = (f32[16,128]{1,0:T(8,128)}, f32[16,128]{1,0:T(8,128)S(1)}, u32[]{:S(2)}, u32[]{:S(2)}) collective-permute-start(f32[16,128]{1,0:T(8,128)} %get-tuple-element.11), channel_id=1, source_target_pairs={{16,0},{32,16},{48,32},{64,48},{80,64},{96,80},{112,96},{128,112},... | collective-permute-start | bytes 24584 | tf_op jit(solution)/shard_map/ppermute | solution.py:572
  10.3 0.0 collective-permute-done.up
  10.3 0.0 copy-start.5
  10.3 4.6 %collective-permute-done.1.down = f32[16,128]{1,0:T(8,128)S(1)} collective-permute-done((f32[16,128]{1,0:T(8,128)}, f32[16,128]{1,0:T(8,128)S(1)}, u32[]{:S(2)}, u32[]{:S(2)}) %collective-permute-start.1) | collective-permute-done | bytes 8224 | tf_op jit(solution)/shard_map/ppermute | solution.py:572
  14.9 0.0 copy-done.5
  14.9 0.6 copy-done.6
  15.5 1.5 %shard_map.177 = f32[16,16,384]{2,1,0:T(8,128)} custom-call(f32[16,256]{1,0:T(8,128)} %get-tuple-element.9.sums, f32[16,128]{1,0:T(8,128)} %copy-done.5, f32[16,128]{1,0:T(8,128)} %copy-done.6, f32[16,128]{1,0:T(8,128)} %pad.16.owned), custom_call_target="tpu_custom_call" | custom-call | tf_op jit(solution)/shard_map/pallas_call | solution.py:573
  17.0 6.6 %all-to-all-start = ((f32[16,16,384]{2,1,0:T(8,128)}), f32[16,16,384]{2,1,0:T(8,128)S(1)}, u32[]{:S(2)}, u32[]{:S(2)}) async-start(f32[16,16,384]{2,1,0:T(8,128)} %shard_map.177), calls=%async_computation | async-start | bytes 786432 | tf_op jit(solution)/shard_map/all_to_all | solution.py:579
  23.6 0.0 copy-done.9
  23.6 0.0 copy-start.3
  23.6 0.0 copy-done.4
  23.7 0.1 concatenate.7
  23.8 0.6 copy-done.3
  24.4 0.6 pad_maximum_fusion.refs_5_
  25.0 9.5 %all-to-all-done.refs_1_ = f32[16,16,384]{2,1,0:T(8,128)S(1)} async-done(((f32[16,16,384]{2,1,0:T(8,128)}), f32[16,16,384]{2,1,0:T(8,128)S(1)}, u32[]{:S(2)}, u32[]{:S(2)}) %all-to-all-start) | async-done | bytes 393248 | tf_op jit(solution)/shard_map/all_to_all | solution.py:579
  34.5 0.7 %broadcast_in_dim.2.refs_6_.refs_9_ = f32[16,128]{1,0:T(8,128)} broadcast(f32[16]{0:T(128)S(1)} %pad.18), dimensions={0} | broadcast | bytes 8256 | tf_op jit(solution)/shard_map/broadcast_in_dim | solution.py:591
  35.3 0.0 copy-done
  35.3 3.8 %fields.1 = (f32[28,16,384]{2,1,0:T(8,128)}, f32[8,384]{1,0:T(8,128)}, f32[16,8,128]{2,1,0:T(8,128)}) custom-call(s32[2]{0:T(128)} %pad_add_fusion.place.refs_0_, f32[16,16,384]{2,1,0:T(8,128)} %copy-done, f32[1,256]{1,0:T(1,128)} %bitcast.5, s32[1,256]{1,0:T(1,128)} %bitcast.7, bf16[336,256]{1,0:T(8,128)(2,1)} %constant.34.clone.refs_4_, ...), custom_call_target="tpu_custom_call" | custom-call | tf_op jit(solution)/shard_map/fields/pallas_call | solution.py:592
  39.1 9.9 %all-to-all-start.1 = ((f32[16,8,128]{2,1,0:T(8,128)}), f32[16,8,128]{2,1,0:T(8,128)S(1)}, u32[]{:S(2)}, u32[]{:S(2)}) async-start(f32[16,8,128]{2,1,0:T(8,128)} %get-tuple-element.12), calls=%async_computation.1 | async-start | bytes 131072 | tf_op jit(solution)/shard_map/all_to_all | solution.py:604
  49.0 0.0 copy-done.8
  49.0 2.0 %collective-permute-start.2 = (f32[8,2048]{1,0:T(8,128)S(1)}, f32[8,2048]{1,0:T(8,128)S(1)}, u32[]{:S(2)}, u32[]{:S(2)}) collective-permute-start(f32[8,2048]{1,0:T(8,128)S(1)} %copy-done.8), channel_id=1, source_target_pairs={{8,24},{9,25},{10,26},{11,27},{12,28},{13,29},{14,30},{15,31},{24,... | collective-permute-start | bytes 196616 | tf_op jit(solution)/shard_map/ppermute | solution.py:583
  51.0 0.6 pad.19.refs_8_
  51.6 4.5 %collective-permute-done.2.refs_15_ = f32[8,2048]{1,0:T(8,128)S(1)} collective-permute-done((f32[8,2048]{1,0:T(8,128)S(1)}, f32[8,2048]{1,0:T(8,128)S(1)}, u32[]{:S(2)}, u32[]{:S(2)}) %collective-permute-start.2) | collective-permute-done | bytes 65568 | tf_op jit(solution)/shard_map/ppermute | solution.py:583
  56.1 0.7 %all-to-all-done.1.refs_1_ = f32[16,8,128]{2,1,0:T(8,128)S(1)} async-done(((f32[16,8,128]{2,1,0:T(8,128)}), f32[16,8,128]{2,1,0:T(8,128)S(1)}, u32[]{:S(2)}, u32[]{:S(2)}) %all-to-all-start.1) | async-done | bytes 65568 | tf_op jit(solution)/shard_map/all_to_all | solution.py:604
  56.8 0.6 copy-done.1
  57.4 8.0 %update.1 = (bf16[2048,256]{1,0:T(8,128)(2,1)}, f32[13,16]{1,0:T(8,128)}) custom-call(s32[2]{0:T(128)} %pad_add_fusion.place.refs_0_, f32[16,8,128]{2,1,0:T(8,128)} %copy-done.1, f32[28,16,384]{2,1,0:T(8,128)} %get-tuple-element.13.refs_2_, f32[8,384]{1,0:T(8,128)} %get-tuple-element.14.refs_3_, s32[8,128]{1,0:T(8,128)} %constant.35.clone.refs_4_, ...), custom_call_target="tpu_custom_call" | custom-call | tf_op jit(solution)/shard_map/update/pallas_call | solution.py:609
  (10 shorter events, 0.0 us)
Async XLA Ops:
  0.6 0.7 %copy-start.7 = (f32[13,16]{1,0:T(8,128)S(1)}, f32[13,16]{1,0:T(8,128)}, u32[]{:S(2)}) copy-start(f32[13,16]{1,0:T(8,128)} %param.18) | copy-start | bytes 2500
  4.5 5.8 %collective-permute-start = (f32[16,128]{1,0:T(8,128)}, f32[16,128]{1,0:T(8,128)S(1)}, u32[]{:S(2)}, u32[]{:S(2)}) collective-permute-start(f32[16,128]{1,0:T(8,128)} %get-tuple-element.10), channel_id=1, source_target_pairs={{0,16},{16,32},{32,48},{48,64},{64,80},{80,96},{96,112},{112,128},... | collective-permute-start | bytes 24584 | tf_op jit(solution)/shard_map/ppermute | solution.py:571
  8.3 6.7 %collective-permute-start.1 = (f32[16,128]{1,0:T(8,128)}, f32[16,128]{1,0:T(8,128)S(1)}, u32[]{:S(2)}, u32[]{:S(2)}) collective-permute-start(f32[16,128]{1,0:T(8,128)} %get-tuple-element.11), channel_id=1, source_target_pairs={{16,0},{32,16},{48,32},{64,48},{80,64},{96,80},{112,96},{128,112},... | collective-permute-start | bytes 24584 | tf_op jit(solution)/shard_map/ppermute | solution.py:572
  10.3 4.6 %copy-start.5 = (f32[16,128]{1,0:T(8,128)}, f32[16,128]{1,0:T(8,128)S(1)}, u32[]{:S(2)}) copy-start(f32[16,128]{1,0:T(8,128)S(1)} %collective-permute-done.up) | copy-start | bytes 24580
  14.9 0.6 copy-start.6
  17.0 6.6 %copy-start.9 = (f32[13]{0:T(128)S(1)}, f32[13]{0:T(128)}, u32[]{:S(2)}) copy-start(f32[13]{0:T(128)} %param.21) | copy-start | bytes 160
  17.0 6.6 %copy-start.4 = (f32[13,13]{1,0:T(8,128)S(1)}, f32[13,13]{1,0:T(8,128)}, u32[]{:S(2)}) copy-start(f32[13,13]{1,0:T(8,128)} %param.22) | copy-start | bytes 2032
  17.0 17.5 %all-to-all-start = ((f32[16,16,384]{2,1,0:T(8,128)}), f32[16,16,384]{2,1,0:T(8,128)S(1)}, u32[]{:S(2)}, u32[]{:S(2)}) async-start(f32[16,16,384]{2,1,0:T(8,128)} %shard_map.177), calls=%async_computation | async-start | bytes 786432 | tf_op jit(solution)/shard_map/all_to_all | solution.py:579
  23.6 0.8 %copy-start.3 = (bf16[160,96]{1,0:T(8,128)(2,1)S(1)}, bf16[160,96]{1,0:T(8,128)(2,1)}, u32[]{:S(2)}) copy-start(bf16[160,96]{1,0:T(8,128)(2,1)} %constant.33.clone) | copy-start | bytes 92164
  34.5 0.7 %copy-start = (f32[16,16,384]{2,1,0:T(8,128)}, f32[16,16,384]{2,1,0:T(8,128)S(1)}, u32[]{:S(2)}) copy-start(f32[16,16,384]{2,1,0:T(8,128)S(1)} %all-to-all-done.refs_1_) | copy-start | bytes 1179652
  39.1 9.9 %copy-start.8 = (f32[8,2048]{1,0:T(8,128)S(1)}, f32[8,2048]{1,0:T(8,128)}, u32[]{:S(2)}) copy-start(f32[8,2048]{1,0:T(8,128)} %get-tuple-element.15) | copy-start | bytes 196612
  39.1 17.7 %all-to-all-start.1 = ((f32[16,8,128]{2,1,0:T(8,128)}), f32[16,8,128]{2,1,0:T(8,128)S(1)}, u32[]{:S(2)}, u32[]{:S(2)}) async-start(f32[16,8,128]{2,1,0:T(8,128)} %get-tuple-element.12), calls=%async_computation.1 | async-start | bytes 131072 | tf_op jit(solution)/shard_map/all_to_all | solution.py:604
  49.0 7.1 %collective-permute-start.2 = (f32[8,2048]{1,0:T(8,128)S(1)}, f32[8,2048]{1,0:T(8,128)S(1)}, u32[]{:S(2)}, u32[]{:S(2)}) collective-permute-start(f32[8,2048]{1,0:T(8,128)S(1)} %copy-done.8), channel_id=1, source_target_pairs={{8,24},{9,25},{10,26},{11,27},{12,28},{13,29},{14,30},{15,31},{24,... | collective-permute-start | bytes 196616 | tf_op jit(solution)/shard_map/ppermute | solution.py:583
  56.1 0.7 %copy-start.2 = (f32[8,2048]{1,0:T(8,128)}, f32[8,2048]{1,0:T(8,128)S(1)}, u32[]{:S(2)}) copy-start(f32[8,2048]{1,0:T(8,128)S(1)} %collective-permute-done.2.refs_15_) | copy-start | bytes 196612
  56.8 0.6 copy-start.1

commit v2 on v1

v2 whole, which is shorter than its diff:
```python
import math

import jax
import jax.numpy as jnp
import numpy as np
from jax import lax
from jax.experimental import pallas as pl
from jax.experimental.pallas import tpu as pltpu
from jax.sharding import PartitionSpec as P

NV1 = 32
K = 13
time_step = 0.125
spacing = 8.0 / NV1
CELLS = 256
WIDE = 384
PEERS = 16
ROWS = 2048
BLOCK = 1024
bf16 = jnp.bfloat16
f32 = jnp.float32


def parts_of(x, number):
    rest = np.asarray(x, np.float64)
    out = []
    for _ in range(number):
        piece = rest.astype(np.float32).astype(bf16)
        out.append(piece)
        rest = rest - piece.astype(np.float64)
    return out


def grid_constants():
    v = (np.arange(NV1) + 0.5) * spacing - 4.0
    w = np.exp(-0.5 * v * v) * spacing / math.sqrt(2.0 * math.pi)
    vy, vz = np.repeat(v, NV1), np.tile(v, NV1)
    wyz = np.repeat(w, NV1) * np.tile(w, NV1)
    one = np.ones_like(vy)
    yz = vy * vy + vz * vz
    phi = np.stack([one, vy, vz, vy * vz, vy * vy, vz * vz, vy * yz, vz * yz])
    cmat = np.zeros((NV1, K, 8))
    for i, x in enumerate(v):
        c = cmat[i]
        c[0, 0] = 1.0
        c[1, 0] = x
        c[2, 1] = 1.0
        c[3, 2] = 1.0
        c[4, 0] = (x * x - 3.0) / math.sqrt(6.0)
        c[4, 4] = c[4, 5] = 1.0 / math.sqrt(6.0)
        c[5, 1] = x
        c[6, 2] = x
        c[7, 3] = 1.0
        c[8, 0] = 0.5 * x * x
        c[8, 4] = -0.5
        c[9, 0] = x * x / math.sqrt(12.0)
        c[9, 4] = 1.0 / math.sqrt(12.0)
        c[9, 5] = -2.0 / math.sqrt(12.0)
        c[10, 0] = x * (x * x - 5.0) / math.sqrt(10.0)
        c[10, 4] = c[10, 5] = x / math.sqrt(10.0)
        c[11, 1] = (x * x - 5.0) / math.sqrt(10.0)
        c[11, 6] = 1.0 / math.sqrt(10.0)
        c[12, 2] = (x * x - 5.0) / math.sqrt(10.0)
        c[12, 7] = 1.0 / math.sqrt(10.0)
    a = time_step * np.abs(v)
    plus = v > 0.0
    proj = phi * wyz
    groups = [np.ones(NV1)]
    for power in (1, 2, 3):
        groups += [a**power * plus, a**power * ~plus]
    big = np.zeros((7 * 16, 8 * NV1))
    for g, factor in enumerate(groups):
        for i in range(NV1):
            big[16 * g : 16 * g + K, 8 * i : 8 * i + 8] = factor[i] * w[i] * cmat[i]
    gram2 = proj @ phi.T
    shakhov = np.array([1.0] * 5 + [0.0] * 5 + [1.0 / 3.0] * 3)

    def between(factor):
        out = np.zeros((16, 16))
        for i in range(NV1):
            out[:K, :K] += factor[i] * w[i] * cmat[i] @ gram2 @ cmat[i].T
        return out

    c16 = np.zeros(16)
    c16[:K] = shakhov
    g, gp, gm, g2p, g2m = (between(groups[k]) for k in (0, 1, 2, 3, 4))
    mats = [g, gp, gm, g * c16, gp * c16, gm * c16, g2p, g2m, g2p * c16, g2m * c16]
    block = np.zeros((BLOCK + 336, 256), bf16)
    block[16:176, 128:224] = six_terms(np.concatenate(mats, axis=0))
    block[BLOCK:] = np.concatenate(parts_of(big, 3), axis=0)
    p3 = np.concatenate(parts_of(proj, 3) + [np.zeros((8, BLOCK), bf16)], axis=0)
    ph, pm = parts_of(phi.T, 2)
    block[0:BLOCK, 0:24] = np.concatenate([ph, ph, pm], axis=1)
    own = np.zeros((PEERS, 16, 16))
    for j in range(PEERS):
        for u in range(2):
            own[j, 8 * u : 8 * u + 8, :K] = cmat[2 * j + u].T
    own = np.concatenate([six_terms(own), np.zeros((PEERS, 16, 32), bf16)], axis=2)
    return block, p3, own


def six_terms(x):
    h, m, low = parts_of(x, 3)
    return np.concatenate([h, h, h, m, m, low], axis=-1)


BASES = (1, 3, 9)


def pair_table():
    entries = []
    for stage, size in enumerate(BASES):
        for quantity in range(4):
            for i in range(size):
                for j in range(i, size):
                    entries.append((stage, quantity, i, j))
    return entries


PAIRS = pair_table()


def pair_arrays():
    kind = np.full((8, 128), -1, np.int32)
    left = np.zeros((8, 128), np.int32)
    right = np.zeros((8, 128), np.int32)
    twice = np.zeros((8, 128), np.int32)
    for n, (stage, quantity, i, j) in enumerate(PAIRS):
        at = (n // 128, n % 128)
        kind[at] = 4 * stage + quantity
        left[at], right[at] = i, j
        twice[at] = 1 if i == j else 2
    return np.concatenate([kind, left, right, twice], axis=0).astype(np.float32)


def lanes_of(shape):
    return lax.broadcasted_iota(jnp.int32, shape, len(shape) - 1)


def rows_of(shape):
    return lax.broadcasted_iota(jnp.int32, shape, 0)


def stack6(f):
    h = f.astype(bf16)
    rest = f - h.astype(f32)
    m = rest.astype(bf16)
    low = (rest - m.astype(f32)).astype(bf16)
    return jnp.concatenate([h, m, low, h, m, h], axis=0)


def relax_of(rate, flags):
    return (time_step * rate) * (1.0 + flags.astype(f32))


def shift_up(x):
    return pltpu.roll(x, 1, 1)


def shift_down(x):
    return pltpu.roll(x, x.shape[1] - 1, 1)


def diff_up(x):
    return x - shift_up(x)


def diff_down(x):
    return x - shift_down(x)


def copies_of(pairs, sems):
    made = [pltpu.make_async_copy(x, y, sems.at[n]) for n, (x, y) in enumerate(pairs)]
    for copy in made:
        copy.start()
    return made


def sums_kernel(
    dist_in,
    p3_in,
    start_in,
    rate_in,
    flags_in,
    sums,
    up,
    down,
    edge,
    owned,
    dist,
    p3,
    start,
    rate,
    flags,
    padded,
    sems,
):
    positive = lax.axis_index("vel") >= PEERS // 2
    halves = [pl.ds(u * BLOCK, BLOCK) for u in range(2)]
    pairs = [(p3_in, p3), (start_in, start), (rate_in, rate), (flags_in, flags)]
    pairs += [(dist_in.at[half, :], dist.at[half, :]) for half in halves]
    waits = copies_of(pairs, sems)
    for copy in waits[:4]:
        copy.wait()
    parts = []
    for u in range(2):
        waits[4 + u].wait()
        y = jnp.dot(p3[...], dist[halves[u], :], preferred_element_type=f32)
        parts.append(y[0:8] + y[8:16] + y[16:24])
    w = jnp.concatenate(parts, axis=0)
    sums[...] = w
    lane = lanes_of((16, 128))
    row = rows_of((16, 128))
    padded[...] = jnp.zeros((16, 128), f32)
    padded[0:K, 0:16] = start[...]
    mine = pltpu.roll(padded[...], 16, 1)
    owned[...] = mine
    relax = relax_of(rate[...], flags[...])
    near_edge = jnp.where(positive, relax[:, 128:256], relax[:, 0:128])
    edge[:, ROWS : ROWS + 128] = jnp.broadcast_to(near_edge, (8, 128))
    r_first = jnp.broadcast_to(pltpu.roll(relax[:, 0:128], 48, 1), (16, 128))
    r_last = jnp.broadcast_to(pltpu.roll(relax[:, 128:256], 48, 1), (16, 128))
    zero = jnp.zeros((16, 128), f32)
    up[...] = (
        jnp.where(lane >= 120, w[:, 128:256], zero)
        + pltpu.roll(mine, 16, 1)
        + jnp.where((row == K) & (lane >= 32) & (lane < 48), r_last, zero)
    )
    down[...] = (
        jnp.where(lane < 8, w[:, 0:128], zero)
        + pltpu.roll(mine, 32, 1)
        + jnp.where((row == K) & (lane >= 48) & (lane < 64), r_first, zero)
    )
    e_lane = lanes_of((16, CELLS))
    e_row = rows_of((16, CELLS))
    first = jnp.where(positive, CELLS - 8, 0)
    pick = jnp.where((e_lane == e_row + first) & (e_row < 8), 1.0, 0.0).astype(bf16)
    for u in range(2):
        e = lax.dot_general(
            pick,
            dist[pl.ds(u * BLOCK, BLOCK), :],
            (((1,), (1,)), ((), ())),
            preferred_element_type=f32,
        )
        edge[:, pl.ds(u * BLOCK, BLOCK)] = e[0:8]


def pack_kernel(sums, up, down, owned, out, whole, sems):
    whole[:, 0:CELLS] = sums[...]
    whole[:, CELLS:WIDE] = up[...] + down[...] + owned[...]
    for copy in copies_of([(whole, out.at[j]) for j in range(PEERS)], sems):
        copy.wait()


N_FIELDS = 28


def fields_kernel(n_space, got, known, block, fields, partial, table, line, sems):
    slab = lax.axis_index("space")
    lane = lanes_of((1, WIDE))
    right = (lane >= CELLS) & (lane < CELLS + 8)
    left = lane >= WIDE - 8
    own = lane < CELLS
    inside = own | (right & (slab < n_space - 1)) | (left & (slab > 0))
    mask = jnp.where(inside, 1.0, 0.0)

    w = got[...].reshape(PEERS * 16, WIDE)
    w = jnp.where(own | right | left, w, 0.0)
    wh = w.astype(bf16)
    w_rest = w - wh.astype(f32)
    wm = w_rest.astype(bf16)
    wl = (w_rest - wm.astype(f32)).astype(bf16)
    y = jnp.dot(block[BLOCK : BLOCK + 336, :], wh, preferred_element_type=f32)
    z = jnp.dot(block[BLOCK : BLOCK + 224, :], wm, preferred_element_type=f32)
    t = jnp.dot(block[BLOCK : BLOCK + 112, :], wl, preferred_element_type=f32)
    mu = ((y[224:336] + z[112:224]) + (y[112:224] + z[0:112])) + t + y[0:112]
    mu = [mu[16 * g : 16 * g + 16] for g in range(7)]

    lane1 = lanes_of((16, 128))
    row1 = rows_of((16, 128))
    zero = jnp.zeros((16, 128), f32)
    halves = [zero, zero]
    for j in range(PEERS):
        tile = got[j, :, 2 * 128 : 3 * 128]
        amount = (16 * j - 16) % 128
        moved = pltpu.roll(tile, amount, 1) if amount else tile
        begin = 16 * (j % 8)
        halves[j // 8] = jnp.where((lane1 >= begin) & (lane1 < begin + 16), moved, halves[j // 8])
    from_first = pltpu.roll(got[0, :, 2 * 128 : 3 * 128], 80, 1)
    from_last = pltpu.roll(got[PEERS - 1, :, 2 * 128 : 3 * 128], 80, 1)
    ends = jnp.where(lane1 < 8, from_first, jnp.where(lane1 >= 120, from_last, zero))
    start = jnp.concatenate([halves[0], halves[1], ends], axis=1)
    start = jnp.where(rows_of((16, WIDE)) < K, start, 0.0)
    relax_ends = jnp.where((lane1 < 8) | (lane1 >= 120), from_first, zero)[K : K + 1]
    relax1 = jnp.concatenate([known[0:1, 0:CELLS], relax_ends], axis=1)
    r = jnp.broadcast_to(relax1, (16, WIDE))
    keep = 1.0 - r
    mask = jnp.broadcast_to(mask, (16, WIDE))
    diffusion = jnp.concatenate([known[8:24, 128:256]] * 3, axis=1)

    def advance(base, ups, downs):
        new = keep * base - diff_up(ups[0]) - diff_down(downs[0])
        new_ups = [keep * ups[n] - diff_up(ups[n + 1]) for n in range(len(ups) - 1)]
        new_downs = [keep * downs[n] - diff_down(downs[n + 1]) for n in range(len(downs) - 1)]
        return new, new_ups, new_downs

    ups, downs = [mu[1], mu[3], mu[5]], [mu[2], mu[4], mu[6]]
    s1, ups, downs = advance(mu[0], ups, downs)
    s2, ups, downs = advance(s1, ups, downs)
    s3, _, _ = advance(s2, ups, downs)

    def times(first, last, inputs):
        stacked = stack6(jnp.concatenate(inputs, axis=1) if len(inputs) > 1 else inputs[0])
        y = jnp.dot(block[16 * first : 16 * last, 128:224], stacked, preferred_element_type=f32)
        out = []
        for n in range(len(inputs)):
            cut = y[:, n * WIDE : (n + 1) * WIDE]
            out.append([cut[16 * g : 16 * g + 16] for g in range(last - first)])
        return out

    def applied(f, coupled):
        return mask * (coupled + diffusion * (2.0 * f - shift_up(f) - shift_down(f)))

    def streamed(g, gp, gm):
        return keep * g - diff_up(gp) - diff_down(gm)

    def streamed_twice(k1, gp, gm, g2p, g2m):
        return keep * k1 - diff_up(keep * gp - diff_up(g2p)) - diff_down(keep * gm - diff_down(g2m))

    ((gc, gcp, gcm, _, _, g2cp, g2cm),) = times(4, 11, [start])
    relaxed = r * gc
    shares = mask * (s1 + relaxed)
    res = mask * (shares - start)
    k1_start = streamed(relaxed, r * gcp, r * gcm)
    k2_start = streamed_twice(k1_start, r * gcp, r * gcm, r * g2cp, r * g2cm)

    def parts(f, ys):
        out = [applied(f, ys[0])]
        k1 = streamed(ys[1], ys[2], ys[3])
        rg = r * ys[4]
        held = rg - f
        out += [mask * (k1 + held), held]
        if len(ys) > 5:
            out.append(streamed_twice(k1, ys[2], ys[3], ys[7], ys[8]))
            out.append(streamed(rg, r * ys[5], r * ys[6]) + held)
        return out

    y_shares, y_res = times(0, 9, [shares, res])
    rg = r * y_shares[4]
    held_shares = rg - shares
    n_shares = streamed(rg, r * y_shares[5], r * y_shares[6]) + held_shares
    p0 = mask * (s2 + k1_start + held_shares)
    e, p1, _, k2_res, n_res = parts(res, y_res)

    y_e, y_p0, y_p1 = times(0, 9, [e, p0, p1])
    ee, p2, _, k2_e, n_e = parts(e, y_e)
    ap0, q3, held_p0 = parts(p0, y_p0[:5])
    ap1, q4, held_p1 = parts(p1, y_p1[:5])
    q0 = mask * (s3 + k2_start + n_shares + held_p0)
    q1 = mask * (k2_res + n_res + held_p1)

    y_p2, y_ap0, y_ap1, y_q0, y_q1, y_q3, y_q4 = times(0, 5, [p2, ap0, ap1, q0, q1, q3, q4])
    ap2, q5, held_p2 = parts(p2, y_p2)
    aap0, q6, _ = parts(ap0, y_ap0)
    aap1, q7, _ = parts(ap1, y_ap1)
    q2 = mask * (k2_e + n_e + held_p2)
    aq0, aq1, aq3, aq4 = (applied(f, y[0]) for f, y in ((q0, y_q0), (q1, y_q1), (q3, y_q3), (q4, y_q4)))

    (y_ap2,) = times(0, 5, [ap2])
    aap2, q8, _ = parts(ap2, y_ap2)
    first = [q2, q5, q6, q7, aq0, aq1, aq3, aq4]
    aq2, aq5, aq6, aq7, aaq0, aaq1, aaq3, aaq4 = (applied(f, y[0]) for f, y in zip(first, times(0, 1, first)))
    second = [q8, aq2, aq5, aq6, aq7]
    aq8, aaq2, aaq5, aaq6, aaq7 = (applied(f, y[0]) for f, y in zip(second, times(0, 1, second)))
    ((y_aq8,),) = times(0, 1, [aq8])
    aaq8 = applied(aq8, y_aq8)

    q = [q0, q1, q2, q3, q4, q5, q6, q7, q8]
    aq = [aq0, aq1, aq2, aq3, aq4, aq5, aq6, aq7, aq8]
    aaq = [aaq0, aaq1, aaq2, aaq3, aaq4, aaq5, aaq6, aaq7, aaq8]
    for n, f in enumerate([start, shares, res, e, p0, p1, p2, ap0, ap1, ap2] + q + aq):
        fields[n] = f

    plain = [[res], [p0, p1, p2], q]
    once = [[e], [ap0, ap1, ap2], aq]
    again = [[ee], [aap0, aap1, aap2], aaq]
    table[...] = jnp.zeros((256, 128), f32)
    for n, (stage, quantity, i, j) in enumerate(PAIRS):
        a, b = ((plain, plain), (plain, once), (once, once), (once, again))[quantity]
        product = a[stage][i][:, 0:CELLS] * b[stage][j][:, 0:CELLS]
        folded = (product[0:8, 0:128] + product[0:8, 128:256]) + (product[8:16, 0:128] + product[8:16, 128:256])
        table[n : n + 1, :] = jnp.sum(folded, axis=0, keepdims=True)
    ones = jnp.ones((8, 128), f32)
    tops = [
        lax.dot_general(
            ones,
            table[128 * n : 128 * n + 128, :],
            (((1,), (1,)), ((), ())),
            precision=lax.Precision.HIGHEST,
            preferred_element_type=f32,
        )
        for n in range(2)
    ]
    row8 = rows_of((8, 128))
    line[...] = jnp.where(row8 == 0, tops[0], jnp.where(row8 == 1, tops[1], 0.0))
    for copy in copies_of([(line, partial.at[j]) for j in range(n_space)], sems):
        copy.wait()


def speeds_of(shape):
    number = 2 * lax.axis_index("vel") + jnp.where(rows_of(shape) >= 8, 1, 0)
    return time_step * jnp.abs((number.astype(f32) + 0.5) * spacing - 4.0)


def stream_kernel(
    halo,
    dist_in,
    block_in,
    pairs_in,
    own_in,
    coupling_in,
    diff_in,
    rate_in,
    flags_in,
    out,
    table,
    block,
    dist,
    own6,
    coupling_raw,
    diff_raw,
    rate,
    flags,
    sems,
):
    vel = lax.axis_index("vel")
    positive = vel >= PEERS // 2
    moves = [(rate_in, rate), (flags_in, flags), (dist_in, dist), (coupling_in, coupling_raw), (diff_in, diff_raw)]
    moves += [(own_in.at[vel], own6), (pairs_in, table.at[24:56, 0:128]), (block_in, block)]
    waits = copies_of(moves, sems)
    waits[0].wait()
    waits[1].wait()
    towards = jnp.where(positive, 1, -1)
    lane = lanes_of((1, 128))
    low = jnp.where(positive, 120, 0)
    ends = jnp.where((lane >= low) & (lane < low + 8), halo[0:1, ROWS : ROWS + 128], 0.0)
    r = jnp.concatenate([relax_of(rate[...], flags[...]), ends], axis=1)
    table[0:8, :] = jnp.broadcast_to(r, (8, WIDE))
    a = speeds_of((16, WIDE))
    stay = 1.0 - jnp.broadcast_to(r, (16, WIDE)) - a

    def before(x):
        return jnp.where(positive, shift_up(x), shift_down(x))

    once = before(stay)
    two = before(once)
    t0 = stay * stay * stay
    t1 = a * (stay * (stay + once) + once * once)
    t2 = a * a * (stay + once + two)
    t3 = a * a * a
    waits[2].wait()
    back = (lanes_of((CELLS, CELLS)) - rows_of((CELLS, CELLS))) * towards
    at8 = rows_of((8, CELLS))
    at8 = jnp.where(positive, at8 - 8, at8 + CELLS)
    back8 = (lanes_of((8, CELLS)) - at8) * towards
    for u in range(2):
        ts = [x[8 * u : 8 * u + 1, 0:CELLS] for x in (t0, t1, t2, t3)]

        def band(distance):
            value = jnp.zeros(distance.shape, f32)
            for n, x in enumerate(ts):
                value = jnp.where(distance == n, jnp.broadcast_to(x, distance.shape), value)
            return value

        b = band(back)
        bh = b.astype(bf16)
        bl = (b - bh.astype(f32)).astype(bf16)
        b8 = band(back8)
        b8h = b8.astype(bf16).astype(f32)
        b8 = jnp.concatenate([b8h, b8 - b8h], axis=0).astype(bf16)
        rows = pl.ds(u * BLOCK, BLOCK)
        x = dist[rows, :]
        value = jnp.dot(x, bh, preferred_element_type=f32)
        value += jnp.dot(x, bl, preferred_element_type=f32)
        h = halo[:, rows]
        h = jnp.concatenate([h, h], axis=0).astype(bf16)
        value += lax.dot_general(h, b8, (((0,), (0,)), ((), ())), preferred_element_type=f32)
        out[rows, :] = value

    for copy in waits[3:]:
        copy.wait()
    table[8:24, 0:128] = jnp.zeros((16, 128), f32)
    table[8 : 8 + K, 0:K] = coupling_raw[...]
    c = table[8:24, 0:128]
    ch = c.astype(bf16).astype(f32)
    cm = (c - ch).astype(bf16).astype(f32)
    pieces = [ch, ch, ch, cm, cm, c - ch - cm]
    six = pieces[0]
    for n in range(1, 6):
        six = six + pltpu.roll(pieces[n], 16 * n, 1)
    block[0:16, 128:256] = six.astype(bf16)
    block[176:192, 128:256] = own6[...]
    shape = (16, K)
    chosen = jnp.where(lanes_of(shape) == rows_of(shape), jnp.broadcast_to(diff_raw[...], shape), 0.0)
    table[8:24, 128:256] = jnp.broadcast_to(jnp.sum(chosen, axis=1, keepdims=True), (16, 128))


UPDATE_ROWS = 512


def update_kernel(
    n_space,
    partial,
    fields,
    known,
    block,
    base,
    out,
    macro,
    done,
    macro_part,
    sems,
):
    place = lax.axis_index("vel")
    positive = place >= PEERS // 2
    total = partial[0]
    for j in range(1, n_space):
        total = total + partial[j]
    total = total * known[48:56, 0:128]
    cpl = known[8:24, 0:128]
    lane16 = lanes_of((16, 128))
    row16 = rows_of((16, 128))
    size = jnp.sum(jnp.abs(cpl), axis=1, keepdims=True)
    middle = jnp.sum(jnp.where(lane16 == row16, cpl, 0.0), axis=1, keepdims=True)
    real = row16[:, 0:1] < K
    most = jnp.max(jnp.where(real, size + 4.0 * known[8:24, 128:129], 0.0), axis=0, keepdims=True)
    least = jnp.min(jnp.where(real, 2.0 * middle - size, 1e30), axis=0, keepdims=True)
    low_step, high_step = 1.0 / most, 1.0 / least

    def summed(weighted, which):
        picked = jnp.where(known[24:32, 0:128] == which, weighted, 0.0)
        return jnp.sum(jnp.sum(picked, axis=0, keepdims=True), axis=1, keepdims=True)

    def clipped(x):
        return jnp.minimum(jnp.maximum(x, low_step), high_step)

    def weights_of(stage, weighted):
        rr, ra, aa, aaa = (summed(weighted, 4 * stage + n) for n in range(4))
        s1 = clipped(rr / ra)
        rr2 = rr - 2.0 * s1 * ra + s1 * s1 * aa
        ra2 = ra - 2.0 * s1 * aa + s1 * s1 * aaa
        s2 = clipped(rr2 / ra2)
        return s1 + s2, -s1 * s2

    li, ri = (known[n : n + 8, 0:128].astype(jnp.int32) for n in (32, 40))

    def choose(index, zero, one, two):
        return jnp.where(index == 0, zero, jnp.where(index == 1, one, two))

    a1, b1 = weights_of(0, total)
    a2, b2 = weights_of(1, total * choose(li, 1.0, a1, b1) * choose(ri, 1.0, a1, b1))

    def both(index):
        outer = (index >= 3).astype(jnp.int32) + (index >= 6).astype(jnp.int32)
        return choose(outer, 1.0, a2, b2) * choose(index - 3 * outer, 1.0, a1, b1)

    a3, b3 = weights_of(2, total * both(li) * both(ri))

    start, shares, res, e = (fields[n] for n in range(4))
    corr1 = a1 * res + b1 * e
    cur1 = shares + corr1
    res2 = fields[4] + a1 * fields[5] + b1 * fields[6]
    e2 = fields[7] + a1 * fields[8] + b1 * fields[9]
    corr2 = a2 * res2 + b2 * e2
    cur2 = res2 + cur1 + corr2

    def third(at):
        rows = [fields[at + 3 * n] + a1 * fields[at + 3 * n + 1] + b1 * fields[at + 3 * n + 2] for n in range(3)]
        return rows[0] + a2 * rows[1] + b2 * rows[2]

    res3, e3 = third(10), third(19)
    corr3 = a3 * res3 + b3 * e3
    cur3 = res3 + cur2 + corr3
    mine = pltpu.roll(cur3[:, 0:CELLS], lax.rem(CELLS - 16 * place, CELLS), 1)
    macro_part[...] = mine[0:K, 0:16]
    macro_copy = pltpu.make_async_copy(macro_part, macro, sems.at[ROWS // UPDATE_ROWS])
    macro_copy.start()

    r = jnp.broadcast_to(known[0:1, :], (16, WIDE))
    row = rows_of((16, WIDE))
    scaled = r * jnp.where(row < 5, 1.0, jnp.where(row < 10, 0.0, 1.0 / 3.0))
    f1 = scaled * start + corr1
    f2 = scaled * cur1 + corr2
    f3 = scaled * cur2 + corr3
    y = jnp.dot(block[176:192, 128:224], stack6(jnp.concatenate([f1, f2, f3], axis=1)), preferred_element_type=f32)
    y1, y2, y3 = (y[:, n * WIDE : (n + 1) * WIDE] for n in range(3))
    a = speeds_of((16, WIDE))

    def before(x):
        return jnp.where(positive, shift_up(x), shift_down(x))

    stay = 1.0 - r - a

    def moved(x):
        return stay * x + a * before(x)

    h = (moved(moved(y1) + y2) + y3)[:, 0:CELLS]
    hh = h.astype(bf16).astype(f32)
    hm = (h - hh).astype(bf16).astype(f32)

    sends = [macro_copy]
    for u in range(2):
        hu, mu = hh[8 * u : 8 * u + 8], hm[8 * u : 8 * u + 8]
        mixed = jnp.concatenate([hu, mu, hu, jnp.zeros((104, CELLS), f32)], axis=0).astype(bf16)
        for n in range(BLOCK // UPDATE_ROWS):
            part = u * (BLOCK // UPDATE_ROWS) + n
            rows = pl.ds(part * UPDATE_ROWS, UPDATE_ROWS)
            value = jnp.dot(block[pl.ds(n * UPDATE_ROWS, UPDATE_ROWS), 0:128], mixed, preferred_element_type=f32)
            done[rows, :] = (base[rows, :] + value).astype(bf16)
            copy = pltpu.make_async_copy(done.at[rows, :], out.at[rows, :], sems.at[part])
            copy.start()
            sends.append(copy)
    for copy in sends:
        copy.wait()


def vmem():
    return pl.BlockSpec(memory_space=pltpu.VMEM)


def hbm():
    return pl.BlockSpec(memory_space=pltpu.HBM)


def shaped(shape, dtype=f32):
    return pltpu.VMEM(shape, dtype)


def stored(shape, dtype=f32):
    return pltpu.HBM(shape, dtype)


def placed_at(space, arrays):
    return [pltpu.with_memory_space_constraint(x, space) for x in arrays]


def near(*arrays):
    return placed_at(pltpu.VMEM, arrays)


def far(*arrays):
    return placed_at(pltpu.HBM, arrays)


def limit(mib):
    return pltpu.CompilerParams(vmem_limit_bytes=mib * 2**20)


def make_per_device(n_space):
    block, p3, own6 = grid_constants()
    pairs = pair_arrays()

    def per_device(velocity_dist, macro_state, collision_rate, wall_flags, diffusivity, coupling):
        rate = collision_rate.reshape(1, CELLS)
        flags = wall_flags.reshape(1, CELLS)
        sums, up, down, edge, owned = pl.pallas_call(
            sums_kernel,
            out_shape=(
                shaped((16, CELLS)),
                shaped((16, 128)),
                shaped((16, 128)),
                shaped((8, ROWS + 128)),
                shaped((16, 128)),
            ),
            in_specs=[hbm()] * 5,
            out_specs=(vmem(),) * 5,
            scratch_shapes=[
                pltpu.VMEM((ROWS, CELLS), bf16),
                pltpu.VMEM((32, BLOCK), bf16),
                pltpu.VMEM((K, 16), f32),
                pltpu.VMEM((1, CELLS), f32),
                pltpu.VMEM((1, CELLS), jnp.int32),
                pltpu.VMEM((16, 128), f32),
                pltpu.SemaphoreType.DMA((6,)),
            ],
            compiler_params=limit(8),
            name="sums",
        )(*far(velocity_dist, jnp.asarray(p3), macro_state, rate, flags))
        rising = [(i, i + 1) for i in range(n_space - 1)]
        falling = [(j, i) for i, j in rising]
        from_left = lax.ppermute(up, "space", rising)
        from_right = lax.ppermute(down, "space", falling)
        packed = pl.pallas_call(
            pack_kernel,
            out_shape=stored((PEERS, 16, WIDE)),
            in_specs=[vmem()] * 4,
            out_specs=hbm(),
            scratch_shapes=[pltpu.VMEM((16, WIDE), f32), pltpu.SemaphoreType.DMA((PEERS,))],
            compiler_params=limit(4),
            name="pack",
        )(*near(sums, from_left, from_right, owned))
        got = lax.all_to_all(packed, "vel", split_axis=0, concat_axis=0, tiled=True)
        half = PEERS // 2
        upwind = [(i * PEERS + n, j * PEERS + n) for i, j in rising for n in range(half, PEERS)]
        upwind += [(j * PEERS + n, i * PEERS + n) for i, j in rising for n in range(half)]
        halo = lax.ppermute(edge, ("space", "vel"), upwind)
        base, known, constants = pl.pallas_call(
            stream_kernel,
            out_shape=(shaped((ROWS, CELLS)), shaped((56, WIDE)), shaped(block.shape, bf16)),
            in_specs=[vmem()] + [hbm()] * 8,
            out_specs=(vmem(),) * 3,
            scratch_shapes=[
                pltpu.VMEM((ROWS, CELLS), bf16),
                pltpu.VMEM((16, 128), bf16),
                pltpu.VMEM((K, K), f32),
                pltpu.VMEM((1, K), f32),
                pltpu.VMEM((1, CELLS), f32),
                pltpu.VMEM((1, CELLS), jnp.int32),
                pltpu.SemaphoreType.DMA((8,)),
            ],
            compiler_params=limit(16),
            name="stream",
        )(
            *near(halo),
            *far(velocity_dist, *(jnp.asarray(x) for x in (block, pairs, own6)), coupling, diffusivity.reshape(1, K), rate, flags),
        )
        got, base = lax.optimization_barrier((got, base))
        fields, partial = pl.pallas_call(
            lambda *refs: fields_kernel(n_space, *refs),
            out_shape=(shaped((N_FIELDS, 16, WIDE)), stored((n_space, 8, 128))),
            in_specs=[vmem()] * 3,
            out_specs=(vmem(), hbm()),
            scratch_shapes=[
                pltpu.VMEM((256, 128), f32),
                pltpu.VMEM((8, 128), f32),
                pltpu.SemaphoreType.DMA((n_space,)),
            ],
            compiler_params=limit(12),
            name="fields",
        )(*near(got, known, constants))
        partial = lax.all_to_all(partial, "space", split_axis=0, concat_axis=0, tiled=True)
        return pl.pallas_call(
            lambda *refs: update_kernel(n_space, *refs),
            out_shape=(stored((ROWS, CELLS), bf16), stored((K, 16))),
            in_specs=[vmem()] * 5,
            out_specs=(hbm(), hbm()),
            scratch_shapes=[
                pltpu.VMEM((ROWS, CELLS), bf16),
                pltpu.VMEM((K, 16), f32),
                pltpu.SemaphoreType.DMA((ROWS // UPDATE_ROWS + 1,)),
            ],
            compiler_params=limit(12),
            name="update",
        )(*near(partial, fields, known, constants, base))

    return per_device


def solution(mesh):
    placed = (P("vel", "space"), P(None, ("space", "vel")), P("space"), P("space"), P(), P())
    return jax.shard_map(
        make_per_device(mesh.shape["space"]),
        mesh=mesh,
        in_specs=placed,
        out_specs=(P("vel", "space"), P(None, ("space", "vel"))),
        check_vma=False,
    )
```

time: 66.1 us -> 55.7 us (0.84)
  blocking collectives: 0 us -> 19.1 us
  starting transfers between devices: 24.3 us -> 14.2 us
  waiting for transfers between devices: 19.2 us -> 10.8 us
  Pallas kernels: 15.7 us -> 10.2 us
  local copies, waits for them, and re-layouts: 4.07 us -> 0 us
  other arithmetic: 1.25 us -> 0 us
    all_to_all x0 -> x1, blocking collectives: none -> 19.1 us  [per_device(): lax.all_to_all(partial, 'space', split_axis=0, concat_axis=0, tiled=True)]
    all_to_all x1 -> x0, starting transfers between devices: 9.93 us -> none  [per_device(): lax.all_to_all(partial, 'space', split_axis=0, concat_axis=0, tiled=True)]
    all_to_all x1, waiting for transfers between devices: 9.5 us -> 1.07 us  [per_device(): got = lax.all_to_all(packed, 'vel', split_axis=0, concat_axis=0, tiled=True)]
    pallas_call x4 -> x5, Pallas kernels: 15.7 us -> 10.2 us  [the longest x1 2.85 us: per_device(): pl.pallas_call(lambda *refs: fields_kernel(n_space, *refs), out_shape=(sh...]
    unnamed x20 -> x0, local copies, waits for them, and re-layouts: 1.97 us -> none
    pad x3 -> x0, local copies, waits for them, and re-layouts: 1.27 us -> none  [the longest x1 0.67 us: per_device(): owned = jnp.pad(macro_state, ((0, 3), (16, 96)))]
    ppermute x1, waiting for transfers between devices: 4.48 us -> 5.35 us  [per_device(): halo = lax.ppermute(edge, ('space', 'vel'), upwind)]
    broadcast_in_dim x1 -> x0, local copies, waits for them, and re-layouts: 0.72 us -> none  [per_device(): jnp.broadcast_to(jnp.pad(diffusivity, (0, 3))[:, None], (16, 128))]
  transfers between devices with their start and end apart: 5 -> 4, of which waited for: 4 -> 3; matrix products, arithmetic and copies ran while one was open for 2% -> 0% of each run, Pallas kernels for 0% -> 5%
where the time goes in v2:
time: 55.7 us; the launch traced here: 55 us
  blocking collectives  19.1 us (34%)
  starting transfers between devices  14.2 us (25%)
  waiting for transfers between devices  10.8 us (19%)
  Pallas kernels  10.2 us (18%)
  between operations  0.7 us (1%)
    all_to_all x1, blocking collectives, per_device(): lax.all_to_all(partial, 'space', split_axis=0, concat_axis=0, tiled=True)  19.1 us
    all_to_all x1, starting transfers between devices, per_device(): got = lax.all_to_all(packed, 'vel', split_axis=0, concat_axis=0, tiled=True)  6.44 us
    ppermute x1, waiting for transfers between devices, per_device(): halo = lax.ppermute(edge, ('space', 'vel'), upwind)  5.35 us
    ppermute x1, waiting for transfers between devices, per_device(): from_right = lax.ppermute(down, 'space', falling)  4.38 us
    ppermute x1, starting transfers between devices, per_device(): from_left = lax.ppermute(up, 'space', rising)  3.8 us
    pallas_call x1, Pallas kernels, per_device(): pl.pallas_call(lambda *refs: fields_kernel(n_space, *refs), out_shape=(sh...  2.85 us
    pallas_call x1, Pallas kernels, per_device(): pl.pallas_call(stream_kernel, out_shape=(shaped((ROWS, CELLS)), shaped((5...  2.57 us
    ppermute x1, starting transfers between devices, per_device(): from_right = lax.ppermute(down, 'space', falling)  2.04 us
  transfers between devices with their start and end apart: 4, of which 3 were waited for; matrix products, arithmetic and copies ran while one was open for 0% of the time, Pallas kernels for 5%

profile of v2, /device:TPU:2, one launch (start us, length us, event | category | flops | bytes accessed | tf_op | source)
XLA Modules:
  0.0 55.0 jit_solution(12629880951016584974)
XLA Ops:
  0.6 2.0 %sums.1 = (f32[16,256]{1,0:T(8,128)S(1)}, f32[16,128]{1,0:T(8,128)S(1)}, f32[16,128]{1,0:T(8,128)S(1)}, f32[8,2176]{1,0:T(8,128)S(1)}, f32[16,128]{1,0:T(8,128)S(1)}) custom-call(bf16[2048,256]{1,0:T(8,128)(2,1)} %dist_in.3, bf16[32,1024]{1,0:T(8,128)(2,1)} %constant.8.clone.p3_in, f32[13,16]{1,0:T(8,128)} %start_in.1, f32[1,256]{1,0:T(1,128)} %bitcast.3, ...), custom_call_target="tpu_custom_call" | custom-call | tf_op jit(solution)/shard_map/sums/pallas_call | solution.py:666
  2.6 3.8 %collective-permute-start = (f32[16,128]{1,0:T(8,128)S(1)}, f32[16,128]{1,0:T(8,128)S(1)}, u32[]{:S(2)}, u32[]{:S(2)}) collective-permute-start(f32[16,128]{1,0:T(8,128)S(1)} %get-tuple-element.15), channel_id=1, source_target_pairs={{0,16},{16,32},{32,48},{48,64},{64,80},{80,96},{96,112},{112,128},... | collective-permute-start | bytes 24584 | tf_op jit(solution)/shard_map/ppermute | solution.py:691
  6.4 2.0 %collective-permute-start.1 = (f32[16,128]{1,0:T(8,128)S(1)}, f32[16,128]{1,0:T(8,128)S(1)}, u32[]{:S(2)}, u32[]{:S(2)}) collective-permute-start(f32[16,128]{1,0:T(8,128)S(1)} %get-tuple-element.16), channel_id=1, source_target_pairs={{16,0},{32,16},{48,32},{64,48},{80,64},{96,80},{112,96},{128,112},... | collective-permute-start | bytes 24584 | tf_op jit(solution)/shard_map/ppermute | solution.py:692
  8.5 0.0 collective-permute-done.up
  8.5 4.4 %collective-permute-done.1.down = f32[16,128]{1,0:T(8,128)S(1)} collective-permute-done((f32[16,128]{1,0:T(8,128)S(1)}, f32[16,128]{1,0:T(8,128)S(1)}, u32[]{:S(2)}, u32[]{:S(2)}) %collective-permute-start.1) | collective-permute-done | bytes 8224 | tf_op jit(solution)/shard_map/ppermute | solution.py:692
  12.9 0.9 %pack.1 = f32[16,16,384]{2,1,0:T(8,128)} custom-call(f32[16,256]{1,0:T(8,128)S(1)} %get-tuple-element.14.sums, f32[16,128]{1,0:T(8,128)S(1)} %collective-permute-done.up, f32[16,128]{1,0:T(8,128)S(1)} %collective-permute-done.1.down, f32[16,128]{1,0:T(8,128)S(1)} %get-tuple-element.17.owned), custom_call_target="tpu_custom_call" | custom-call | tf_op jit(solution)/shard_map/pack/pallas_call | solution.py:693
  13.7 6.4 %all-to-all-start = ((f32[16,16,384]{2,1,0:T(8,128)}), f32[16,16,384]{2,1,0:T(8,128)S(1)}, u32[]{:S(2)}, u32[]{:S(2)}) async-start(f32[16,16,384]{2,1,0:T(8,128)} %pack.1), calls=%async_computation | async-start | bytes 786432 | tf_op jit(solution)/shard_map/all_to_all | solution.py:702
  20.2 1.9 %collective-permute-start.2 = (f32[8,2176]{1,0:T(8,128)S(1)}, f32[8,2176]{1,0:T(8,128)S(1)}, u32[]{:S(2)}, u32[]{:S(2)}) collective-permute-start(f32[8,2176]{1,0:T(8,128)S(1)} %get-tuple-element.18), channel_id=1, source_target_pairs={{8,24},{9,25},{10,26},{11,27},{12,28},{13,29},{14,30},{15,31},{24,... | collective-permute-start | bytes 208904 | tf_op jit(solution)/shard_map/ppermute | solution.py:706
  22.1 5.3 %collective-permute-done.2.halo = f32[8,2176]{1,0:T(8,128)S(1)} collective-permute-done((f32[8,2176]{1,0:T(8,128)S(1)}, f32[8,2176]{1,0:T(8,128)S(1)}, u32[]{:S(2)}, u32[]{:S(2)}) %collective-permute-start.2) | collective-permute-done | bytes 69664 | tf_op jit(solution)/shard_map/ppermute | solution.py:706
  27.5 2.6 %stream.1 = (f32[2048,256]{1,0:T(8,128)S(1)}, f32[56,384]{1,0:T(8,128)S(1)}, bf16[1360,256]{1,0:T(8,128)(2,1)S(1)}) custom-call(f32[8,2176]{1,0:T(8,128)S(1)} %collective-permute-done.2.halo, bf16[2048,256]{1,0:T(8,128)(2,1)} %dist_in.3, bf16[1360,256]{1,0:T(8,128)(2,1)} %constant.9.clone.block_in, f32[32,128]{1,0:T(8,128)} %constant.10.clone.pairs_in, ...), custom_call_target="tpu_custom_call" | custom-call | tf_op jit(solution)/shard_map/stream/pallas_call | solution.py:707
  30.0 1.1 %all-to-all-done.refs_0_ = f32[16,16,384]{2,1,0:T(8,128)S(1)} async-done(((f32[16,16,384]{2,1,0:T(8,128)}), f32[16,16,384]{2,1,0:T(8,128)S(1)}, u32[]{:S(2)}, u32[]{:S(2)}) %all-to-all-start) | async-done | bytes 393248 | tf_op jit(solution)/shard_map/all_to_all | solution.py:702
  31.1 2.8 %fields.1 = (f32[28,16,384]{2,1,0:T(8,128)S(1)}, f32[16,8,128]{2,1,0:T(8,128)}) custom-call(f32[16,16,384]{2,1,0:T(8,128)S(1)} %all-to-all-done.refs_0_, f32[56,384]{1,0:T(8,128)S(1)} %get-tuple-element.21.refs_1_.refs_2_, bf16[1360,256]{1,0:T(8,128)(2,1)S(1)} %get-tuple-element.22.refs_2_.refs_3_), custom_call_target="tpu_custom_call" | custom-call | tf_op jit(solution)/shard_map/fields/pallas_call | solution.py:728
  34.0 19.1 %all_to_all.10.refs_0_ = f32[16,8,128]{2,1,0:T(8,128)S(1)} all-to-all(f32[16,8,128]{2,1,0:T(8,128)} %get-tuple-element.23), channel_id=1, replica_groups=mesh['space'=16,'vel'=16] {'space'}, dimensions={0} | all-to-all | bytes 131072 | tf_op jit(solution)/shard_map/all_to_all | solution.py:741
  53.0 2.0 %update.1 = (bf16[2048,256]{1,0:T(8,128)(2,1)}, f32[13,16]{1,0:T(8,128)}) custom-call(f32[16,8,128]{2,1,0:T(8,128)S(1)} %all_to_all.10.refs_0_, f32[28,16,384]{2,1,0:T(8,128)S(1)} %get-tuple-element.24.refs_1_, f32[56,384]{1,0:T(8,128)S(1)} %get-tuple-element.21.refs_1_.refs_2_, bf16[1360,256]{1,0:T(8,128)(2,1)S(1)} %get-tuple-element.22.refs_2_.refs_3_, ...), custom_call_target="tpu_custom_call" | custom-call | tf_op jit(solution)/shard_map/update/pallas_call | solution.py:742
Async XLA Ops:
  2.6 5.9 %collective-permute-start = (f32[16,128]{1,0:T(8,128)S(1)}, f32[16,128]{1,0:T(8,128)S(1)}, u32[]{:S(2)}, u32[]{:S(2)}) collective-permute-start(f32[16,128]{1,0:T(8,128)S(1)} %get-tuple-element.15), channel_id=1, source_target_pairs={{0,16},{16,32},{32,48},{48,64},{64,80},{80,96},{96,112},{112,128},... | collective-permute-start | bytes 24584 | tf_op jit(solution)/shard_map/ppermute | solution.py:691
  6.4 6.4 %collective-permute-start.1 = (f32[16,128]{1,0:T(8,128)S(1)}, f32[16,128]{1,0:T(8,128)S(1)}, u32[]{:S(2)}, u32[]{:S(2)}) collective-permute-start(f32[16,128]{1,0:T(8,128)S(1)} %get-tuple-element.16), channel_id=1, source_target_pairs={{16,0},{32,16},{48,32},{64,48},{80,64},{96,80},{112,96},{128,112},... | collective-permute-start | bytes 24584 | tf_op jit(solution)/shard_map/ppermute | solution.py:692
  13.7 17.4 %all-to-all-start = ((f32[16,16,384]{2,1,0:T(8,128)}), f32[16,16,384]{2,1,0:T(8,128)S(1)}, u32[]{:S(2)}, u32[]{:S(2)}) async-start(f32[16,16,384]{2,1,0:T(8,128)} %pack.1), calls=%async_computation | async-start | bytes 786432 | tf_op jit(solution)/shard_map/all_to_all | solution.py:702
  20.2 7.3 %collective-permute-start.2 = (f32[8,2176]{1,0:T(8,128)S(1)}, f32[8,2176]{1,0:T(8,128)S(1)}, u32[]{:S(2)}, u32[]{:S(2)}) collective-permute-start(f32[8,2176]{1,0:T(8,128)S(1)} %get-tuple-element.18), channel_id=1, source_target_pairs={{8,24},{9,25},{10,26},{11,27},{12,28},{13,29},{14,30},{15,31},{24,... | collective-permute-start | bytes 208904 | tf_op jit(solution)/shard_map/ppermute | solution.py:706

commit v3 on v2

--- a/solution.py
+++ b/solution.py
@@ -183,9 +183,8 @@
     rate_in,
     flags_in,
     sums,
-    up,
-    down,
-    edge,
+    ahead,
+    back,
     owned,
     dist,
     p3,
@@ -216,39 +215,37 @@
     mine = pltpu.roll(padded[...], 16, 1)
     owned[...] = mine
     relax = relax_of(rate[...], flags[...])
-    near_edge = jnp.where(positive, relax[:, 128:256], relax[:, 0:128])
-    edge[:, ROWS : ROWS + 128] = jnp.broadcast_to(near_edge, (8, 128))
     r_first = jnp.broadcast_to(pltpu.roll(relax[:, 0:128], 48, 1), (16, 128))
     r_last = jnp.broadcast_to(pltpu.roll(relax[:, 128:256], 48, 1), (16, 128))
     zero = jnp.zeros((16, 128), f32)
-    up[...] = (
+    up = (
         jnp.where(lane >= 120, w[:, 128:256], zero)
         + pltpu.roll(mine, 16, 1)
         + jnp.where((row == K) & (lane >= 32) & (lane < 48), r_last, zero)
     )
-    down[...] = (
+    down = (
         jnp.where(lane < 8, w[:, 0:128], zero)
         + pltpu.roll(mine, 32, 1)
         + jnp.where((row == K) & (lane >= 48) & (lane < 64), r_first, zero)
     )
+    ahead[0:16, :] = jnp.where(positive, up, down)
+    back[...] = jnp.where(positive, down, up)
     e_lane = lanes_of((16, CELLS))
     e_row = rows_of((16, CELLS))
-    first = jnp.where(positive, CELLS - 8, 0)
-    pick = jnp.where((e_lane == e_row + first) & (e_row < 8), 1.0, 0.0).astype(bf16)
+    cell = jnp.where(positive, CELLS - 1 - e_row, e_row)
+    pick = jnp.where((e_lane == cell) & (e_row < 3), 1.0, 0.0).astype(bf16)
     for u in range(2):
-        e = lax.dot_general(
-            pick,
-            dist[pl.ds(u * BLOCK, BLOCK), :],
-            (((1,), (1,)), ((), ())),
-            preferred_element_type=f32,
-        )
-        edge[:, pl.ds(u * BLOCK, BLOCK)] = e[0:8]
-
-
-def pack_kernel(sums, up, down, owned, out, whole, sems):
+        e = lax.dot_general(pick, dist[halves[u], :], (((1,), (1,)), ((), ())), preferred_element_type=f32)
+        for n in range(3):
+            for k in range(8):
+                at = 16 + 16 * n + 8 * u + k
+                ahead[at : at + 1, :] = e[n : n + 1, 128 * k : 128 * k + 128]
+
+
+def pack_kernel(sums, ahead, back, owned, out, edges, whole, sems):
     whole[:, 0:CELLS] = sums[...]
-    whole[:, CELLS:WIDE] = up[...] + down[...] + owned[...]
-    for copy in copies_of([(whole, out.at[j]) for j in range(PEERS)], sems):
+    whole[:, CELLS:WIDE] = ahead[0:16, :] + back[...] + owned[...]
+    for copy in copies_of([(whole, out.at[j]) for j in range(PEERS)] + [(ahead.at[16:64, :], edges)], sems):
         copy.wait()
 
 
@@ -292,11 +289,15 @@
     start = jnp.concatenate([halves[0], halves[1], ends], axis=1)
     start = jnp.where(rows_of((16, WIDE)) < K, start, 0.0)
     relax_ends = jnp.where((lane1 < 8) | (lane1 >= 120), from_first, zero)[K : K + 1]
-    relax1 = jnp.concatenate([known[0:1, 0:CELLS], relax_ends], axis=1)
+    relax1 = jnp.concatenate([known[16:17, 0:CELLS], relax_ends], axis=1)
     r = jnp.broadcast_to(relax1, (16, WIDE))
+    fields[N_FIELDS] = r
+    for n in range(3):
+        fields[N_FIELDS + 1 + n] = known[16 * n : 16 * n + 16, :]
+    fields[N_FIELDS + 4, 0:8] = known[48:56, :]
     keep = 1.0 - r
     mask = jnp.broadcast_to(mask, (16, WIDE))
-    diffusion = jnp.concatenate([known[8:24, 128:256]] * 3, axis=1)
+    diffusion = jnp.concatenate([known[0:16, 128:256]] * 3, axis=1)
 
     def advance(base, ups, downs):
         new = keep * base - diff_up(ups[0]) - diff_down(downs[0])
@@ -412,9 +413,7 @@
     return time_step * jnp.abs((number.astype(f32) + 0.5) * spacing - 4.0)
 
 
-def stream_kernel(
-    halo,
-    dist_in,
+def prep_kernel(
     block_in,
     pairs_in,
     own_in,
@@ -422,10 +421,8 @@
     diff_in,
     rate_in,
     flags_in,
-    out,
     table,
     block,
-    dist,
     own6,
     coupling_raw,
     diff_raw,
@@ -434,18 +431,42 @@
     sems,
 ):
     vel = lax.axis_index("vel")
-    positive = vel >= PEERS // 2
-    moves = [(rate_in, rate), (flags_in, flags), (dist_in, dist), (coupling_in, coupling_raw), (diff_in, diff_raw)]
+    moves = [(rate_in, rate), (flags_in, flags), (coupling_in, coupling_raw), (diff_in, diff_raw)]
     moves += [(own_in.at[vel], own6), (pairs_in, table.at[24:56, 0:128]), (block_in, block)]
     waits = copies_of(moves, sems)
     waits[0].wait()
     waits[1].wait()
+    table[16:24, 0:CELLS] = jnp.broadcast_to(relax_of(rate[...], flags[...]), (8, CELLS))
+    for copy in waits[2:]:
+        copy.wait()
+    table[0:16, 0:128] = jnp.zeros((16, 128), f32)
+    table[0:K, 0:K] = coupling_raw[...]
+    c = table[0:16, 0:128]
+    ch = c.astype(bf16).astype(f32)
+    cm = (c - ch).astype(bf16).astype(f32)
+    pieces = [ch, ch, ch, cm, cm, c - ch - cm]
+    six = pieces[0]
+    for n in range(1, 6):
+        six = six + pltpu.roll(pieces[n], 16 * n, 1)
+    block[0:16, 128:256] = six.astype(bf16)
+    block[176:192, 128:256] = own6[...]
+    shape = (16, K)
+    chosen = jnp.where(lanes_of(shape) == rows_of(shape), jnp.broadcast_to(diff_raw[...], shape), 0.0)
+    table[0:16, 128:256] = jnp.broadcast_to(jnp.sum(chosen, axis=1, keepdims=True), (16, 128))
+
+
+def stream_kernel(fields, _, edges_in, dist_in, out, dist, edges, ends, sems):
+    waits = copies_of([(edges_in, edges), (dist_in, dist)], sems)
+    positive = lax.axis_index("vel") >= PEERS // 2
     towards = jnp.where(positive, 1, -1)
-    lane = lanes_of((1, 128))
-    low = jnp.where(positive, 120, 0)
-    ends = jnp.where((lane >= low) & (lane < low + 8), halo[0:1, ROWS : ROWS + 128], 0.0)
-    r = jnp.concatenate([relax_of(rate[...], flags[...]), ends], axis=1)
-    table[0:8, :] = jnp.broadcast_to(r, (8, WIDE))
+    ends[...] = jnp.zeros((16, ROWS), f32)
+    waits[0].wait()
+    for n in range(3):
+        for k in range(16):
+            row = edges[16 * n + k : 16 * n + k + 1, :]
+            ends[n : n + 1, 128 * k : 128 * k + 128] = row
+            ends[8 + n : 9 + n, 128 * k : 128 * k + 128] = row
+    r = fields[N_FIELDS, 0:1, :]
     a = speeds_of((16, WIDE))
     stay = 1.0 - jnp.broadcast_to(r, (16, WIDE)) - a
 
@@ -458,10 +479,10 @@
     t1 = a * (stay * (stay + once) + once * once)
     t2 = a * a * (stay + once + two)
     t3 = a * a * a
-    waits[2].wait()
+    waits[1].wait()
     back = (lanes_of((CELLS, CELLS)) - rows_of((CELLS, CELLS))) * towards
     at8 = rows_of((8, CELLS))
-    at8 = jnp.where(positive, at8 - 8, at8 + CELLS)
+    at8 = jnp.where(positive, -1 - at8, at8 + CELLS)
     back8 = (lanes_of((8, CELLS)) - at8) * towards
     for u in range(2):
         ts = [x[8 * u : 8 * u + 1, 0:CELLS] for x in (t0, t1, t2, t3)]
@@ -482,27 +503,9 @@
         x = dist[rows, :]
         value = jnp.dot(x, bh, preferred_element_type=f32)
         value += jnp.dot(x, bl, preferred_element_type=f32)
-        h = halo[:, rows]
-        h = jnp.concatenate([h, h], axis=0).astype(bf16)
+        h = ends[:, rows].astype(bf16)
         value += lax.dot_general(h, b8, (((0,), (0,)), ((), ())), preferred_element_type=f32)
         out[rows, :] = value
-
-    for copy in waits[3:]:
-        copy.wait()
-    table[8:24, 0:128] = jnp.zeros((16, 128), f32)
-    table[8 : 8 + K, 0:K] = coupling_raw[...]
-    c = table[8:24, 0:128]
-    ch = c.astype(bf16).astype(f32)
-    cm = (c - ch).astype(bf16).astype(f32)
-    pieces = [ch, ch, ch, cm, cm, c - ch - cm]
-    six = pieces[0]
-    for n in range(1, 6):
-        six = six + pltpu.roll(pieces[n], 16 * n, 1)
-    block[0:16, 128:256] = six.astype(bf16)
-    block[176:192, 128:256] = own6[...]
-    shape = (16, K)
-    chosen = jnp.where(lanes_of(shape) == rows_of(shape), jnp.broadcast_to(diff_raw[...], shape), 0.0)
-    table[8:24, 128:256] = jnp.broadcast_to(jnp.sum(chosen, axis=1, keepdims=True), (16, 128))
 
 
 UPDATE_ROWS = 512
@@ -512,7 +515,6 @@
     n_space,
     partial,
     fields,
-    known,
     block,
     base,
     out,
@@ -523,22 +525,26 @@
 ):
     place = lax.axis_index("vel")
     positive = place >= PEERS // 2
+
+    def known(at):
+        return fields[N_FIELDS + 1 + at // 16, at % 16 : at % 16 + 8, 0:128]
+
     total = partial[0]
     for j in range(1, n_space):
         total = total + partial[j]
-    total = total * known[48:56, 0:128]
-    cpl = known[8:24, 0:128]
+    total = total * known(48)
+    cpl = fields[N_FIELDS + 1, :, 0:128]
     lane16 = lanes_of((16, 128))
     row16 = rows_of((16, 128))
     size = jnp.sum(jnp.abs(cpl), axis=1, keepdims=True)
     middle = jnp.sum(jnp.where(lane16 == row16, cpl, 0.0), axis=1, keepdims=True)
     real = row16[:, 0:1] < K
-    most = jnp.max(jnp.where(real, size + 4.0 * known[8:24, 128:129], 0.0), axis=0, keepdims=True)
+    most = jnp.max(jnp.where(real, size + 4.0 * fields[N_FIELDS + 1, :, 128:129], 0.0), axis=0, keepdims=True)
     least = jnp.min(jnp.where(real, 2.0 * middle - size, 1e30), axis=0, keepdims=True)
     low_step, high_step = 1.0 / most, 1.0 / least
 
     def summed(weighted, which):
-        picked = jnp.where(known[24:32, 0:128] == which, weighted, 0.0)
+        picked = jnp.where(known(24) == which, weighted, 0.0)
         return jnp.sum(jnp.sum(picked, axis=0, keepdims=True), axis=1, keepdims=True)
 
     def clipped(x):
@@ -552,7 +558,7 @@
         s2 = clipped(rr2 / ra2)
         return s1 + s2, -s1 * s2
 
-    li, ri = (known[n : n + 8, 0:128].astype(jnp.int32) for n in (32, 40))
+    li, ri = (known(n).astype(jnp.int32) for n in (32, 40))
 
     def choose(index, zero, one, two):
         return jnp.where(index == 0, zero, jnp.where(index == 1, one, two))
@@ -586,7 +592,7 @@
     macro_copy = pltpu.make_async_copy(macro_part, macro, sems.at[ROWS // UPDATE_ROWS])
     macro_copy.start()
 
-    r = jnp.broadcast_to(known[0:1, :], (16, WIDE))
+    r = fields[N_FIELDS]
     row = rows_of((16, WIDE))
     scaled = r * jnp.where(row < 5, 1.0, jnp.where(row < 10, 0.0, 1.0 / 3.0))
     f1 = scaled * start + corr1
@@ -663,17 +669,16 @@
     def per_device(velocity_dist, macro_state, collision_rate, wall_flags, diffusivity, coupling):
         rate = collision_rate.reshape(1, CELLS)
         flags = wall_flags.reshape(1, CELLS)
-        sums, up, down, edge, owned = pl.pallas_call(
+        sums, ahead, back, owned = pl.pallas_call(
             sums_kernel,
             out_shape=(
                 shaped((16, CELLS)),
+                shaped((64, 128)),
                 shaped((16, 128)),
-                shaped((16, 128)),
-                shaped((8, ROWS + 128)),
                 shaped((16, 128)),
             ),
             in_specs=[hbm()] * 5,
-            out_specs=(vmem(),) * 5,
+            out_specs=(vmem(),) * 4,
             scratch_shapes=[
                 pltpu.VMEM((ROWS, CELLS), bf16),
                 pltpu.VMEM((32, BLOCK), bf16),
@@ -687,47 +692,41 @@
             name="sums",
         )(*far(velocity_dist, jnp.asarray(p3), macro_state, rate, flags))
         rising = [(i, i + 1) for i in range(n_space - 1)]
-        falling = [(j, i) for i, j in rising]
-        from_left = lax.ppermute(up, "space", rising)
-        from_right = lax.ppermute(down, "space", falling)
-        packed = pl.pallas_call(
+        half = PEERS // 2
+        downwind = [(i * PEERS + n, j * PEERS + n) for i, j in rising for n in range(half, PEERS)]
+        downwind += [(j * PEERS + n, i * PEERS + n) for i, j in rising for n in range(half)]
+        upwind = [(j, i) for i, j in downwind]
+        ahead = lax.ppermute(ahead, ("space", "vel"), downwind)
+        back = lax.ppermute(back, ("space", "vel"), upwind)
+        packed, edges = pl.pallas_call(
             pack_kernel,
-            out_shape=stored((PEERS, 16, WIDE)),
+            out_shape=(stored((PEERS, 16, WIDE)), stored((48, 128))),
             in_specs=[vmem()] * 4,
-            out_specs=hbm(),
-            scratch_shapes=[pltpu.VMEM((16, WIDE), f32), pltpu.SemaphoreType.DMA((PEERS,))],
+            out_specs=(hbm(),) * 2,
+            scratch_shapes=[pltpu.VMEM((16, WIDE), f32), pltpu.SemaphoreType.DMA((PEERS + 1,))],
             compiler_params=limit(4),
             name="pack",
-        )(*near(sums, from_left, from_right, owned))
+        )(*near(sums, ahead, back, owned))
         got = lax.all_to_all(packed, "vel", split_axis=0, concat_axis=0, tiled=True)
-        half = PEERS // 2
-        upwind = [(i * PEERS + n, j * PEERS + n) for i, j in rising for n in range(half, PEERS)]
-        upwind += [(j * PEERS + n, i * PEERS + n) for i, j in rising for n in range(half)]
-        halo = lax.ppermute(edge, ("space", "vel"), upwind)
-        base, known, constants = pl.pallas_call(
-            stream_kernel,
-            out_shape=(shaped((ROWS, CELLS)), shaped((56, WIDE)), shaped(block.shape, bf16)),
-            in_specs=[vmem()] + [hbm()] * 8,
-            out_specs=(vmem(),) * 3,
+        known, constants = pl.pallas_call(
+            prep_kernel,
+            out_shape=(shaped((56, WIDE)), shaped(block.shape, bf16)),
+            in_specs=[hbm()] * 7,
+            out_specs=(vmem(),) * 2,
             scratch_shapes=[
-                pltpu.VMEM((ROWS, CELLS), bf16),
                 pltpu.VMEM((16, 128), bf16),
                 pltpu.VMEM((K, K), f32),
                 pltpu.VMEM((1, K), f32),
                 pltpu.VMEM((1, CELLS), f32),
                 pltpu.VMEM((1, CELLS), jnp.int32),
-                pltpu.SemaphoreType.DMA((8,)),
+                pltpu.SemaphoreType.DMA((7,)),
             ],
-            compiler_params=limit(16),
-            name="stream",
-        )(
-            *near(halo),
-            *far(velocity_dist, *(jnp.asarray(x) for x in (block, pairs, own6)), coupling, diffusivity.reshape(1, K), rate, flags),
-        )
-        got, base = lax.optimization_barrier((got, base))
+            compiler_params=limit(4),
+            name="prep",
+        )(*far(*(jnp.asarray(x) for x in (block, pairs, own6)), coupling, diffusivity.reshape(1, K), rate, flags))
         fields, partial = pl.pallas_call(
             lambda *refs: fields_kernel(n_space, *refs),
-            out_shape=(shaped((N_FIELDS, 16, WIDE)), stored((n_space, 8, 128))),
+            out_shape=(shaped((N_FIELDS + 5, 16, WIDE)), stored((n_space, 8, 128))),
             in_specs=[vmem()] * 3,
             out_specs=(vmem(), hbm()),
             scratch_shapes=[
@@ -738,11 +737,25 @@
             compiler_params=limit(12),
             name="fields",
         )(*near(got, known, constants))
+        base = pl.pallas_call(
+            stream_kernel,
+            out_shape=shaped((ROWS, CELLS)),
+            in_specs=[vmem()] * 2 + [hbm()] * 2,
+            out_specs=vmem(),
+            scratch_shapes=[
+                pltpu.VMEM((ROWS, CELLS), bf16),
+                pltpu.VMEM((48, 128), f32),
+                pltpu.VMEM((16, ROWS), f32),
+                pltpu.SemaphoreType.DMA((2,)),
+            ],
+            compiler_params=limit(16),
+            name="stream",
+        )(*near(fields, constants), *far(edges, velocity_dist))
         partial = lax.all_to_all(partial, "space", split_axis=0, concat_axis=0, tiled=True)
         return pl.pallas_call(
             lambda *refs: update_kernel(n_space, *refs),
             out_shape=(stored((ROWS, CELLS), bf16), stored((K, 16))),
-            in_specs=[vmem()] * 5,
+            in_specs=[vmem()] * 4,
             out_specs=(hbm(), hbm()),
             scratch_shapes=[
                 pltpu.VMEM((ROWS, CELLS), bf16),
@@ -751,7 +764,7 @@
             ],
             compiler_params=limit(12),
             name="update",
-        )(*near(partial, fields, known, constants, base))
+        )(*near(partial, fields, constants, base))
 
     return per_device
 

time: 55.7 us -> 56 us (level)
  blocking collectives: 19.1 us -> 0 us
  starting transfers between devices: 14.2 us -> 23.5 us
  waiting for transfers between devices: 10.8 us -> 16.7 us
  local copies, waits for them, and re-layouts: 0 us -> 3.16 us
  Pallas kernels: 10.2 us -> 11.5 us
    all_to_all x1 -> x0, blocking collectives: 19.1 us -> none  [per_device(): lax.all_to_all(partial, 'space', split_axis=0, concat_axis=0, tiled=True)]
    all_to_all x0 -> x1, starting transfers between devices: none -> 9.8 us  [per_device(): lax.all_to_all(partial, 'space', split_axis=0, concat_axis=0, tiled=True)]
    all_to_all x1, waiting for transfers between devices: 1.07 us -> 9.54 us  [per_device(): got = lax.all_to_all(packed, 'vel', split_axis=0, concat_axis=0, tiled=True)]
    ppermute x3 -> x2, waiting for transfers between devices: 9.73 us -> 2.95 us  [the longest x1 2.95 us: per_device(): back = lax.ppermute(back, ('space', 'vel'), upwind)]
    all_to_all x0 -> x1, waiting for transfers between devices: none -> 4.23 us  [per_device(): lax.all_to_all(partial, 'space', split_axis=0, concat_axis=0, tiled=True)]
    unnamed x0 -> x6, local copies, waits for them, and re-layouts: none -> 3.16 us
    pallas_call x3 -> x4, Pallas kernels: 5.41 us -> 6.63 us  [the longest x1 2.39 us: per_device(): pl.pallas_call(stream_kernel, out_shape=shaped((ROWS, CELLS)), in_specs=[...]
    ppermute x3 -> x2, starting transfers between devices: 7.76 us -> 6.74 us  [the longest x1 4.15 us: per_device(): ahead = lax.ppermute(ahead, ('space', 'vel'), downwind)]
  transfers between devices with their start and end apart: 4 -> 4, of which waited for: 3 -> 3; matrix products, arithmetic and copies ran while one was open for 0% -> 0% of each run, Pallas kernels for 5% -> 7%
where the time goes in v3:
time: 56 us; the launch traced here: 55.6 us
  starting transfers between devices  23.5 us (42%)
  waiting for transfers between devices  16.7 us (30%)
  Pallas kernels  11.5 us (21%)
  local copies, waits for them, and re-layouts  3.16 us (6%)
  between operations  0.71 us (1%)
    all_to_all x1, starting transfers between devices, per_device(): lax.all_to_all(partial, 'space', split_axis=0, concat_axis=0, tiled=True)  9.8 us
    all_to_all x1, waiting for transfers between devices, per_device(): got = lax.all_to_all(packed, 'vel', split_axis=0, concat_axis=0, tiled=True)  9.54 us
    all_to_all x1, starting transfers between devices, per_device(): got = lax.all_to_all(packed, 'vel', split_axis=0, concat_axis=0, tiled=True)  6.99 us
    all_to_all x1, waiting for transfers between devices, per_device(): lax.all_to_all(partial, 'space', split_axis=0, concat_axis=0, tiled=True)  4.23 us
    ppermute x1, starting transfers between devices, per_device(): ahead = lax.ppermute(ahead, ('space', 'vel'), downwind)  4.15 us
    unnamed x6, local copies, waits for them, and re-layouts  3.16 us
    ppermute x1, waiting for transfers between devices, per_device(): back = lax.ppermute(back, ('space', 'vel'), upwind)  2.95 us
    pallas_call x1, Pallas kernels, per_device(): pl.pallas_call(lambda *refs: fields_kernel(n_space, *refs), out_shape=(sh...  2.84 us
  transfers between devices with their start and end apart: 4, of which 3 were waited for; matrix products, arithmetic and copies ran while one was open for 0% of the time, Pallas kernels for 7%

profile of v3, /device:TPU:2, one launch (start us, length us, event | category | flops | bytes accessed | tf_op | source)
XLA Modules:
  0.0 55.6 jit_solution(6016055760487976456)
XLA Ops:
  0.6 2.0 %sums.1 = (f32[16,256]{1,0:T(8,128)S(1)}, f32[64,128]{1,0:T(8,128)S(1)}, f32[16,128]{1,0:T(8,128)S(1)}, f32[16,128]{1,0:T(8,128)S(1)}) custom-call(bf16[2048,256]{1,0:T(8,128)(2,1)} %dist_in.3, bf16[32,1024]{1,0:T(8,128)(2,1)} %constant.8.clone.p3_in, f32[13,16]{1,0:T(8,128)} %start_in.1, f32[1,256]{1,0:T(1,128)} %bitcast.3, s32[1,256]{1,0:T(1,128)} %bitcast.5), custom_call_target="tpu_custom_call" | custom-call | tf_op jit(solution)/shard_map/sums/pallas_call | solution.py:672
  2.6 4.2 %collective-permute-start = (f32[64,128]{1,0:T(8,128)S(1)}, f32[64,128]{1,0:T(8,128)S(1)}, u32[]{:S(2)}, u32[]{:S(2)}) collective-permute-start(f32[64,128]{1,0:T(8,128)S(1)} %get-tuple-element.13), channel_id=1, source_target_pairs={{8,24},{9,25},{10,26},{11,27},{12,28},{13,29},{14,30},{15,31},{24,... | collective-permute-start | bytes 98312 | tf_op jit(solution)/shard_map/ppermute | solution.py:699
  6.8 2.6 %collective-permute-start.1 = (f32[16,128]{1,0:T(8,128)S(1)}, f32[16,128]{1,0:T(8,128)S(1)}, u32[]{:S(2)}, u32[]{:S(2)}) collective-permute-start(f32[16,128]{1,0:T(8,128)S(1)} %get-tuple-element.14), channel_id=1, source_target_pairs={{24,8},{25,9},{26,10},{27,11},{28,12},{29,13},{30,14},{31,15},{40,... | collective-permute-start | bytes 24584 | tf_op jit(solution)/shard_map/ppermute | solution.py:700
  9.4 2.9 %collective-permute-done.1.back = f32[16,128]{1,0:T(8,128)S(1)} collective-permute-done((f32[16,128]{1,0:T(8,128)S(1)}, f32[16,128]{1,0:T(8,128)S(1)}, u32[]{:S(2)}, u32[]{:S(2)}) %collective-permute-start.1) | collective-permute-done | bytes 8224 | tf_op jit(solution)/shard_map/ppermute | solution.py:700
  12.3 0.0 collective-permute-done.ahead
  12.3 0.9 %pack.1 = (f32[16,16,384]{2,1,0:T(8,128)}, f32[48,128]{1,0:T(8,128)}) custom-call(f32[16,256]{1,0:T(8,128)S(1)} %get-tuple-element.12.sums, f32[64,128]{1,0:T(8,128)S(1)} %collective-permute-done.ahead, f32[16,128]{1,0:T(8,128)S(1)} %collective-permute-done.1.back, f32[16,128]{1,0:T(8,128)S(1)} %get-tuple-element.15.owned), custom_call_target="tpu_custom_call" | custom-call | tf_op jit(solution)/shard_map/pack/pallas_call | solution.py:701
  13.2 7.0 %all-to-all-start = ((f32[16,16,384]{2,1,0:T(8,128)}), f32[16,16,384]{2,1,0:T(8,128)S(1)}, u32[]{:S(2)}, u32[]{:S(2)}) async-start(f32[16,16,384]{2,1,0:T(8,128)} %get-tuple-element.16), calls=%async_computation | async-start | bytes 786432 | tf_op jit(solution)/shard_map/all_to_all | solution.py:710
  20.2 1.4 %prep.1 = (f32[56,384]{1,0:T(8,128)S(1)}, bf16[1360,256]{1,0:T(8,128)(2,1)S(1)}) custom-call(bf16[1360,256]{1,0:T(8,128)(2,1)} %constant.9.clone.block_in, f32[32,128]{1,0:T(8,128)} %constant.10.clone.pairs_in, bf16[16,16,128]{2,1,0:T(8,128)(2,1)} %constant.11.clone.own_in, f32[13,13]{1,0:T(8,128)} %coupling_in.1, f32[1,13]{1,0:T(1,128)} %bitcast.7, ...), custom_call_target="tpu_custom_call" | custom-call | tf_op jit(solution)/shard_map/prep/pallas_call | solution.py:711
  21.6 9.5 %all-to-all-done.refs_0_ = f32[16,16,384]{2,1,0:T(8,128)S(1)} async-done(((f32[16,16,384]{2,1,0:T(8,128)}), f32[16,16,384]{2,1,0:T(8,128)S(1)}, u32[]{:S(2)}, u32[]{:S(2)}) %all-to-all-start) | async-done | bytes 393248 | tf_op jit(solution)/shard_map/all_to_all | solution.py:710
  31.1 2.8 %fields.1 = (f32[33,16,384]{2,1,0:T(8,128)S(1)}, f32[16,8,128]{2,1,0:T(8,128)}) custom-call(f32[16,16,384]{2,1,0:T(8,128)S(1)} %all-to-all-done.refs_0_, f32[56,384]{1,0:T(8,128)S(1)} %get-tuple-element.17.refs_1_, bf16[1360,256]{1,0:T(8,128)(2,1)S(1)} %get-tuple-element.18.refs_2_._), custom_call_target="tpu_custom_call" | custom-call | tf_op jit(solution)/shard_map/fields/pallas_call | solution.py:727
  34.0 0.0 copy-start
  34.0 0.9 %copy-done = f32[33,16,384]{2,1,0:T(8,128)} copy-done((f32[33,16,384]{2,1,0:T(8,128)}, f32[33,16,384]{2,1,0:T(8,128)S(1)}, u32[]{:S(2)}) %copy-start) | copy-done | bytes 811032
  34.9 9.8 %all-to-all-start.1 = ((f32[16,8,128]{2,1,0:T(8,128)}), f32[16,8,128]{2,1,0:T(8,128)S(1)}, u32[]{:S(2)}, u32[]{:S(2)}) async-start(f32[16,8,128]{2,1,0:T(8,128)} %get-tuple-element.19), calls=%async_computation.1 | async-start | bytes 131072 | tf_op jit(solution)/shard_map/all_to_all | solution.py:754
  44.7 0.0 copy-start.1
  44.7 1.1 %copy-done.1 = f32[33,16,384]{2,1,0:T(8,128)S(1)} copy-done((f32[33,16,384]{2,1,0:T(8,128)S(1)}, f32[33,16,384]{2,1,0:T(8,128)}, u32[]{:S(2)}) %copy-start.1) | copy-done | bytes 811032
  45.8 2.4 %stream.1.refs_3_ = f32[2048,256]{1,0:T(8,128)S(1)} custom-call(f32[33,16,384]{2,1,0:T(8,128)S(1)} %copy-done.1, bf16[1360,256]{1,0:T(8,128)(2,1)S(1)} %get-tuple-element.18.refs_2_._, f32[48,128]{1,0:T(8,128)} %get-tuple-element.21.edges_in, bf16[2048,256]{1,0:T(8,128)(2,1)} %dist_in.3), custom_call_target="tpu_custom_call" | custom-call | tf_op jit(solution)/shard_map/stream/pallas_call | solution.py:740
  48.2 4.2 %all-to-all-done.1.refs_0_ = f32[16,8,128]{2,1,0:T(8,128)S(1)} async-done(((f32[16,8,128]{2,1,0:T(8,128)}), f32[16,8,128]{2,1,0:T(8,128)S(1)}, u32[]{:S(2)}, u32[]{:S(2)}) %all-to-all-start.1) | async-done | bytes 65568 | tf_op jit(solution)/shard_map/all_to_all | solution.py:754
  52.4 0.0 copy-start.2
  52.4 1.1 %copy-done.2 = f32[33,16,384]{2,1,0:T(8,128)S(1)} copy-done((f32[33,16,384]{2,1,0:T(8,128)S(1)}, f32[33,16,384]{2,1,0:T(8,128)}, u32[]{:S(2)}) %copy-start.2) | copy-done | bytes 811032
  53.6 2.0 %update.1 = (bf16[2048,256]{1,0:T(8,128)(2,1)}, f32[13,16]{1,0:T(8,128)}) custom-call(f32[16,8,128]{2,1,0:T(8,128)S(1)} %all-to-all-done.1.refs_0_, f32[33,16,384]{2,1,0:T(8,128)S(1)} %copy-done.2, bf16[1360,256]{1,0:T(8,128)(2,1)S(1)} %get-tuple-element.18.refs_2_._, f32[2048,256]{1,0:T(8,128)S(1)} %stream.1.refs_3_), custom_call_target="tpu_custom_call" | custom-call | tf_op jit(solution)/shard_map/update/pallas_call | solution.py:755
Async XLA Ops:
  2.6 9.7 %collective-permute-start = (f32[64,128]{1,0:T(8,128)S(1)}, f32[64,128]{1,0:T(8,128)S(1)}, u32[]{:S(2)}, u32[]{:S(2)}) collective-permute-start(f32[64,128]{1,0:T(8,128)S(1)} %get-tuple-element.13), channel_id=1, source_target_pairs={{8,24},{9,25},{10,26},{11,27},{12,28},{13,29},{14,30},{15,31},{24,... | collective-permute-start | bytes 98312 | tf_op jit(solution)/shard_map/ppermute | solution.py:699
  6.8 5.5 %collective-permute-start.1 = (f32[16,128]{1,0:T(8,128)S(1)}, f32[16,128]{1,0:T(8,128)S(1)}, u32[]{:S(2)}, u32[]{:S(2)}) collective-permute-start(f32[16,128]{1,0:T(8,128)S(1)} %get-tuple-element.14), channel_id=1, source_target_pairs={{24,8},{25,9},{26,10},{27,11},{28,12},{29,13},{30,14},{31,15},{40,... | collective-permute-start | bytes 24584 | tf_op jit(solution)/shard_map/ppermute | solution.py:700
  13.2 17.9 %all-to-all-start = ((f32[16,16,384]{2,1,0:T(8,128)}), f32[16,16,384]{2,1,0:T(8,128)S(1)}, u32[]{:S(2)}, u32[]{:S(2)}) async-start(f32[16,16,384]{2,1,0:T(8,128)} %get-tuple-element.16), calls=%async_computation | async-start | bytes 786432 | tf_op jit(solution)/shard_map/all_to_all | solution.py:710
  34.0 0.9 %copy-start = (f32[33,16,384]{2,1,0:T(8,128)}, f32[33,16,384]{2,1,0:T(8,128)S(1)}, u32[]{:S(2)}) copy-start(f32[33,16,384]{2,1,0:T(8,128)S(1)} %get-tuple-element.20.fields.refs_1_) | copy-start | bytes 2433028
  34.9 17.6 %all-to-all-start.1 = ((f32[16,8,128]{2,1,0:T(8,128)}), f32[16,8,128]{2,1,0:T(8,128)S(1)}, u32[]{:S(2)}, u32[]{:S(2)}) async-start(f32[16,8,128]{2,1,0:T(8,128)} %get-tuple-element.19), calls=%async_computation.1 | async-start | bytes 131072 | tf_op jit(solution)/shard_map/all_to_all | solution.py:754
  44.7 1.1 %copy-start.1 = (f32[33,16,384]{2,1,0:T(8,128)S(1)}, f32[33,16,384]{2,1,0:T(8,128)}, u32[]{:S(2)}) copy-start(f32[33,16,384]{2,1,0:T(8,128)} %copy-done) | copy-start | bytes 2433028
  52.4 1.1 %copy-start.2 = (f32[33,16,384]{2,1,0:T(8,128)S(1)}, f32[33,16,384]{2,1,0:T(8,128)}, u32[]{:S(2)}) copy-start(f32[33,16,384]{2,1,0:T(8,128)} %copy-done) | copy-start | bytes 2433028

commit v4 on v3

--- a/solution.py
+++ b/solution.py
@@ -245,7 +245,7 @@
 def pack_kernel(sums, ahead, back, owned, out, edges, whole, sems):
     whole[:, 0:CELLS] = sums[...]
     whole[:, CELLS:WIDE] = ahead[0:16, :] + back[...] + owned[...]
-    for copy in copies_of([(whole, out.at[j]) for j in range(PEERS)] + [(ahead.at[16:64, :], edges)], sems):
+    for copy in copies_of([(whole, out.at[j]) for j in range(PEERS)] + [(ahead, edges)], sems):
         copy.wait()
 
 
@@ -292,9 +292,6 @@
     relax1 = jnp.concatenate([known[16:17, 0:CELLS], relax_ends], axis=1)
     r = jnp.broadcast_to(relax1, (16, WIDE))
     fields[N_FIELDS] = r
-    for n in range(3):
-        fields[N_FIELDS + 1 + n] = known[16 * n : 16 * n + 16, :]
-    fields[N_FIELDS + 4, 0:8] = known[48:56, :]
     keep = 1.0 - r
     mask = jnp.broadcast_to(mask, (16, WIDE))
     diffusion = jnp.concatenate([known[0:16, 128:256]] * 3, axis=1)
@@ -413,7 +410,9 @@
     return time_step * jnp.abs((number.astype(f32) + 0.5) * spacing - 4.0)
 
 
-def prep_kernel(
+def stream_kernel(
+    edges_in,
+    dist_in,
     block_in,
     pairs_in,
     own_in,
@@ -421,8 +420,12 @@
     diff_in,
     rate_in,
     flags_in,
+    out,
     table,
     block,
+    dist,
+    edges,
+    ends,
     own6,
     coupling_raw,
     diff_raw,
@@ -431,13 +434,68 @@
     sems,
 ):
     vel = lax.axis_index("vel")
-    moves = [(rate_in, rate), (flags_in, flags), (coupling_in, coupling_raw), (diff_in, diff_raw)]
-    moves += [(own_in.at[vel], own6), (pairs_in, table.at[24:56, 0:128]), (block_in, block)]
+    moves = [(edges_in, edges), (rate_in, rate), (flags_in, flags), (dist_in, dist)]
+    moves += [(coupling_in, coupling_raw), (diff_in, diff_raw), (own_in.at[vel], own6)]
+    moves += [(pairs_in, table.at[24:56, 0:128]), (block_in, block)]
     waits = copies_of(moves, sems)
+    positive = vel >= PEERS // 2
+    towards = jnp.where(positive, 1, -1)
+    ends[...] = jnp.zeros((16, ROWS), f32)
     waits[0].wait()
+    for n in range(3):
+        for k in range(16):
+            row = edges[16 + 16 * n + k : 17 + 16 * n + k, :]
+            ends[n : n + 1, 128 * k : 128 * k + 128] = row
+            ends[8 + n : 9 + n, 128 * k : 128 * k + 128] = row
     waits[1].wait()
-    table[16:24, 0:CELLS] = jnp.broadcast_to(relax_of(rate[...], flags[...]), (8, CELLS))
-    for copy in waits[2:]:
+    waits[2].wait()
+    lane = lanes_of((1, 128))
+    low = jnp.where(positive, 120, 0)
+    near_edge = pltpu.roll(edges[0:16, :], 80, 1)[K : K + 1]
+    near_edge = jnp.where((lane >= low) & (lane < low + 8), near_edge, 0.0)
+    r = jnp.concatenate([relax_of(rate[...], flags[...]), near_edge], axis=1)
+    table[16:24, :] = jnp.broadcast_to(r, (8, WIDE))
+    a = speeds_of((16, WIDE))
+    stay = 1.0 - jnp.broadcast_to(r, (16, WIDE)) - a
+
+    def before(x):
+        return jnp.where(positive, shift_up(x), shift_down(x))
+
+    once = before(stay)
+    two = before(once)
+    t0 = stay * stay * stay
+    t1 = a * (stay * (stay + once) + once * once)
+    t2 = a * a * (stay + once + two)
+    t3 = a * a * a
+    waits[3].wait()
+    back = (lanes_of((CELLS, CELLS)) - rows_of((CELLS, CELLS))) * towards
+    at8 = rows_of((8, CELLS))
+    at8 = jnp.where(positive, -1 - at8, at8 + CELLS)
+    back8 = (lanes_of((8, CELLS)) - at8) * towards
+    for u in range(2):
+        ts = [x[8 * u : 8 * u + 1, 0:CELLS] for x in (t0, t1, t2, t3)]
+
+        def band(distance):
+            value = jnp.zeros(distance.shape, f32)
+            for n, x in enumerate(ts):
+                value = jnp.where(distance == n, jnp.broadcast_to(x, distance.shape), value)
+            return value
+
+        b = band(back)
+        bh = b.astype(bf16)
+        bl = (b - bh.astype(f32)).astype(bf16)
+        b8 = band(back8)
+        b8h = b8.astype(bf16).astype(f32)
+        b8 = jnp.concatenate([b8h, b8 - b8h], axis=0).astype(bf16)
+        rows = pl.ds(u * BLOCK, BLOCK)
+        x = dist[rows, :]
+        value = jnp.dot(x, bh, preferred_element_type=f32)
+        value += jnp.dot(x, bl, preferred_element_type=f32)
+        h = ends[:, rows].astype(bf16)
+        value += lax.dot_general(h, b8, (((0,), (0,)), ((), ())), preferred_element_type=f32)
+        out[rows, :] = value
+
+    for copy in waits[4:]:
         copy.wait()
     table[0:16, 0:128] = jnp.zeros((16, 128), f32)
     table[0:K, 0:K] = coupling_raw[...]
@@ -455,59 +513,6 @@
     table[0:16, 128:256] = jnp.broadcast_to(jnp.sum(chosen, axis=1, keepdims=True), (16, 128))
 
 
-def stream_kernel(fields, _, edges_in, dist_in, out, dist, edges, ends, sems):
-    waits = copies_of([(edges_in, edges), (dist_in, dist)], sems)
-    positive = lax.axis_index("vel") >= PEERS // 2
-    towards = jnp.where(positive, 1, -1)
-    ends[...] = jnp.zeros((16, ROWS), f32)
-    waits[0].wait()
-    for n in range(3):
-        for k in range(16):
-            row = edges[16 * n + k : 16 * n + k + 1, :]
-            ends[n : n + 1, 128 * k : 128 * k + 128] = row
-            ends[8 + n : 9 + n, 128 * k : 128 * k + 128] = row
-    r = fields[N_FIELDS, 0:1, :]
-    a = speeds_of((16, WIDE))
-    stay = 1.0 - jnp.broadcast_to(r, (16, WIDE)) - a
-
-    def before(x):
-        return jnp.where(positive, shift_up(x), shift_down(x))
-
-    once = before(stay)
-    two = before(once)
-    t0 = stay * stay * stay
-    t1 = a * (stay * (stay + once) + once * once)
-    t2 = a * a * (stay + once + two)
-    t3 = a * a * a
-    waits[1].wait()
-    back = (lanes_of((CELLS, CELLS)) - rows_of((CELLS, CELLS))) * towards
-    at8 = rows_of((8, CELLS))
-    at8 = jnp.where(positive, -1 - at8, at8 + CELLS)
-    back8 = (lanes_of((8, CELLS)) - at8) * towards
-    for u in range(2):
-        ts = [x[8 * u : 8 * u + 1, 0:CELLS] for x in (t0, t1, t2, t3)]
-
-        def band(distance):
-            value = jnp.zeros(distance.shape, f32)
-            for n, x in enumerate(ts):
-                value = jnp.where(distance == n, jnp.broadcast_to(x, distance.shape), value)
-            return value
-
-        b = band(back)
-        bh = b.astype(bf16)
-        bl = (b - bh.astype(f32)).astype(bf16)
-        b8 = band(back8)
-        b8h = b8.astype(bf16).astype(f32)
-        b8 = jnp.concatenate([b8h, b8 - b8h], axis=0).astype(bf16)
-        rows = pl.ds(u * BLOCK, BLOCK)
-        x = dist[rows, :]
-        value = jnp.dot(x, bh, preferred_element_type=f32)
-        value += jnp.dot(x, bl, preferred_element_type=f32)
-        h = ends[:, rows].astype(bf16)
-        value += lax.dot_general(h, b8, (((0,), (0,)), ((), ())), preferred_element_type=f32)
-        out[rows, :] = value
-
-
 UPDATE_ROWS = 512
 
 
@@ -515,6 +520,7 @@
     n_space,
     partial,
     fields,
+    table,
     block,
     base,
     out,
@@ -527,19 +533,19 @@
     positive = place >= PEERS // 2
 
     def known(at):
-        return fields[N_FIELDS + 1 + at // 16, at % 16 : at % 16 + 8, 0:128]
+        return table[at : at + 8, 0:128]
 
     total = partial[0]
     for j in range(1, n_space):
         total = total + partial[j]
     total = total * known(48)
-    cpl = fields[N_FIELDS + 1, :, 0:128]
+    cpl = table[0:16, 0:128]
     lane16 = lanes_of((16, 128))
     row16 = rows_of((16, 128))
     size = jnp.sum(jnp.abs(cpl), axis=1, keepdims=True)
     middle = jnp.sum(jnp.where(lane16 == row16, cpl, 0.0), axis=1, keepdims=True)
     real = row16[:, 0:1] < K
-    most = jnp.max(jnp.where(real, size + 4.0 * fields[N_FIELDS + 1, :, 128:129], 0.0), axis=0, keepdims=True)
+    most = jnp.max(jnp.where(real, size + 4.0 * table[0:16, 128:129], 0.0), axis=0, keepdims=True)
     least = jnp.min(jnp.where(real, 2.0 * middle - size, 1e30), axis=0, keepdims=True)
     low_step, high_step = 1.0 / most, 1.0 / least
 
@@ -700,7 +706,7 @@
         back = lax.ppermute(back, ("space", "vel"), upwind)
         packed, edges = pl.pallas_call(
             pack_kernel,
-            out_shape=(stored((PEERS, 16, WIDE)), stored((48, 128))),
+            out_shape=(stored((PEERS, 16, WIDE)), stored((64, 128))),
             in_specs=[vmem()] * 4,
             out_specs=(hbm(),) * 2,
             scratch_shapes=[pltpu.VMEM((16, WIDE), f32), pltpu.SemaphoreType.DMA((PEERS + 1,))],
@@ -708,25 +714,32 @@
             name="pack",
         )(*near(sums, ahead, back, owned))
         got = lax.all_to_all(packed, "vel", split_axis=0, concat_axis=0, tiled=True)
-        known, constants = pl.pallas_call(
-            prep_kernel,
-            out_shape=(shaped((56, WIDE)), shaped(block.shape, bf16)),
-            in_specs=[hbm()] * 7,
-            out_specs=(vmem(),) * 2,
+        base, known, constants = pl.pallas_call(
+            stream_kernel,
+            out_shape=(shaped((ROWS, CELLS)), shaped((56, WIDE)), shaped(block.shape, bf16)),
+            in_specs=[hbm()] * 9,
+            out_specs=(vmem(),) * 3,
             scratch_shapes=[
+                pltpu.VMEM((ROWS, CELLS), bf16),
+                pltpu.VMEM((64, 128), f32),
+                pltpu.VMEM((16, ROWS), f32),
                 pltpu.VMEM((16, 128), bf16),
                 pltpu.VMEM((K, K), f32),
                 pltpu.VMEM((1, K), f32),
                 pltpu.VMEM((1, CELLS), f32),
                 pltpu.VMEM((1, CELLS), jnp.int32),
-                pltpu.SemaphoreType.DMA((7,)),
+                pltpu.SemaphoreType.DMA((9,)),
             ],
-            compiler_params=limit(4),
-            name="prep",
-        )(*far(*(jnp.asarray(x) for x in (block, pairs, own6)), coupling, diffusivity.reshape(1, K), rate, flags))
+            compiler_params=limit(16),
+            name="stream",
+        )(
+            *far(edges, velocity_dist, *(jnp.asarray(x) for x in (block, pairs, own6))),
+            *far(coupling, diffusivity.reshape(1, K), rate, flags),
+        )
+        got, base = lax.optimization_barrier((got, base))
         fields, partial = pl.pallas_call(
             lambda *refs: fields_kernel(n_space, *refs),
-            out_shape=(shaped((N_FIELDS + 5, 16, WIDE)), stored((n_space, 8, 128))),
+            out_shape=(shaped((N_FIELDS + 1, 16, WIDE)), stored((n_space, 8, 128))),
             in_specs=[vmem()] * 3,
             out_specs=(vmem(), hbm()),
             scratch_shapes=[
@@ -737,25 +750,11 @@
             compiler_params=limit(12),
             name="fields",
         )(*near(got, known, constants))
-        base = pl.pallas_call(
-            stream_kernel,
-            out_shape=shaped((ROWS, CELLS)),
-            in_specs=[vmem()] * 2 + [hbm()] * 2,
-            out_specs=vmem(),
-            scratch_shapes=[
-                pltpu.VMEM((ROWS, CELLS), bf16),
-                pltpu.VMEM((48, 128), f32),
-                pltpu.VMEM((16, ROWS), f32),
-                pltpu.SemaphoreType.DMA((2,)),
-            ],
-            compiler_params=limit(16),
-            name="stream",
-        )(*near(fields, constants), *far(edges, velocity_dist))
         partial = lax.all_to_all(partial, "space", split_axis=0, concat_axis=0, tiled=True)
         return pl.pallas_call(
             lambda *refs: update_kernel(n_space, *refs),
             out_shape=(stored((ROWS, CELLS), bf16), stored((K, 16))),
-            in_specs=[vmem()] * 4,
+            in_specs=[vmem()] * 5,
             out_specs=(hbm(), hbm()),
             scratch_shapes=[
                 pltpu.VMEM((ROWS, CELLS), bf16),
@@ -764,7 +763,7 @@
             ],
             compiler_params=limit(12),
             name="update",
-        )(*near(partial, fields, constants, base))
+        )(*near(partial, fields, known, constants, base))
 
     return per_device
 

time: 56 us -> 53.9 us (0.963)
  blocking collectives: 0 us -> 17.6 us
  starting transfers between devices: 23.5 us -> 13.7 us
  waiting for transfers between devices: 16.7 us -> 11.3 us
  local copies, waits for them, and re-layouts: 3.16 us -> 0 us
  Pallas kernels: 11.5 us -> 10.3 us
    all_to_all x0 -> x1, blocking collectives: none -> 17.6 us  [per_device(): lax.all_to_all(partial, 'space', split_axis=0, concat_axis=0, tiled=True)]
    all_to_all x1 -> x0, starting transfers between devices: 9.8 us -> none  [per_device(): lax.all_to_all(partial, 'space', split_axis=0, concat_axis=0, tiled=True)]
    all_to_all x1 -> x0, waiting for transfers between devices: 4.23 us -> none  [per_device(): lax.all_to_all(partial, 'space', split_axis=0, concat_axis=0, tiled=True)]
    unnamed x6 -> x0, local copies, waits for them, and re-layouts: 3.16 us -> none
    all_to_all x1, waiting for transfers between devices: 9.54 us -> 8.31 us  [per_device(): got = lax.all_to_all(packed, 'vel', split_axis=0, concat_axis=0, tiled=True)]
    pallas_call x2 -> x1, Pallas kernels: 3.77 us -> 2.61 us  [per_device(): pl.pallas_call(stream_kernel, out_shape=(shaped((ROWS, CELLS)), shaped((5...]
  transfers between devices with their start and end apart: 4 -> 3, of which waited for: 3 -> 2; matrix products, arithmetic and copies ran while one was open for 0% -> 0% of each run, Pallas kernels for 7% -> 5%
where the time goes in v4:
time: 53.9 us; the launch traced here: 53.5 us
  blocking collectives  17.6 us (33%)
  starting transfers between devices  13.7 us (25%)
  waiting for transfers between devices  11.3 us (21%)
  Pallas kernels  10.3 us (19%)
  between operations  0.69 us (1%)
    all_to_all x1, blocking collectives, per_device(): lax.all_to_all(partial, 'space', split_axis=0, concat_axis=0, tiled=True)  17.6 us
    all_to_all x1, waiting for transfers between devices, per_device(): got = lax.all_to_all(packed, 'vel', split_axis=0, concat_axis=0, tiled=True)  8.31 us
    all_to_all x1, starting transfers between devices, per_device(): got = lax.all_to_all(packed, 'vel', split_axis=0, concat_axis=0, tiled=True)  6.99 us
    ppermute x1, starting transfers between devices, per_device(): ahead = lax.ppermute(ahead, ('space', 'vel'), downwind)  4.15 us
    ppermute x1, waiting for transfers between devices, per_device(): back = lax.ppermute(back, ('space', 'vel'), upwind)  2.95 us
    pallas_call x1, Pallas kernels, per_device(): pl.pallas_call(lambda *refs: fields_kernel(n_space, *refs), out_shape=(sh...  2.84 us
    pallas_call x1, Pallas kernels, per_device(): pl.pallas_call(stream_kernel, out_shape=(shaped((ROWS, CELLS)), shaped((5...  2.61 us
    ppermute x1, starting transfers between devices, per_device(): back = lax.ppermute(back, ('space', 'vel'), upwind)  2.59 us
  transfers between devices with their start and end apart: 3, of which 2 were waited for; matrix products, arithmetic and copies ran while one was open for 0% of the time, Pallas kernels for 5%

profile of v4, /device:TPU:2, one launch (start us, length us, event | category | flops | bytes accessed | tf_op | source)
XLA Modules:
  0.0 53.5 jit_solution(12703855747232055883)
XLA Ops:
  0.6 2.0 %sums.1 = (f32[16,256]{1,0:T(8,128)S(1)}, f32[64,128]{1,0:T(8,128)S(1)}, f32[16,128]{1,0:T(8,128)S(1)}, f32[16,128]{1,0:T(8,128)S(1)}) custom-call(bf16[2048,256]{1,0:T(8,128)(2,1)} %dist_in.3, bf16[32,1024]{1,0:T(8,128)(2,1)} %constant.8.clone.p3_in, f32[13,16]{1,0:T(8,128)} %start_in.1, f32[1,256]{1,0:T(1,128)} %bitcast.3, s32[1,256]{1,0:T(1,128)} %bitcast.5), custom_call_target="tpu_custom_call" | custom-call | tf_op jit(solution)/shard_map/sums/pallas_call | solution.py:678
  2.6 4.2 %collective-permute-start = (f32[64,128]{1,0:T(8,128)S(1)}, f32[64,128]{1,0:T(8,128)S(1)}, u32[]{:S(2)}, u32[]{:S(2)}) collective-permute-start(f32[64,128]{1,0:T(8,128)S(1)} %get-tuple-element.16), channel_id=1, source_target_pairs={{8,24},{9,25},{10,26},{11,27},{12,28},{13,29},{14,30},{15,31},{24,... | collective-permute-start | bytes 98312 | tf_op jit(solution)/shard_map/ppermute | solution.py:705
  6.8 2.6 %collective-permute-start.1 = (f32[16,128]{1,0:T(8,128)S(1)}, f32[16,128]{1,0:T(8,128)S(1)}, u32[]{:S(2)}, u32[]{:S(2)}) collective-permute-start(f32[16,128]{1,0:T(8,128)S(1)} %get-tuple-element.17), channel_id=1, source_target_pairs={{24,8},{25,9},{26,10},{27,11},{28,12},{29,13},{30,14},{31,15},{40,... | collective-permute-start | bytes 24584 | tf_op jit(solution)/shard_map/ppermute | solution.py:706
  9.4 2.9 %collective-permute-done.1.back = f32[16,128]{1,0:T(8,128)S(1)} collective-permute-done((f32[16,128]{1,0:T(8,128)S(1)}, f32[16,128]{1,0:T(8,128)S(1)}, u32[]{:S(2)}, u32[]{:S(2)}) %collective-permute-start.1) | collective-permute-done | bytes 8224 | tf_op jit(solution)/shard_map/ppermute | solution.py:706
  12.3 0.0 collective-permute-done.ahead
  12.3 0.9 %pack.1 = (f32[16,16,384]{2,1,0:T(8,128)}, f32[64,128]{1,0:T(8,128)}) custom-call(f32[16,256]{1,0:T(8,128)S(1)} %get-tuple-element.15.sums, f32[64,128]{1,0:T(8,128)S(1)} %collective-permute-done.ahead, f32[16,128]{1,0:T(8,128)S(1)} %collective-permute-done.1.back, f32[16,128]{1,0:T(8,128)S(1)} %get-tuple-element.18.owned), custom_call_target="tpu_custom_call" | custom-call | tf_op jit(solution)/shard_map/pack/pallas_call | solution.py:707
  13.2 7.0 %all-to-all-start = ((f32[16,16,384]{2,1,0:T(8,128)}), f32[16,16,384]{2,1,0:T(8,128)S(1)}, u32[]{:S(2)}, u32[]{:S(2)}) async-start(f32[16,16,384]{2,1,0:T(8,128)} %get-tuple-element.19), calls=%async_computation | async-start | bytes 786432 | tf_op jit(solution)/shard_map/all_to_all | solution.py:716
  20.2 2.6 %stream.1 = (f32[2048,256]{1,0:T(8,128)S(1)}, f32[56,384]{1,0:T(8,128)S(1)}, bf16[1360,256]{1,0:T(8,128)(2,1)S(1)}) custom-call(f32[64,128]{1,0:T(8,128)} %get-tuple-element.20.edges_in, bf16[2048,256]{1,0:T(8,128)(2,1)} %dist_in.3, bf16[1360,256]{1,0:T(8,128)(2,1)} %constant.9.clone.block_in, f32[32,128]{1,0:T(8,128)} %constant.10.clone.pairs_in, ...), custom_call_target="tpu_custom_call" | custom-call | tf_op jit(solution)/shard_map/stream/pallas_call | solution.py:717
  22.8 8.3 %all-to-all-done.refs_0_ = f32[16,16,384]{2,1,0:T(8,128)S(1)} async-done(((f32[16,16,384]{2,1,0:T(8,128)}), f32[16,16,384]{2,1,0:T(8,128)S(1)}, u32[]{:S(2)}, u32[]{:S(2)}) %all-to-all-start) | async-done | bytes 393248 | tf_op jit(solution)/shard_map/all_to_all | solution.py:716
  31.1 2.8 %fields.1 = (f32[29,16,384]{2,1,0:T(8,128)S(1)}, f32[16,8,128]{2,1,0:T(8,128)}) custom-call(f32[16,16,384]{2,1,0:T(8,128)S(1)} %all-to-all-done.refs_0_, f32[56,384]{1,0:T(8,128)S(1)} %get-tuple-element.23.refs_1_.refs_2_, bf16[1360,256]{1,0:T(8,128)(2,1)S(1)} %get-tuple-element.24.refs_2_.refs_3_), custom_call_target="tpu_custom_call" | custom-call | tf_op jit(solution)/shard_map/fields/pallas_call | solution.py:740
  34.0 17.6 %all_to_all.10.refs_0_ = f32[16,8,128]{2,1,0:T(8,128)S(1)} all-to-all(f32[16,8,128]{2,1,0:T(8,128)} %get-tuple-element.25), channel_id=1, replica_groups=mesh['space'=16,'vel'=16] {'space'}, dimensions={0} | all-to-all | bytes 131072 | tf_op jit(solution)/shard_map/all_to_all | solution.py:753
  51.5 2.0 %update.1 = (bf16[2048,256]{1,0:T(8,128)(2,1)}, f32[13,16]{1,0:T(8,128)}) custom-call(f32[16,8,128]{2,1,0:T(8,128)S(1)} %all_to_all.10.refs_0_, f32[29,16,384]{2,1,0:T(8,128)S(1)} %get-tuple-element.26.refs_1_, f32[56,384]{1,0:T(8,128)S(1)} %get-tuple-element.23.refs_1_.refs_2_, bf16[1360,256]{1,0:T(8,128)(2,1)S(1)} %get-tuple-element.24.refs_2_.refs_3_, ...), custom_call_target="tpu_custom_call" | custom-call | tf_op jit(solution)/shard_map/update/pallas_call | solution.py:754
Async XLA Ops:
  2.6 9.7 %collective-permute-start = (f32[64,128]{1,0:T(8,128)S(1)}, f32[64,128]{1,0:T(8,128)S(1)}, u32[]{:S(2)}, u32[]{:S(2)}) collective-permute-start(f32[64,128]{1,0:T(8,128)S(1)} %get-tuple-element.16), channel_id=1, source_target_pairs={{8,24},{9,25},{10,26},{11,27},{12,28},{13,29},{14,30},{15,31},{24,... | collective-permute-start | bytes 98312 | tf_op jit(solution)/shard_map/ppermute | solution.py:705
  6.8 5.5 %collective-permute-start.1 = (f32[16,128]{1,0:T(8,128)S(1)}, f32[16,128]{1,0:T(8,128)S(1)}, u32[]{:S(2)}, u32[]{:S(2)}) collective-permute-start(f32[16,128]{1,0:T(8,128)S(1)} %get-tuple-element.17), channel_id=1, source_target_pairs={{24,8},{25,9},{26,10},{27,11},{28,12},{29,13},{30,14},{31,15},{40,... | collective-permute-start | bytes 24584 | tf_op jit(solution)/shard_map/ppermute | solution.py:706
  13.2 17.9 %all-to-all-start = ((f32[16,16,384]{2,1,0:T(8,128)}), f32[16,16,384]{2,1,0:T(8,128)S(1)}, u32[]{:S(2)}, u32[]{:S(2)}) async-start(f32[16,16,384]{2,1,0:T(8,128)} %get-tuple-element.19), calls=%async_computation | async-start | bytes 786432 | tf_op jit(solution)/shard_map/all_to_all | solution.py:716

commit v5 on v4

v5 whole, which is shorter than its diff:
```python
import math

import jax
import jax.numpy as jnp
import numpy as np
from jax import lax
from jax.experimental import pallas as pl
from jax.experimental.pallas import tpu as pltpu
from jax.sharding import PartitionSpec as P

NV1 = 32
K = 13
time_step = 0.125
spacing = 8.0 / NV1
CELLS = 256
WIDE = 384
PEERS = 16
ROWS = 2048
BLOCK = 1024
bf16 = jnp.bfloat16
f32 = jnp.float32


def parts_of(x, number):
    rest = np.asarray(x, np.float64)
    out = []
    for _ in range(number):
        piece = rest.astype(np.float32).astype(bf16)
        out.append(piece)
        rest = rest - piece.astype(np.float64)
    return out


def grid_constants():
    v = (np.arange(NV1) + 0.5) * spacing - 4.0
    w = np.exp(-0.5 * v * v) * spacing / math.sqrt(2.0 * math.pi)
    vy, vz = np.repeat(v, NV1), np.tile(v, NV1)
    wyz = np.repeat(w, NV1) * np.tile(w, NV1)
    one = np.ones_like(vy)
    yz = vy * vy + vz * vz
    phi = np.stack([one, vy, vz, vy * vz, vy * vy, vz * vz, vy * yz, vz * yz])
    cmat = np.zeros((NV1, K, 8))
    for i, x in enumerate(v):
        c = cmat[i]
        c[0, 0] = 1.0
        c[1, 0] = x
        c[2, 1] = 1.0
        c[3, 2] = 1.0
        c[4, 0] = (x * x - 3.0) / math.sqrt(6.0)
        c[4, 4] = c[4, 5] = 1.0 / math.sqrt(6.0)
        c[5, 1] = x
        c[6, 2] = x
        c[7, 3] = 1.0
        c[8, 0] = 0.5 * x * x
        c[8, 4] = -0.5
        c[9, 0] = x * x / math.sqrt(12.0)
        c[9, 4] = 1.0 / math.sqrt(12.0)
        c[9, 5] = -2.0 / math.sqrt(12.0)
        c[10, 0] = x * (x * x - 5.0) / math.sqrt(10.0)
        c[10, 4] = c[10, 5] = x / math.sqrt(10.0)
        c[11, 1] = (x * x - 5.0) / math.sqrt(10.0)
        c[11, 6] = 1.0 / math.sqrt(10.0)
        c[12, 2] = (x * x - 5.0) / math.sqrt(10.0)
        c[12, 7] = 1.0 / math.sqrt(10.0)
    a = time_step * np.abs(v)
    plus = v > 0.0
    proj = phi * wyz
    groups = [np.ones(NV1)]
    for power in (1, 2, 3):
        groups += [a**power * plus, a**power * ~plus]
    big = np.zeros((7 * 16, 8 * NV1))
    for g, factor in enumerate(groups):
        for i in range(NV1):
            big[16 * g : 16 * g + K, 8 * i : 8 * i + 8] = factor[i] * w[i] * cmat[i]
    gram2 = proj @ phi.T
    shakhov = np.array([1.0] * 5 + [0.0] * 5 + [1.0 / 3.0] * 3)

    def between(factor):
        out = np.zeros((16, 16))
        for i in range(NV1):
            out[:K, :K] += factor[i] * w[i] * cmat[i] @ gram2 @ cmat[i].T
        return out

    c16 = np.zeros(16)
    c16[:K] = shakhov
    g, gp, gm, g2p, g2m = (between(groups[k]) for k in (0, 1, 2, 3, 4))
    mats = [g, gp, gm, g * c16, gp * c16, gm * c16, g2p, g2m, g2p * c16, g2m * c16]
    block = np.zeros((BLOCK + 336, 256), bf16)
    block[16:176, 128:224] = six_terms(np.concatenate(mats, axis=0))
    block[BLOCK:] = np.concatenate(parts_of(big, 3), axis=0)
    p3 = np.concatenate(parts_of(proj, 3) + [np.zeros((8, BLOCK), bf16)], axis=0)
    ph, pm = parts_of(phi.T, 2)
    block[0:BLOCK, 0:24] = np.concatenate([ph, ph, pm], axis=1)
    own = np.zeros((PEERS, 16, 16))
    for j in range(PEERS):
        for u in range(2):
            own[j, 8 * u : 8 * u + 8, :K] = cmat[2 * j + u].T
    own = np.concatenate([six_terms(own), np.zeros((PEERS, 16, 32), bf16)], axis=2)
    return block, p3, own


def six_terms(x):
    h, m, low = parts_of(x, 3)
    return np.concatenate([h, h, h, m, m, low], axis=-1)


BASES = (1, 3, 9)


def pair_table():
    entries = []
    for stage, size in enumerate(BASES):
        for quantity in range(4):
            for i in range(size):
                for j in range(i, size):
                    entries.append((stage, quantity, i, j))
    return entries


PAIRS = pair_table()


def pair_arrays():
    kind = np.full((8, 128), -1, np.int32)
    left = np.zeros((8, 128), np.int32)
    right = np.zeros((8, 128), np.int32)
    twice = np.zeros((8, 128), np.int32)
    for n, (stage, quantity, i, j) in enumerate(PAIRS):
        at = (n // 128, n % 128)
        kind[at] = 4 * stage + quantity
        left[at], right[at] = i, j
        twice[at] = 1 if i == j else 2
    return np.concatenate([kind, left, right, twice], axis=0).astype(np.float32)


def lanes_of(shape):
    return lax.broadcasted_iota(jnp.int32, shape, len(shape) - 1)


def rows_of(shape):
    return lax.broadcasted_iota(jnp.int32, shape, 0)


def stack6(f):
    h = f.astype(bf16)
    rest = f - h.astype(f32)
    m = rest.astype(bf16)
    low = (rest - m.astype(f32)).astype(bf16)
    return jnp.concatenate([h, m, low, h, m, h], axis=0)


def relax_of(rate, flags):
    return (time_step * rate) * (1.0 + flags.astype(f32))


def shift_up(x):
    return pltpu.roll(x, 1, 1)


def shift_down(x):
    return pltpu.roll(x, x.shape[1] - 1, 1)


def diff_up(x):
    return x - shift_up(x)


def diff_down(x):
    return x - shift_down(x)


def copies_of(pairs, sems):
    made = [pltpu.make_async_copy(x, y, sems.at[n]) for n, (x, y) in enumerate(pairs)]
    for copy in made:
        copy.start()
    return made


def sums_kernel(dist_in, p3_in, start_in, packed, edges, dist, p3, start, whole, padded, sems, sends):
    positive = lax.axis_index("vel") >= PEERS // 2
    halves = [pl.ds(u * BLOCK, BLOCK) for u in range(2)]
    pairs = [(p3_in, p3), (start_in, start)]
    pairs += [(dist_in.at[half, :], dist.at[half, :]) for half in halves]
    waits = copies_of(pairs, sems)
    waits[0].wait()
    waits[1].wait()
    padded[...] = jnp.zeros((16, 128), f32)
    padded[0:K, 0:16] = start[...]
    whole[32:40, :] = padded[0:8, :] + pltpu.roll(padded[8:16, :], 16, 1)
    for u in range(2):
        waits[2 + u].wait()
        y = jnp.dot(p3[...], dist[halves[u], :], preferred_element_type=f32)
        w = y[0:8] + y[8:16] + y[16:24]
        whole[8 * u : 8 * u + 8, :] = w[:, 0:128]
        whole[16 + 8 * u : 24 + 8 * u, :] = w[:, 128:256]
    going = copies_of([(whole, packed.at[j]) for j in range(PEERS)], sends)
    e_lane = lanes_of((16, CELLS))
    e_row = rows_of((16, CELLS))
    cell = jnp.where(positive, CELLS - 1 - e_row, e_row)
    pick = jnp.where((e_lane == cell) & (e_row < 3), 1.0, 0.0).astype(bf16)
    for u in range(2):
        e = lax.dot_general(pick, dist[halves[u], :], (((1,), (1,)), ((), ())), preferred_element_type=f32)
        for n in range(3):
            for k in range(8):
                at = 16 * n + 8 * u + k
                edges[at : at + 1, :] = e[n : n + 1, 128 * k : 128 * k + 128]
    for copy in going:
        copy.wait()


N_FIELDS = 28
RIM = 7
SIDE = 13
STRIPS = 512


def own_shifts():
    lane = lanes_of((16, CELLS))

    def up(x):
        return jnp.where(lane == 0, 0.0, pltpu.roll(x, 1, 1))

    def down(x):
        return jnp.where(lane == CELLS - 1, 0.0, pltpu.roll(x, CELLS - 1, 1))

    return up, down


def advance_three(keep, base, ups, downs, up, down):
    out = []
    for _ in range(3):
        base = keep * base
        if ups:
            base = base - (ups[0] - up(ups[0]))
        if downs:
            base = base - (downs[0] - down(downs[0]))
        ups = [keep * x - (y - up(y)) for x, y in zip(ups[:-1], ups[1:])]
        downs = [keep * x - (y - down(y)) for x, y in zip(downs[:-1], downs[1:])]
        out.append(base)
    return out


def fields_of(s1, s2, s3, start, r, mask, diffusion, block, up, down):
    width = r.shape[1]
    keep = 1.0 - r

    def up_diff(x):
        return x - up(x)

    def down_diff(x):
        return x - down(x)

    def times(first, last, inputs):
        stacked = stack6(jnp.concatenate(inputs, axis=1) if len(inputs) > 1 else inputs[0])
        y = jnp.dot(block[16 * first : 16 * last, 128:224], stacked, preferred_element_type=f32)
        out = []
        for n in range(len(inputs)):
            cut = y[:, n * width : (n + 1) * width]
            out.append([cut[16 * g : 16 * g + 16] for g in range(last - first)])
        return out

    def applied(f, coupled):
        return mask * (coupled + diffusion * (2.0 * f - up(f) - down(f)))

    def streamed(g, gp, gm):
        return keep * g - up_diff(gp) - down_diff(gm)

    def streamed_twice(k1, gp, gm, g2p, g2m):
        return keep * k1 - up_diff(keep * gp - up_diff(g2p)) - down_diff(keep * gm - down_diff(g2m))

    ((gc, gcp, gcm, _, _, g2cp, g2cm),) = times(4, 11, [start])
    relaxed = r * gc
    shares = mask * (s1 + relaxed)
    res = mask * (shares - start)
    k1_start = streamed(relaxed, r * gcp, r * gcm)
    k2_start = streamed_twice(k1_start, r * gcp, r * gcm, r * g2cp, r * g2cm)

    def parts(f, ys):
        out = [applied(f, ys[0])]
        k1 = streamed(ys[1], ys[2], ys[3])
        rg = r * ys[4]
        held = rg - f
        out += [mask * (k1 + held), held]
        if len(ys) > 5:
            out.append(streamed_twice(k1, ys[2], ys[3], ys[7], ys[8]))
            out.append(streamed(rg, r * ys[5], r * ys[6]) + held)
        return out

    y_shares, y_res = times(0, 9, [shares, res])
    rg = r * y_shares[4]
    held_shares = rg - shares
    n_shares = streamed(rg, r * y_shares[5], r * y_shares[6]) + held_shares
    p0 = mask * (s2 + k1_start + held_shares)
    e, p1, _, k2_res, n_res = parts(res, y_res)

    y_e, y_p0, y_p1 = times(0, 9, [e, p0, p1])
    ee, p2, _, k2_e, n_e = parts(e, y_e)
    ap0, q3, held_p0 = parts(p0, y_p0[:5])
    ap1, q4, held_p1 = parts(p1, y_p1[:5])
    q0 = mask * (s3 + k2_start + n_shares + held_p0)
    q1 = mask * (k2_res + n_res + held_p1)

    y_p2, y_ap0, y_ap1, y_q0, y_q1, y_q3, y_q4 = times(0, 5, [p2, ap0, ap1, q0, q1, q3, q4])
    ap2, q5, held_p2 = parts(p2, y_p2)
    aap0, q6, _ = parts(ap0, y_ap0)
    aap1, q7, _ = parts(ap1, y_ap1)
    q2 = mask * (k2_e + n_e + held_p2)
    aq0, aq1, aq3, aq4 = (applied(f, y[0]) for f, y in ((q0, y_q0), (q1, y_q1), (q3, y_q3), (q4, y_q4)))

    (y_ap2,) = times(0, 5, [ap2])
    aap2, q8, _ = parts(ap2, y_ap2)
    first = [q2, q5, q6, q7, aq0, aq1, aq3, aq4]
    aq2, aq5, aq6, aq7, aaq0, aaq1, aaq3, aaq4 = (applied(f, y[0]) for f, y in zip(first, times(0, 1, first)))
    second = [q8, aq2, aq5, aq6, aq7]
    aq8, aaq2, aaq5, aaq6, aaq7 = (applied(f, y[0]) for f, y in zip(second, times(0, 1, second)))
    ((y_aq8,),) = times(0, 1, [aq8])
    aaq8 = applied(aq8, y_aq8)

    q = [q0, q1, q2, q3, q4, q5, q6, q7, q8]
    aq = [aq0, aq1, aq2, aq3, aq4, aq5, aq6, aq7, aq8]
    aaq = [aaq0, aaq1, aaq2, aaq3, aaq4, aaq5, aaq6, aaq7, aaq8]
    fields = [start, shares, res, e, p0, p1, p2, ap0, ap1, ap2] + q + aq
    plain = [[res], [p0, p1, p2], q]
    once = [[e], [ap0, ap1, ap2], aq]
    again = [[ee], [aap0, aap1, aap2], aaq]
    return fields, plain, once, again


def inner_products(plain, once, again, counted, table):
    kept_plain = [[counted * x for x in xs] for xs in plain]
    kept_once = [[counted * x for x in xs] for xs in once]
    tiles = counted.shape[1] // 128
    table[208:256, :] = jnp.zeros((48, 128), f32)
    for n, (stage, quantity, i, j) in enumerate(PAIRS):
        a, b = ((kept_plain, plain), (kept_plain, once), (kept_once, once), (kept_once, again))[quantity]
        product = a[stage][i] * b[stage][j]
        folded = product[:, 0:128]
        for t in range(1, tiles):
            folded = folded + product[:, 128 * t : 128 * t + 128]
        table[n : n + 1, :] = jnp.sum(folded[0:8] + folded[8:16], axis=0, keepdims=True)
    ones = jnp.ones((8, 128), f32)
    return [
        lax.dot_general(
            ones,
            table[128 * n : 128 * n + 128, :],
            (((1,), (1,)), ((), ())),
            precision=lax.Precision.HIGHEST,
            preferred_element_type=f32,
        )
        for n in range(2)
    ]


def fields_kernel(n_space, got, known, block, fields, sent, table, line, sems):
    slab = lax.axis_index("space")
    wide = (16, CELLS)
    w = jnp.concatenate([got[:, 16 * t : 16 * t + 16, :].reshape(PEERS * 16, 128) for t in range(2)], axis=1)
    wh = w.astype(bf16)
    w_rest = w - wh.astype(f32)
    wm = w_rest.astype(bf16)
    wl = (w_rest - wm.astype(f32)).astype(bf16)
    y = jnp.dot(block[BLOCK : BLOCK + 336, :], wh, preferred_element_type=f32)
    z = jnp.dot(block[BLOCK : BLOCK + 224, :], wm, preferred_element_type=f32)
    t = jnp.dot(block[BLOCK : BLOCK + 112, :], wl, preferred_element_type=f32)
    mu = ((y[224:336] + z[112:224]) + (y[112:224] + z[0:112])) + t + y[0:112]
    mu = [mu[16 * g : 16 * g + 16] for g in range(7)]

    lane8 = lanes_of((8, 128))
    parts = [[jnp.zeros((8, 128), f32)] * 2 for _ in range(2)]
    for j in range(PEERS):
        tile = got[j, 32:40, :]
        here = lane8 // 16 == j % 8
        for half in range(2):
            amount = (16 * j - 16 * half) % 128
            moved = pltpu.roll(tile, amount, 1) if amount else tile
            parts[half][j // 8] = jnp.where(here, moved, parts[half][j // 8])
    start = jnp.concatenate([jnp.concatenate(x, axis=1) for x in parts], axis=0)

    r = jnp.broadcast_to(known[16:17, 0:CELLS], wide)
    diffusion = jnp.concatenate([known[0:16, 128:256]] * 2, axis=1)
    up, down = own_shifts()
    s1, s2, s3 = advance_three(1.0 - r, mu[0], [mu[1], mu[3], mu[5]], [mu[2], mu[4], mu[6]], up, down)
    out, plain, once, again = fields_of(s1, s2, s3, start, r, 1.0, diffusion, block, up, down)
    for n, f in enumerate(out):
        fields[n] = f
    lane = lanes_of(wide)
    low = jnp.where(slab > 0, RIM, 0)
    high = jnp.where(slab < n_space - 1, CELLS - RIM, CELLS)
    counted = jnp.where((lane >= low) & (lane < high), 1.0, 0.0)
    tops = inner_products(plain, once, again, counted, table)

    lane1 = lanes_of((16, 128))
    row1 = rows_of((16, 128))
    start_relax = jnp.where(rows_of(wide) == K, r, start)
    tile = jnp.zeros((16, 128), f32)
    for n, f in enumerate([s1, s2, s3, start_relax]):
        at = lane1 - 32 * n
        begin = pltpu.roll(f[:, 0:128], 32 * n, 1) if n else f[:, 0:128]
        tile = jnp.where((at >= 0) & (at < SIDE), begin, tile)
        end = pltpu.roll(f[:, 128:256], (32 * n + 16 + SIDE) % 128, 1)
        tile = jnp.where((at >= 16) & (at < 16 + SIDE), end, tile)
        if n < 3:
            begin = pltpu.roll(mu[2 + 2 * n][:, 0:128], 32 * n + SIDE, 1)
            tile = jnp.where((at >= SIDE) & (at < 16), begin, tile)
            end = pltpu.roll(mu[1 + 2 * n][:, 128:256], (32 * n + 32) % 128, 1)
            tile = jnp.where((at >= 16 + SIDE) & (at < 32), end, tile)
    row_a = jnp.broadcast_to(tops[0][0:1], (16, 128))
    row_b = jnp.broadcast_to(tops[1][0:1], (16, 128))
    line[...] = jnp.where(row1 == 14, row_a, jnp.where(row1 == 15, row_b, tile))
    for copy in copies_of([(line, sent.at[j]) for j in range(n_space)], sems):
        copy.wait()


def speeds_of(shape):
    number = 2 * lax.axis_index("vel") + jnp.where(rows_of(shape) >= 8, 1, 0)
    return time_step * jnp.abs((number.astype(f32) + 0.5) * spacing - 4.0)


def bands_of(r, positive):
    a = speeds_of(r.shape)
    stay = 1.0 - r - a

    def before(x):
        return jnp.where(positive, shift_up(x), shift_down(x))

    once = before(stay)
    two = before(once)
    t0 = stay * stay * stay
    t1 = a * (stay * (stay + once) + once * once)
    t2 = a * a * (stay + once + two)
    return t0, t1, t2, a * a * a


def banded(weights, u, distance):
    value = jnp.zeros(distance.shape, f32)
    for n, x in enumerate(weights):
        row = jnp.broadcast_to(x[8 * u : 8 * u + 1, 0:CELLS], distance.shape)
        value = jnp.where(distance == n, row, value)
    return value


def stream_kernel(
    dist_in,
    block_in,
    pairs_in,
    own_in,
    coupling_in,
    diff_in,
    rate_in,
    flags_in,
    out,
    table,
    block,
    dist,
    own6,
    coupling_raw,
    diff_raw,
    rate,
    flags,
    sems,
):
    vel = lax.axis_index("vel")
    positive = vel >= PEERS // 2
    moves = [(rate_in, rate), (flags_in, flags), (dist_in, dist)]
    moves += [(coupling_in, coupling_raw), (diff_in, diff_raw), (own_in.at[vel], own6)]
    moves += [(pairs_in, table.at[24:56, 0:128]), (block_in, block)]
    waits = copies_of(moves, sems)
    waits[0].wait()
    waits[1].wait()
    relax = relax_of(rate[...], flags[...])
    table[16:24, 0:CELLS] = jnp.broadcast_to(relax, (8, CELLS))
    weights = bands_of(jnp.broadcast_to(relax, (16, CELLS)), positive)
    towards = jnp.where(positive, 1, -1)
    distance = (lanes_of((CELLS, CELLS)) - rows_of((CELLS, CELLS))) * towards
    waits[2].wait()
    for u in range(2):
        b = banded(weights, u, distance)
        bh = b.astype(bf16)
        bl = (b - bh.astype(f32)).astype(bf16)
        rows = pl.ds(u * BLOCK, BLOCK)
        x = dist[rows, :]
        value = jnp.dot(x, bh, preferred_element_type=f32)
        value += jnp.dot(x, bl, preferred_element_type=f32)
        out[rows, :] = value

    for copy in waits[3:]:
        copy.wait()
    table[0:16, 0:128] = jnp.zeros((16, 128), f32)
    table[0:K, 0:K] = coupling_raw[...]
    c = table[0:16, 0:128]
    ch = c.astype(bf16).astype(f32)
    cm = (c - ch).astype(bf16).astype(f32)
    pieces = [ch, ch, ch, cm, cm, c - ch - cm]
    six = pieces[0]
    for n in range(1, 6):
        six = six + pltpu.roll(pieces[n], 16 * n, 1)
    block[0:16, 128:256] = six.astype(bf16)
    block[176:192, 128:256] = own6[...]
    shape = (16, K)
    chosen = jnp.where(lanes_of(shape) == rows_of(shape), jnp.broadcast_to(diff_raw[...], shape), 0.0)
    table[0:16, 128:256] = jnp.broadcast_to(jnp.sum(chosen, axis=1, keepdims=True), (16, 128))


UPDATE_ROWS = 512


def strips_of(n_space, sent):
    quarter = lanes_of((16, 128)) // 32
    raw = []
    for n in range(4):
        tiles = []
        for t in range(4):
            tile = jnp.zeros((16, 128), f32)
            for k in range(4):
                j = 4 * t + k
                if j < n_space:
                    amount = 32 * (k - n) % 128
                    moved = pltpu.roll(sent[j], amount, 1) if amount else sent[j]
                    tile = jnp.where(quarter == k, moved, tile)
            tiles.append(tile)
        raw.append(jnp.concatenate(tiles, axis=1))
    shape = (16, STRIPS)
    lane = lanes_of(shape)
    row = rows_of(shape)
    at = (lane + 16) % 32
    valid = (lane >= 16) & (lane < 16 + 32 * (n_space - 1)) & (at < 2 * SIDE)
    mask = jnp.where(valid, 1.0, 0.0)
    moments = jnp.where(row < K, mask, 0.0)
    closer = [pltpu.roll(x, STRIPS - 3, 1) for x in raw]
    arrays = [jnp.where(at < SIDE, x, y) for x, y in zip(raw, closer)]
    r = mask * jnp.broadcast_to(arrays[3][K : K + 1], shape)
    s1, s2, s3, start = (moments * x for x in arrays)
    ups = [jnp.where((at >= SIDE - 3) & (at < SIDE), moments * x, 0.0) for x in closer[:3]]
    downs = [pltpu.roll(x, STRIPS - 16, 1) for x in raw[:3]]
    downs = [jnp.where((at >= SIDE) & (at < SIDE + 3), moments * x, 0.0) for x in downs]
    zero = jnp.zeros(shape, f32)
    over_up = advance_three(1.0 - r, zero, ups, [], shift_up, shift_down)
    over_down = advance_three(1.0 - r, zero, [], downs, shift_up, shift_down)
    s = [x + jnp.where(at < SIDE, y, z) for x, y, z in zip((s1, s2, s3), over_down, over_up)]
    s = [mask * x for x in s]
    counted = jnp.where((at >= SIDE - RIM) & (at < SIDE + RIM), mask, 0.0)
    return s, start, r, mask, counted


def update_kernel(
    n_space,
    sent,
    fields,
    table,
    block,
    base,
    edges_in,
    out,
    macro,
    done,
    macro_part,
    products,
    edges,
    ends,
    sems,
):
    place = lax.axis_index("vel")
    slab = lax.axis_index("space")
    positive = place >= PEERS // 2
    (edge_copy,) = copies_of([(edges_in, edges)], sems.at[pl.ds(ROWS // UPDATE_ROWS + 1, 1)])

    def known(at):
        return table[at : at + 8, 0:128]

    (s1, s2, s3), strip_start, strip_r, strip_mask, counted = strips_of(n_space, sent)
    diffusion = jnp.concatenate([table[0:16, 128:256]] * 4, axis=1)
    strip_fields, plain, once, again = fields_of(
        s1, s2, s3, strip_start, strip_r, strip_mask, diffusion, block, shift_up, shift_down
    )
    tops = inner_products(plain, once, again, counted, products)
    gathered = sent[0, 8:16, :]
    for j in range(1, n_space):
        gathered = gathered + sent[j, 8:16, :]
    row8 = rows_of((8, 128))
    line_a = gathered[6:7] + tops[0][0:1]
    line_b = gathered[7:8] + tops[1][0:1]
    total = jnp.where(row8 == 0, line_a, jnp.where(row8 == 1, line_b, 0.0))
    total = total * known(48)
    cpl = table[0:16, 0:128]
    lane16 = lanes_of((16, 128))
    row16 = rows_of((16, 128))
    size = jnp.sum(jnp.abs(cpl), axis=1, keepdims=True)
    middle = jnp.sum(jnp.where(lane16 == row16, cpl, 0.0), axis=1, keepdims=True)
    real = row16[:, 0:1] < K
    most = jnp.max(jnp.where(real, size + 4.0 * table[0:16, 128:129], 0.0), axis=0, keepdims=True)
    least = jnp.min(jnp.where(real, 2.0 * middle - size, 1e30), axis=0, keepdims=True)
    low_step, high_step = 1.0 / most, 1.0 / least

    def summed(weighted, which):
        picked = jnp.where(known(24) == which, weighted, 0.0)
        return jnp.sum(jnp.sum(picked, axis=0, keepdims=True), axis=1, keepdims=True)

    def clipped(x):
        return jnp.minimum(jnp.maximum(x, low_step), high_step)

    def weights_of(stage, weighted):
        rr, ra, aa, aaa = (summed(weighted, 4 * stage + n) for n in range(4))
        s1 = clipped(rr / ra)
        rr2 = rr - 2.0 * s1 * ra + s1 * s1 * aa
        ra2 = ra - 2.0 * s1 * aa + s1 * s1 * aaa
        s2 = clipped(rr2 / ra2)
        return s1 + s2, -s1 * s2

    li, ri = (known(n).astype(jnp.int32) for n in (32, 40))

    def choose(index, zero, one, two):
        return jnp.where(index == 0, zero, jnp.where(index == 1, one, two))

    a1, b1 = weights_of(0, total)
    a2, b2 = weights_of(1, total * choose(li, 1.0, a1, b1) * choose(ri, 1.0, a1, b1))

    def both(index):
        outer = (index >= 3).astype(jnp.int32) + (index >= 6).astype(jnp.int32)
        return choose(outer, 1.0, a2, b2) * choose(index - 3 * outer, 1.0, a1, b1)

    a3, b3 = weights_of(2, total * both(li) * both(ri))

    def last_fields(at, r):
        start, shares, res, e = (at(n) for n in range(4))
        corr1 = a1 * res + b1 * e
        cur1 = shares + corr1
        res2 = at(4) + a1 * at(5) + b1 * at(6)
        e2 = at(7) + a1 * at(8) + b1 * at(9)
        corr2 = a2 * res2 + b2 * e2
        cur2 = res2 + cur1 + corr2

        def third(first):
            rows = [at(first + 3 * n) + a1 * at(first + 3 * n + 1) + b1 * at(first + 3 * n + 2) for n in range(3)]
            return rows[0] + a2 * rows[1] + b2 * rows[2]

        res3, e3 = third(10), third(19)
        corr3 = a3 * res3 + b3 * e3
        row = rows_of(r.shape)
        scaled = r * jnp.where(row < 5, 1.0, jnp.where(row < 10, 0.0, 1.0 / 3.0))
        f1 = scaled * start + corr1
        f2 = scaled * cur1 + corr2
        f3 = scaled * cur2 + corr3
        return f1, f2, f3, res3 + cur2 + corr3, r

    own = last_fields(lambda n: fields[n], jnp.broadcast_to(table[16:17, 0:CELLS], (16, CELLS)))
    strips = last_fields(lambda n: strip_fields[n], strip_r)
    lane1 = lanes_of((16, 128))
    has_left, has_right = jnp.where(slab > 0, 1, 0), jnp.where(slab < n_space - 1, 1, 0)
    near_left = (lane1 < RIM * has_left)
    near_right = (lane1 >= 128 - RIM * has_right)
    far_left = (lane1 >= 128 - 2 * has_left)
    far_right = (lane1 < 2 * has_right)
    wide = []
    for x, y in zip(own, strips):
        y = pltpu.roll(y, lax.rem(STRIPS + 16 - 32 * slab, STRIPS), 1)[:, 0:128]
        from_left = pltpu.roll(y, 128 - SIDE, 1)
        from_right = pltpu.roll(y, 96 - SIDE, 1)
        tiles = [
            jnp.where(near_left, from_left, x[:, 0:128]),
            jnp.where(near_right, from_right, x[:, 128:256]),
            jnp.where(far_left, from_left, jnp.where(far_right, from_right, 0.0)),
        ]
        wide.append(jnp.concatenate(tiles, axis=1))
    f1, f2, f3, cur3, r = wide
    mine = pltpu.roll(cur3[:, 0:CELLS], lax.rem(CELLS - 16 * place, CELLS), 1)
    macro_part[...] = mine[0:K, 0:16]
    macro_copy = pltpu.make_async_copy(macro_part, macro, sems.at[ROWS // UPDATE_ROWS])
    macro_copy.start()
    y = jnp.dot(
        block[176:192, 128:224], stack6(jnp.concatenate([f1, f2, f3], axis=1)), preferred_element_type=f32
    )
    y1, y2, y3 = (y[:, n * WIDE : (n + 1) * WIDE] for n in range(3))
    a = speeds_of((16, WIDE))
    stay = 1.0 - r - a

    def moved(x):
        return stay * x + a * jnp.where(positive, shift_up(x), shift_down(x))

    h = (moved(moved(y1) + y2) + y3)[:, 0:CELLS]
    hh = h.astype(bf16).astype(f32)
    hm = (h - hh).astype(bf16).astype(f32)

    weights = bands_of(r, positive)
    towards = jnp.where(positive, 1, -1)
    at8 = rows_of((8, CELLS))
    at8 = jnp.where(positive, -1 - at8, at8 + CELLS)
    distance = (lanes_of((8, CELLS)) - at8) * towards
    ends[...] = jnp.zeros((16, ROWS), f32)
    edge_copy.wait()
    for n in range(3):
        for k in range(16):
            row = edges[16 * n + k : 16 * n + k + 1, :]
            ends[n : n + 1, 128 * k : 128 * k + 128] = row
            ends[8 + n : 9 + n, 128 * k : 128 * k + 128] = row

    sends = [macro_copy]
    for u in range(2):
        hu, mu = hh[8 * u : 8 * u + 8], hm[8 * u : 8 * u + 8]
        mixed = jnp.concatenate([hu, mu, hu, jnp.zeros((104, CELLS), f32)], axis=0).astype(bf16)
        b = banded(weights, u, distance)
        bh = b.astype(bf16).astype(f32)
        b = jnp.concatenate([bh, b - bh], axis=0).astype(bf16)
        for n in range(BLOCK // UPDATE_ROWS):
            part = u * (BLOCK // UPDATE_ROWS) + n
            rows = pl.ds(part * UPDATE_ROWS, UPDATE_ROWS)
            value = jnp.dot(block[pl.ds(n * UPDATE_ROWS, UPDATE_ROWS), 0:128], mixed, preferred_element_type=f32)
            value += lax.dot_general(
                ends[:, rows].astype(bf16), b, (((0,), (0,)), ((), ())), preferred_element_type=f32
            )
            done[rows, :] = (base[rows, :] + value).astype(bf16)
            copy = pltpu.make_async_copy(done.at[rows, :], out.at[rows, :], sems.at[part])
            copy.start()
            sends.append(copy)
    for copy in sends:
        copy.wait()


def vmem():
    return pl.BlockSpec(memory_space=pltpu.VMEM)


def hbm():
    return pl.BlockSpec(memory_space=pltpu.HBM)


def shaped(shape, dtype=f32):
    return pltpu.VMEM(shape, dtype)


def stored(shape, dtype=f32):
    return pltpu.HBM(shape, dtype)


def placed_at(space, arrays):
    return [pltpu.with_memory_space_constraint(x, space) for x in arrays]


def near(*arrays):
    return placed_at(pltpu.VMEM, arrays)


def far(*arrays):
    return placed_at(pltpu.HBM, arrays)


def limit(mib):
    return pltpu.CompilerParams(vmem_limit_bytes=mib * 2**20)


def make_per_device(n_space):
    block, p3, own6 = grid_constants()
    pairs = pair_arrays()

    def per_device(velocity_dist, macro_state, collision_rate, wall_flags, diffusivity, coupling):
        rate = collision_rate.reshape(1, CELLS)
        flags = wall_flags.reshape(1, CELLS)
        packed, edges = pl.pallas_call(
            sums_kernel,
            out_shape=(stored((PEERS, 40, 128)), stored((48, 128))),
            in_specs=[hbm()] * 3,
            out_specs=(hbm(), vmem()),
            scratch_shapes=[
                pltpu.VMEM((ROWS, CELLS), bf16),
                pltpu.VMEM((32, BLOCK), bf16),
                pltpu.VMEM((K, 16), f32),
                pltpu.VMEM((40, 128), f32),
                pltpu.VMEM((16, 128), f32),
                pltpu.SemaphoreType.DMA((4,)),
                pltpu.SemaphoreType.DMA((PEERS,)),
            ],
            compiler_params=limit(8),
            name="sums",
        )(*far(velocity_dist, jnp.asarray(p3), macro_state))
        got = lax.all_to_all(packed, "vel", split_axis=0, concat_axis=0, tiled=True)
        rising = [(i, i + 1) for i in range(n_space - 1)]
        half = PEERS // 2
        downwind = [(i * PEERS + n, j * PEERS + n) for i, j in rising for n in range(half, PEERS)]
        downwind += [(j * PEERS + n, i * PEERS + n) for i, j in rising for n in range(half)]
        edges = lax.ppermute(edges, ("space", "vel"), downwind)
        base, known, constants = pl.pallas_call(
            stream_kernel,
            out_shape=(shaped((ROWS, CELLS)), shaped((56, WIDE)), shaped(block.shape, bf16)),
            in_specs=[hbm()] * 8,
            out_specs=(vmem(),) * 3,
            scratch_shapes=[
                pltpu.VMEM((ROWS, CELLS), bf16),
                pltpu.VMEM((16, 128), bf16),
                pltpu.VMEM((K, K), f32),
                pltpu.VMEM((1, K), f32),
                pltpu.VMEM((1, CELLS), f32),
                pltpu.VMEM((1, CELLS), jnp.int32),
                pltpu.SemaphoreType.DMA((8,)),
            ],
            compiler_params=limit(16),
            cost_estimate=pl.CostEstimate(flops=600_000_000, bytes_accessed=4_000_000, transcendentals=0),
            name="stream",
        )(
            *far(velocity_dist, *(jnp.asarray(x) for x in (block, pairs, own6))),
            *far(coupling, diffusivity.reshape(1, K), rate, flags),
        )
        got, base, edges = lax.optimization_barrier((got, base, edges))
        fields, sent = pl.pallas_call(
            lambda *refs: fields_kernel(n_space, *refs),
            out_shape=(shaped((N_FIELDS, 16, CELLS)), stored((n_space, 16, 128))),
            in_specs=[vmem()] * 3,
            out_specs=(vmem(), hbm()),
            scratch_shapes=[
                pltpu.VMEM((256, 128), f32),
                pltpu.VMEM((16, 128), f32),
                pltpu.SemaphoreType.DMA((n_space,)),
            ],
            compiler_params=limit(12),
            name="fields",
        )(*near(got, known, constants))
        sent = lax.all_to_all(sent, "space", split_axis=0, concat_axis=0, tiled=True)
        return pl.pallas_call(
            lambda *refs: update_kernel(n_space, *refs),
            out_shape=(stored((ROWS, CELLS), bf16), stored((K, 16))),
            in_specs=[vmem()] * 5 + [hbm()],
            out_specs=(hbm(), hbm()),
            scratch_shapes=[
                pltpu.VMEM((ROWS, CELLS), bf16),
                pltpu.VMEM((K, 16), f32),
                pltpu.VMEM((256, 128), f32),
                pltpu.VMEM((48, 128), f32),
                pltpu.VMEM((16, ROWS), f32),
                pltpu.SemaphoreType.DMA((ROWS // UPDATE_ROWS + 2,)),
            ],
            compiler_params=limit(12),
            name="update",
        )(*near(sent, fields, known, constants, base), *far(edges))

    return per_device


def solution(mesh):
    placed = (P("vel", "space"), P(None, ("space", "vel")), P("space"), P("space"), P(), P())
    return jax.shard_map(
        make_per_device(mesh.shape["space"]),
        mesh=mesh,
        in_specs=placed,
        out_specs=(P("vel", "space"), P(None, ("space", "vel"))),
        check_vma=False,
    )
```

time: 53.9 us -> 47.8 us (0.89)
  waiting for transfers between devices: 11.3 us -> 4.58 us
  starting transfers between devices: 13.7 us -> 9.49 us
  Pallas kernels: 10.3 us -> 14.1 us
  blocking collectives: 17.6 us -> 18.6 us
    all_to_all x1, waiting for transfers between devices: 8.31 us -> 3.39 us  [per_device(): got = lax.all_to_all(packed, 'vel', split_axis=0, concat_axis=0, tiled=True)]
    pallas_call x1, Pallas kernels: 1.99 us -> 5.89 us  [per_device(): pl.pallas_call(lambda *refs: update_kernel(n_space, *refs), out_shape=(st...]
    ppermute x2 -> x1, starting transfers between devices: 6.74 us -> 3.34 us  [per_device(): edges = lax.ppermute(edges, ('space', 'vel'), downwind)]
    ppermute x2 -> x1, waiting for transfers between devices: 2.95 us -> 1.2 us  [per_device(): edges = lax.ppermute(edges, ('space', 'vel'), downwind)]
    all_to_all x1, blocking collectives: 17.6 us -> 18.6 us  [per_device(): lax.all_to_all(sent, 'space', split_axis=0, concat_axis=0, tiled=True)]
    all_to_all x1, starting transfers between devices: 6.99 us -> 6.15 us  [per_device(): got = lax.all_to_all(packed, 'vel', split_axis=0, concat_axis=0, tiled=True)]
    pallas_call x2 -> x1, Pallas kernels: 2.85 us -> 3.1 us  [per_device(): pl.pallas_call(sums_kernel, out_shape=(stored((PEERS, 40, 128)), stored((...]
  transfers between devices with their start and end apart: 3 -> 2, of which waited for: 2 -> 2; matrix products, arithmetic and copies ran while one was open for 0% -> 0% of each run, Pallas kernels for 5% -> 5%
where the time goes in v5:
time: 47.8 us; the launch traced here: 47.4 us
  blocking collectives  18.6 us (39%)
  Pallas kernels  14.1 us (29%)
  starting transfers between devices  9.49 us (20%)
  waiting for transfers between devices  4.58 us (10%)
  between operations  0.67 us (1%)
    all_to_all x1, blocking collectives, per_device(): lax.all_to_all(sent, 'space', split_axis=0, concat_axis=0, tiled=True)  18.6 us
    all_to_all x1, starting transfers between devices, per_device(): got = lax.all_to_all(packed, 'vel', split_axis=0, concat_axis=0, tiled=True)  6.15 us
    pallas_call x1, Pallas kernels, per_device(): pl.pallas_call(lambda *refs: update_kernel(n_space, *refs), out_shape=(st...  5.89 us
    all_to_all x1, waiting for transfers between devices, per_device(): got = lax.all_to_all(packed, 'vel', split_axis=0, concat_axis=0, tiled=True)  3.39 us
    ppermute x1, starting transfers between devices, per_device(): edges = lax.ppermute(edges, ('space', 'vel'), downwind)  3.34 us
    pallas_call x1, Pallas kernels, per_device(): pl.pallas_call(sums_kernel, out_shape=(stored((PEERS, 40, 128)), stored((...  3.1 us
    pallas_call x1, Pallas kernels, per_device(): pl.pallas_call(lambda *refs: fields_kernel(n_space, *refs), out_shape=(sh...  2.79 us
    pallas_call x1, Pallas kernels, per_device(): pl.pallas_call(stream_kernel, out_shape=(shaped((ROWS, CELLS)), shaped((5...  2.28 us
  transfers between devices with their start and end apart: 2, of which 2 were waited for; matrix products, arithmetic and copies ran while one was open for 0% of the time, Pallas kernels for 5%

profile of v5, /device:TPU:2, one launch (start us, length us, event | category | flops | bytes accessed | tf_op | source)
XLA Modules:
  0.0 47.4 jit_solution(17167576722034748041)
XLA Ops:
  0.6 3.1 %sums.1 = (f32[16,40,128]{2,1,0:T(8,128)}, f32[48,128]{1,0:T(8,128)}) custom-call(bf16[2048,256]{1,0:T(8,128)(2,1)} %dist_in.3, bf16[32,1024]{1,0:T(8,128)(2,1)} %constant.8.clone.p3_in, f32[13,16]{1,0:T(8,128)} %start_in.1), custom_call_target="tpu_custom_call" | custom-call | tf_op jit(solution)/shard_map/sums/pallas_call | solution.py:757
  3.7 6.1 %all-to-all-start = ((f32[16,40,128]{2,1,0:T(8,128)}), f32[16,40,128]{2,1,0:T(8,128)S(1)}, u32[]{:S(2)}, u32[]{:S(2)}) async-start(f32[16,40,128]{2,1,0:T(8,128)} %get-tuple-element.12), calls=%async_computation | async-start | bytes 655360 | tf_op jit(solution)/shard_map/all_to_all | solution.py:774
  9.9 3.3 %collective-permute-start = (f32[48,128]{1,0:T(8,128)}, f32[48,128]{1,0:T(8,128)S(1)}, u32[]{:S(2)}, u32[]{:S(2)}) collective-permute-start(f32[48,128]{1,0:T(8,128)} %get-tuple-element.14), channel_id=1, source_target_pairs={{8,24},{9,25},{10,26},{11,27},{12,28},{13,29},{14,30},{15,31},{24,... | collective-permute-start | bytes 73736 | tf_op jit(solution)/shard_map/ppermute | solution.py:779
  13.2 2.3 %stream.1 = (f32[2048,256]{1,0:T(8,128)S(1)}, f32[56,384]{1,0:T(8,128)S(1)}, bf16[1360,256]{1,0:T(8,128)(2,1)S(1)}) custom-call(bf16[2048,256]{1,0:T(8,128)(2,1)} %dist_in.3, bf16[1360,256]{1,0:T(8,128)(2,1)} %constant.9.clone.block_in, f32[32,128]{1,0:T(8,128)} %constant.10.clone.pairs_in, bf16[16,16,128]{2,1,0:T(8,128)(2,1)} %constant.11.clone.own_in, ...), custom_call_target="tpu_custom_call" | custom-call | flops 600000000 | bytes 4000000 | tf_op jit(solution)/shard_map/stream/pallas_call | solution.py:780
  15.5 1.2 %collective-permute-done.refs_5_ = f32[48,128]{1,0:T(8,128)S(1)} collective-permute-done((f32[48,128]{1,0:T(8,128)}, f32[48,128]{1,0:T(8,128)S(1)}, u32[]{:S(2)}, u32[]{:S(2)}) %collective-permute-start) | collective-permute-done | bytes 24608 | tf_op jit(solution)/shard_map/ppermute | solution.py:779
  16.7 0.0 copy-start
  16.7 3.4 %all-to-all-done.refs_0_ = f32[16,40,128]{2,1,0:T(8,128)S(1)} async-done(((f32[16,40,128]{2,1,0:T(8,128)}), f32[16,40,128]{2,1,0:T(8,128)S(1)}, u32[]{:S(2)}, u32[]{:S(2)}) %all-to-all-start) | async-done | bytes 327712 | tf_op jit(solution)/shard_map/all_to_all | solution.py:774
  20.1 2.8 %fields.1 = (f32[28,16,256]{2,1,0:T(8,128)S(1)}, f32[16,16,128]{2,1,0:T(8,128)}) custom-call(f32[16,40,128]{2,1,0:T(8,128)S(1)} %all-to-all-done.refs_0_, f32[56,384]{1,0:T(8,128)S(1)} %get-tuple-element.16.refs_1_.refs_2_, bf16[1360,256]{1,0:T(8,128)(2,1)S(1)} %get-tuple-element.17.refs_2_.refs_3_), custom_call_target="tpu_custom_call" | custom-call | tf_op jit(solution)/shard_map/fields/pallas_call | solution.py:802
  22.9 18.6 %all_to_all.10.refs_0_ = f32[16,16,128]{2,1,0:T(8,128)S(1)} all-to-all(f32[16,16,128]{2,1,0:T(8,128)} %get-tuple-element.18), channel_id=1, replica_groups=mesh['space'=16,'vel'=16] {'space'}, dimensions={0} | all-to-all | bytes 262144 | tf_op jit(solution)/shard_map/all_to_all | solution.py:815
  41.5 0.0 copy-done
  41.5 5.9 %update.1 = (bf16[2048,256]{1,0:T(8,128)(2,1)}, f32[13,16]{1,0:T(8,128)}) custom-call(f32[16,16,128]{2,1,0:T(8,128)S(1)} %all_to_all.10.refs_0_, f32[28,16,256]{2,1,0:T(8,128)S(1)} %get-tuple-element.19.refs_1_, f32[56,384]{1,0:T(8,128)S(1)} %get-tuple-element.16.refs_1_.refs_2_, bf16[1360,256]{1,0:T(8,128)(2,1)S(1)} %get-tuple-element.17.refs_2_.refs_3_, ...), custom_call_target="tpu_custom_call" | custom-call | tf_op jit(solution)/shard_map/update/pallas_call | solution.py:816
Async XLA Ops:
  3.7 16.4 %all-to-all-start = ((f32[16,40,128]{2,1,0:T(8,128)}), f32[16,40,128]{2,1,0:T(8,128)S(1)}, u32[]{:S(2)}, u32[]{:S(2)}) async-start(f32[16,40,128]{2,1,0:T(8,128)} %get-tuple-element.12), calls=%async_computation | async-start | bytes 655360 | tf_op jit(solution)/shard_map/all_to_all | solution.py:774
  9.9 6.8 %collective-permute-start = (f32[48,128]{1,0:T(8,128)}, f32[48,128]{1,0:T(8,128)S(1)}, u32[]{:S(2)}, u32[]{:S(2)}) collective-permute-start(f32[48,128]{1,0:T(8,128)} %get-tuple-element.14), channel_id=1, source_target_pairs={{8,24},{9,25},{10,26},{11,27},{12,28},{13,29},{14,30},{15,31},{24,... | collective-permute-start | bytes 73736 | tf_op jit(solution)/shard_map/ppermute | solution.py:779
  16.7 24.8 %copy-start = (f32[48,128]{1,0:T(8,128)}, f32[48,128]{1,0:T(8,128)S(1)}, u32[]{:S(2)}) copy-start(f32[48,128]{1,0:T(8,128)S(1)} %collective-permute-done.refs_5_) | copy-start | bytes 73732

commit v6 on v5

--- a/solution.py
+++ b/solution.py
@@ -176,7 +176,7 @@
     return made
 
 
-def sums_kernel(dist_in, p3_in, start_in, packed, edges, dist, p3, start, whole, padded, sems, sends):
+def sums_kernel(dist_in, p3_in, start_in, packed, edges, dist, p3, start, padded, sems):
     positive = lax.axis_index("vel") >= PEERS // 2
     halves = [pl.ds(u * BLOCK, BLOCK) for u in range(2)]
     pairs = [(p3_in, p3), (start_in, start)]
@@ -186,14 +186,16 @@
     waits[1].wait()
     padded[...] = jnp.zeros((16, 128), f32)
     padded[0:K, 0:16] = start[...]
-    whole[32:40, :] = padded[0:8, :] + pltpu.roll(padded[8:16, :], 16, 1)
+    owned = padded[0:8, :] + pltpu.roll(padded[8:16, :], 16, 1)
+    for j in range(PEERS):
+        packed[j, 32:40, :] = owned
     for u in range(2):
         waits[2 + u].wait()
         y = jnp.dot(p3[...], dist[halves[u], :], preferred_element_type=f32)
         w = y[0:8] + y[8:16] + y[16:24]
-        whole[8 * u : 8 * u + 8, :] = w[:, 0:128]
-        whole[16 + 8 * u : 24 + 8 * u, :] = w[:, 128:256]
-    going = copies_of([(whole, packed.at[j]) for j in range(PEERS)], sends)
+        for j in range(PEERS):
+            packed[j, 8 * u : 8 * u + 8, :] = w[:, 0:128]
+            packed[j, 16 + 8 * u : 24 + 8 * u, :] = w[:, 128:256]
     e_lane = lanes_of((16, CELLS))
     e_row = rows_of((16, CELLS))
     cell = jnp.where(positive, CELLS - 1 - e_row, e_row)
@@ -204,8 +206,6 @@
             for k in range(8):
                 at = 16 * n + 8 * u + k
                 edges[at : at + 1, :] = e[n : n + 1, 128 * k : 128 * k + 128]
-    for copy in going:
-        copy.wait()
 
 
 N_FIELDS = 28
@@ -214,16 +214,31 @@
 STRIPS = 512
 
 
+def tiles_of(x):
+    return [x[:, 128 * t : 128 * t + 128] for t in range(x.shape[1] // 128)]
+
+
 def own_shifts():
-    lane = lanes_of((16, CELLS))
+    lane = lanes_of((16, 128))
+    zero = jnp.zeros((16, 128), f32)
 
     def up(x):
-        return jnp.where(lane == 0, 0.0, pltpu.roll(x, 1, 1))
+        first, second = (pltpu.roll(t, 1, 1) for t in tiles_of(x))
+        return jnp.concatenate([jnp.where(lane == 0, zero, first), jnp.where(lane == 0, first, second)], axis=1)
 
     def down(x):
-        return jnp.where(lane == CELLS - 1, 0.0, pltpu.roll(x, CELLS - 1, 1))
+        first, second = (pltpu.roll(t, 127, 1) for t in tiles_of(x))
+        return jnp.concatenate([jnp.where(lane == 127, second, first), jnp.where(lane == 127, zero, second)], axis=1)
 
     return up, down
+
+
+def strip_up(x):
+    return jnp.concatenate([pltpu.roll(t, 1, 1) for t in tiles_of(x)], axis=1)
+
+
+def strip_down(x):
+    return jnp.concatenate([pltpu.roll(t, 127, 1) for t in tiles_of(x)], axis=1)
 
 
 def advance_three(keep, base, ups, downs, up, down):
@@ -326,32 +341,45 @@
     return fields, plain, once, again
 
 
+EARLY = 4 * 1 + 4 * 6
+
+
 def inner_products(plain, once, again, counted, table):
-    kept_plain = [[counted * x for x in xs] for xs in plain]
-    kept_once = [[counted * x for x in xs] for xs in once]
-    tiles = counted.shape[1] // 128
-    table[208:256, :] = jnp.zeros((48, 128), f32)
+    lefts = [[[counted * x for x in xs] for xs in xss] for xss in (plain, once)]
+    rights = [plain, once, again]
+    if counted.shape[1] == STRIPS:
+        def folded(x):
+            halves = [x[:, 0:256], x[:, 256:512]]
+            moved = [pltpu.roll(t, 16, 1) for t in tiles_of(halves[1])]
+            return halves[0] + jnp.concatenate(moved, axis=1)
+
+        lefts = [[[folded(x) for x in xs] for xs in xss] for xss in lefts]
+        rights = lefts + [[[folded(counted * x) for x in xs] for xs in again]]
+    table[EARLY:256, :] = jnp.zeros((256 - EARLY, 128), f32)
+    table[256 : 256 + EARLY, :] = jnp.zeros((EARLY, 128), f32)
+    table[len(PAIRS) + 128 : 384, :] = jnp.zeros((256 - len(PAIRS), 128), f32)
+    ones = jnp.ones((8, 128), f32)
+    tops = []
     for n, (stage, quantity, i, j) in enumerate(PAIRS):
-        a, b = ((kept_plain, plain), (kept_plain, once), (kept_once, once), (kept_once, again))[quantity]
-        product = a[stage][i] * b[stage][j]
-        folded = product[:, 0:128]
-        for t in range(1, tiles):
-            folded = folded + product[:, 128 * t : 128 * t + 128]
-        table[n : n + 1, :] = jnp.sum(folded[0:8] + folded[8:16], axis=0, keepdims=True)
-    ones = jnp.ones((8, 128), f32)
-    return [
-        lax.dot_general(
-            ones,
-            table[128 * n : 128 * n + 128, :],
-            (((1,), (1,)), ((), ())),
-            precision=lax.Precision.HIGHEST,
-            preferred_element_type=f32,
+        x, y = ((0, 0), (0, 1), (1, 1), (1, 2))[quantity]
+        product = lefts[x][stage][i] * rights[y][stage][j]
+        half = product[:, 0:128] + product[:, 128:256]
+        at = n if n < EARLY else n + 128
+        table[at : at + 1, :] = jnp.sum(half[0:8] + half[8:16], axis=0, keepdims=True)
+    for n in range(3):
+        tops.append(
+            lax.dot_general(
+                ones,
+                table[128 * n : 128 * n + 128, :],
+                (((1,), (1,)), ((), ())),
+                precision=lax.Precision.HIGHEST,
+                preferred_element_type=f32,
+            )
         )
-        for n in range(2)
-    ]
-
-
-def fields_kernel(n_space, got, known, block, fields, sent, table, line, sems):
+    return tops
+
+
+def fields_kernel(n_space, got, known, block, fields, sent, table):
     slab = lax.axis_index("space")
     wide = (16, CELLS)
     w = jnp.concatenate([got[:, 16 * t : 16 * t + 16, :].reshape(PEERS * 16, 128) for t in range(2)], axis=1)
@@ -404,11 +432,11 @@
             tile = jnp.where((at >= SIDE) & (at < 16), begin, tile)
             end = pltpu.roll(mu[1 + 2 * n][:, 128:256], (32 * n + 32) % 128, 1)
             tile = jnp.where((at >= 16 + SIDE) & (at < 32), end, tile)
-    row_a = jnp.broadcast_to(tops[0][0:1], (16, 128))
-    row_b = jnp.broadcast_to(tops[1][0:1], (16, 128))
-    line[...] = jnp.where(row1 == 14, row_a, jnp.where(row1 == 15, row_b, tile))
-    for copy in copies_of([(line, sent.at[j]) for j in range(n_space)], sems):
-        copy.wait()
+    row_a = jnp.broadcast_to(tops[0][0:1] + tops[1][0:1], (16, 128))
+    row_b = jnp.broadcast_to(tops[2][0:1], (16, 128))
+    tile = jnp.where(row1 == 14, row_a, jnp.where(row1 == 15, row_b, tile))
+    for j in range(n_space):
+        sent[j] = tile
 
 
 def speeds_of(shape):
@@ -434,7 +462,7 @@
 def banded(weights, u, distance):
     value = jnp.zeros(distance.shape, f32)
     for n, x in enumerate(weights):
-        row = jnp.broadcast_to(x[8 * u : 8 * u + 1, 0:CELLS], distance.shape)
+        row = jnp.broadcast_to(x[8 * u : 8 * u + 1, 0 : distance.shape[1]], distance.shape)
         value = jnp.where(distance == n, row, value)
     return value
 
@@ -522,10 +550,11 @@
     shape = (16, STRIPS)
     lane = lanes_of(shape)
     row = rows_of(shape)
-    at = (lane + 16) % 32
-    valid = (lane >= 16) & (lane < 16 + 32 * (n_space - 1)) & (at < 2 * SIDE)
+    at = lane % 32
+    valid = (lane < 32 * (n_space - 1)) & (at < 2 * SIDE)
     mask = jnp.where(valid, 1.0, 0.0)
     moments = jnp.where(row < K, mask, 0.0)
+    raw = [pltpu.roll(x, STRIPS - 16, 1) for x in raw]
     closer = [pltpu.roll(x, STRIPS - 3, 1) for x in raw]
     arrays = [jnp.where(at < SIDE, x, y) for x, y in zip(raw, closer)]
     r = mask * jnp.broadcast_to(arrays[3][K : K + 1], shape)
@@ -534,8 +563,8 @@
     downs = [pltpu.roll(x, STRIPS - 16, 1) for x in raw[:3]]
     downs = [jnp.where((at >= SIDE) & (at < SIDE + 3), moments * x, 0.0) for x in downs]
     zero = jnp.zeros(shape, f32)
-    over_up = advance_three(1.0 - r, zero, ups, [], shift_up, shift_down)
-    over_down = advance_three(1.0 - r, zero, [], downs, shift_up, shift_down)
+    over_up = advance_three(1.0 - r, zero, ups, [], strip_up, strip_down)
+    over_down = advance_three(1.0 - r, zero, [], downs, strip_up, strip_down)
     s = [x + jnp.where(at < SIDE, y, z) for x, y, z in zip((s1, s2, s3), over_down, over_up)]
     s = [mask * x for x in s]
     counted = jnp.where((at >= SIDE - RIM) & (at < SIDE + RIM), mask, 0.0)
@@ -570,15 +599,16 @@
     (s1, s2, s3), strip_start, strip_r, strip_mask, counted = strips_of(n_space, sent)
     diffusion = jnp.concatenate([table[0:16, 128:256]] * 4, axis=1)
     strip_fields, plain, once, again = fields_of(
-        s1, s2, s3, strip_start, strip_r, strip_mask, diffusion, block, shift_up, shift_down
+        s1, s2, s3, strip_start, strip_r, strip_mask, diffusion, block, strip_up, strip_down
     )
     tops = inner_products(plain, once, again, counted, products)
     gathered = sent[0, 8:16, :]
     for j in range(1, n_space):
         gathered = gathered + sent[j, 8:16, :]
     row8 = rows_of((8, 128))
-    line_a = gathered[6:7] + tops[0][0:1]
-    line_b = gathered[7:8] + tops[1][0:1]
+    early = jnp.where(row8 == 0, gathered[6:7] + tops[0][0:1], 0.0) * known(48)
+    line_a = gathered[6:7] + tops[1][0:1]
+    line_b = gathered[7:8] + tops[2][0:1]
     total = jnp.where(row8 == 0, line_a, jnp.where(row8 == 1, line_b, 0.0))
     total = total * known(48)
     cpl = table[0:16, 0:128]
@@ -611,8 +641,8 @@
     def choose(index, zero, one, two):
         return jnp.where(index == 0, zero, jnp.where(index == 1, one, two))
 
-    a1, b1 = weights_of(0, total)
-    a2, b2 = weights_of(1, total * choose(li, 1.0, a1, b1) * choose(ri, 1.0, a1, b1))
+    a1, b1 = weights_of(0, early)
+    a2, b2 = weights_of(1, early * choose(li, 1.0, a1, b1) * choose(ri, 1.0, a1, b1))
 
     def both(index):
         outer = (index >= 3).astype(jnp.int32) + (index >= 6).astype(jnp.int32)
@@ -652,7 +682,7 @@
     far_right = (lane1 < 2 * has_right)
     wide = []
     for x, y in zip(own, strips):
-        y = pltpu.roll(y, lax.rem(STRIPS + 16 - 32 * slab, STRIPS), 1)[:, 0:128]
+        y = pltpu.roll(y, lax.rem(STRIPS + 32 - 32 * slab, STRIPS), 1)[:, 0:128]
         from_left = pltpu.roll(y, 128 - SIDE, 1)
         from_right = pltpu.roll(y, 96 - SIDE, 1)
         tiles = [
@@ -682,9 +712,11 @@
 
     weights = bands_of(r, positive)
     towards = jnp.where(positive, 1, -1)
-    at8 = rows_of((8, CELLS))
+    at8 = rows_of((8, 128))
     at8 = jnp.where(positive, -1 - at8, at8 + CELLS)
-    distance = (lanes_of((8, CELLS)) - at8) * towards
+    low = jnp.where(positive, 0, CELLS - 128)
+    distance = (lanes_of((8, 128)) + low - at8) * towards
+    weights = [jnp.where(positive, x[:, 0:128], x[:, 128:256]) for x in weights]
     ends[...] = jnp.zeros((16, ROWS), f32)
     edge_copy.wait()
     for n in range(3):
@@ -704,10 +736,10 @@
             part = u * (BLOCK // UPDATE_ROWS) + n
             rows = pl.ds(part * UPDATE_ROWS, UPDATE_ROWS)
             value = jnp.dot(block[pl.ds(n * UPDATE_ROWS, UPDATE_ROWS), 0:128], mixed, preferred_element_type=f32)
-            value += lax.dot_general(
-                ends[:, rows].astype(bf16), b, (((0,), (0,)), ((), ())), preferred_element_type=f32
-            )
-            done[rows, :] = (base[rows, :] + value).astype(bf16)
+            near = lax.dot_general(ends[:, rows].astype(bf16), b, (((0,), (0,)), ((), ())), preferred_element_type=f32)
+            value += base[rows, :]
+            done[rows, 0:128] = (value[:, 0:128] + jnp.where(positive, near, 0.0)).astype(bf16)
+            done[rows, 128:256] = (value[:, 128:256] + jnp.where(positive, 0.0, near)).astype(bf16)
             copy = pltpu.make_async_copy(done.at[rows, :], out.at[rows, :], sems.at[part])
             copy.start()
             sends.append(copy)
@@ -756,17 +788,15 @@
         flags = wall_flags.reshape(1, CELLS)
         packed, edges = pl.pallas_call(
             sums_kernel,
-            out_shape=(stored((PEERS, 40, 128)), stored((48, 128))),
+            out_shape=(shaped((PEERS, 40, 128)), shaped((48, 128))),
             in_specs=[hbm()] * 3,
-            out_specs=(hbm(), vmem()),
+            out_specs=(vmem(), vmem()),
             scratch_shapes=[
                 pltpu.VMEM((ROWS, CELLS), bf16),
                 pltpu.VMEM((32, BLOCK), bf16),
                 pltpu.VMEM((K, 16), f32),
-                pltpu.VMEM((40, 128), f32),
                 pltpu.VMEM((16, 128), f32),
                 pltpu.SemaphoreType.DMA((4,)),
-                pltpu.SemaphoreType.DMA((PEERS,)),
             ],
             compiler_params=limit(8),
             name="sums",
@@ -801,14 +831,10 @@
         got, base, edges = lax.optimization_barrier((got, base, edges))
         fields, sent = pl.pallas_call(
             lambda *refs: fields_kernel(n_space, *refs),
-            out_shape=(shaped((N_FIELDS, 16, CELLS)), stored((n_space, 16, 128))),
+            out_shape=(shaped((N_FIELDS, 16, CELLS)), shaped((n_space, 16, 128))),
             in_specs=[vmem()] * 3,
-            out_specs=(vmem(), hbm()),
-            scratch_shapes=[
-                pltpu.VMEM((256, 128), f32),
-                pltpu.VMEM((16, 128), f32),
-                pltpu.SemaphoreType.DMA((n_space,)),
-            ],
+            out_specs=(vmem(), vmem()),
+            scratch_shapes=[pltpu.VMEM((384, 128), f32)],
             compiler_params=limit(12),
             name="fields",
         )(*near(got, known, constants))
@@ -821,7 +847,7 @@
             scratch_shapes=[
                 pltpu.VMEM((ROWS, CELLS), bf16),
                 pltpu.VMEM((K, 16), f32),
-                pltpu.VMEM((256, 128), f32),
+                pltpu.VMEM((384, 128), f32),
                 pltpu.VMEM((48, 128), f32),
                 pltpu.VMEM((16, ROWS), f32),
                 pltpu.SemaphoreType.DMA((ROWS // UPDATE_ROWS + 2,)),

time: 47.8 us -> 45.7 us (0.956)
  Pallas kernels: 14.1 us -> 12.2 us
    pallas_call x1, Pallas kernels: 2.79 us -> 1.95 us  [per_device(): pl.pallas_call(lambda *refs: fields_kernel(n_space, *refs), out_shape=(sh...]
    pallas_call x1, Pallas kernels: 3.1 us -> 2.39 us  [per_device(): pl.pallas_call(sums_kernel, out_shape=(shaped((PEERS, 40, 128)), shaped((...]
where the time goes in v6:
time: 45.7 us; the launch traced here: 45.4 us
  blocking collectives  18.4 us (40%)
  Pallas kernels  12.2 us (27%)
  starting transfers between devices  9.49 us (21%)
  waiting for transfers between devices  4.58 us (10%)
  between operations  0.66 us (1%)
    all_to_all x1, blocking collectives, per_device(): lax.all_to_all(sent, 'space', split_axis=0, concat_axis=0, tiled=True)  18.4 us
    all_to_all x1, starting transfers between devices, per_device(): got = lax.all_to_all(packed, 'vel', split_axis=0, concat_axis=0, tiled=True)  6.15 us
    pallas_call x1, Pallas kernels, per_device(): pl.pallas_call(lambda *refs: update_kernel(n_space, *refs), out_shape=(st...  5.62 us
    all_to_all x1, waiting for transfers between devices, per_device(): got = lax.all_to_all(packed, 'vel', split_axis=0, concat_axis=0, tiled=True)  3.6 us
    ppermute x1, starting transfers between devices, per_device(): edges = lax.ppermute(edges, ('space', 'vel'), downwind)  3.34 us
    pallas_call x1, Pallas kernels, per_device(): pl.pallas_call(sums_kernel, out_shape=(shaped((PEERS, 40, 128)), shaped((...  2.39 us
    pallas_call x1, Pallas kernels, per_device(): pl.pallas_call(stream_kernel, out_shape=(shaped((ROWS, CELLS)), shaped((5...  2.28 us
    pallas_call x1, Pallas kernels, per_device(): pl.pallas_call(lambda *refs: fields_kernel(n_space, *refs), out_shape=(sh...  1.95 us
  transfers between devices with their start and end apart: 2, of which 2 were waited for; matrix products, arithmetic and copies ran while one was open for 0% of the time, Pallas kernels for 5%

profile of v6, /device:TPU:2, one launch (start us, length us, event | category | flops | bytes accessed | tf_op | source)
XLA Modules:
  0.0 45.4 jit_solution(11176292406597748684)
XLA Ops:
  0.6 2.4 %sums.1 = (f32[16,40,128]{2,1,0:T(8,128)}, f32[48,128]{1,0:T(8,128)S(1)}) custom-call(bf16[2048,256]{1,0:T(8,128)(2,1)} %dist_in.3, bf16[32,1024]{1,0:T(8,128)(2,1)} %constant.8.clone.p3_in, f32[13,16]{1,0:T(8,128)} %start_in.1), custom_call_target="tpu_custom_call" | custom-call | tf_op jit(solution)/shard_map/sums/pallas_call | solution.py:789
  3.0 6.1 %all-to-all-start = ((f32[16,40,128]{2,1,0:T(8,128)}), f32[16,40,128]{2,1,0:T(8,128)S(1)}, u32[]{:S(2)}, u32[]{:S(2)}) async-start(f32[16,40,128]{2,1,0:T(8,128)} %get-tuple-element.12), calls=%async_computation | async-start | bytes 655360 | tf_op jit(solution)/shard_map/all_to_all | solution.py:804
  9.2 3.3 %collective-permute-start = (f32[48,128]{1,0:T(8,128)S(1)}, f32[48,128]{1,0:T(8,128)S(1)}, u32[]{:S(2)}, u32[]{:S(2)}) collective-permute-start(f32[48,128]{1,0:T(8,128)S(1)} %get-tuple-element.14), channel_id=1, source_target_pairs={{8,24},{9,25},{10,26},{11,27},{12,28},{13,29},{14,30},{15,31},{24,... | collective-permute-start | bytes 73736 | tf_op jit(solution)/shard_map/ppermute | solution.py:809
  12.5 2.3 %stream.1 = (f32[2048,256]{1,0:T(8,128)S(1)}, f32[56,384]{1,0:T(8,128)S(1)}, bf16[1360,256]{1,0:T(8,128)(2,1)S(1)}) custom-call(bf16[2048,256]{1,0:T(8,128)(2,1)} %dist_in.3, bf16[1360,256]{1,0:T(8,128)(2,1)} %constant.9.clone.block_in, f32[32,128]{1,0:T(8,128)} %constant.10.clone.pairs_in, bf16[16,16,128]{2,1,0:T(8,128)(2,1)} %constant.11.clone.own_in, ...), custom_call_target="tpu_custom_call" | custom-call | flops 600000000 | bytes 4000000 | tf_op jit(solution)/shard_map/stream/pallas_call | solution.py:810
  14.8 1.0 %collective-permute-done.refs_5_ = f32[48,128]{1,0:T(8,128)S(1)} collective-permute-done((f32[48,128]{1,0:T(8,128)S(1)}, f32[48,128]{1,0:T(8,128)S(1)}, u32[]{:S(2)}, u32[]{:S(2)}) %collective-permute-start) | collective-permute-done | bytes 24608 | tf_op jit(solution)/shard_map/ppermute | solution.py:809
  15.8 0.0 copy-start
  15.8 3.6 %all-to-all-done.refs_0_ = f32[16,40,128]{2,1,0:T(8,128)S(1)} async-done(((f32[16,40,128]{2,1,0:T(8,128)}), f32[16,40,128]{2,1,0:T(8,128)S(1)}, u32[]{:S(2)}, u32[]{:S(2)}) %all-to-all-start) | async-done | bytes 327712 | tf_op jit(solution)/shard_map/all_to_all | solution.py:804
  19.4 2.0 %fields.1 = (f32[28,16,256]{2,1,0:T(8,128)S(1)}, f32[16,16,128]{2,1,0:T(8,128)S(1)}) custom-call(f32[16,40,128]{2,1,0:T(8,128)S(1)} %all-to-all-done.refs_0_, f32[56,384]{1,0:T(8,128)S(1)} %get-tuple-element.16.refs_1_.refs_2_, bf16[1360,256]{1,0:T(8,128)(2,1)S(1)} %get-tuple-element.17.refs_2_.refs_3_), custom_call_target="tpu_custom_call" | custom-call | tf_op jit(solution)/shard_map/fields/pallas_call | solution.py:832
  21.4 18.4 %all_to_all.10.refs_0_ = f32[16,16,128]{2,1,0:T(8,128)S(1)} all-to-all(f32[16,16,128]{2,1,0:T(8,128)S(1)} %get-tuple-element.18), channel_id=1, replica_groups=mesh['space'=16,'vel'=16] {'space'}, dimensions={0} | all-to-all | bytes 262144 | tf_op jit(solution)/shard_map/all_to_all | solution.py:841
  39.8 0.0 copy-done
  39.8 5.6 %update.1 = (bf16[2048,256]{1,0:T(8,128)(2,1)}, f32[13,16]{1,0:T(8,128)}) custom-call(f32[16,16,128]{2,1,0:T(8,128)S(1)} %all_to_all.10.refs_0_, f32[28,16,256]{2,1,0:T(8,128)S(1)} %get-tuple-element.19.refs_1_, f32[56,384]{1,0:T(8,128)S(1)} %get-tuple-element.16.refs_1_.refs_2_, bf16[1360,256]{1,0:T(8,128)(2,1)S(1)} %get-tuple-element.17.refs_2_.refs_3_, ...), custom_call_target="tpu_custom_call" | custom-call | tf_op jit(solution)/shard_map/update/pallas_call | solution.py:842
Async XLA Ops:
  3.0 16.4 %all-to-all-start = ((f32[16,40,128]{2,1,0:T(8,128)}), f32[16,40,128]{2,1,0:T(8,128)S(1)}, u32[]{:S(2)}, u32[]{:S(2)}) async-start(f32[16,40,128]{2,1,0:T(8,128)} %get-tuple-element.12), calls=%async_computation | async-start | bytes 655360 | tf_op jit(solution)/shard_map/all_to_all | solution.py:804
  9.2 6.6 %collective-permute-start = (f32[48,128]{1,0:T(8,128)S(1)}, f32[48,128]{1,0:T(8,128)S(1)}, u32[]{:S(2)}, u32[]{:S(2)}) collective-permute-start(f32[48,128]{1,0:T(8,128)S(1)} %get-tuple-element.14), channel_id=1, source_target_pairs={{8,24},{9,25},{10,26},{11,27},{12,28},{13,29},{14,30},{15,31},{24,... | collective-permute-start | bytes 73736 | tf_op jit(solution)/shard_map/ppermute | solution.py:809
  15.8 24.0 %copy-start = (f32[48,128]{1,0:T(8,128)}, f32[48,128]{1,0:T(8,128)S(1)}, u32[]{:S(2)}) copy-start(f32[48,128]{1,0:T(8,128)S(1)} %collective-permute-done.refs_5_) | copy-start | bytes 73732

commit v7 on v6

--- a/solution.py
+++ b/solution.py
@@ -85,23 +85,23 @@
     c16[:K] = shakhov
     g, gp, gm, g2p, g2m = (between(groups[k]) for k in (0, 1, 2, 3, 4))
     mats = [g, gp, gm, g * c16, gp * c16, gm * c16, g2p, g2m, g2p * c16, g2m * c16]
-    block = np.zeros((BLOCK + 336, 256), bf16)
-    block[16:176, 128:224] = six_terms(np.concatenate(mats, axis=0))
-    block[BLOCK:] = np.concatenate(parts_of(big, 3), axis=0)
-    p3 = np.concatenate(parts_of(proj, 3) + [np.zeros((8, BLOCK), bf16)], axis=0)
+    block = np.zeros((BLOCK + 224, 256), bf16)
+    block[16:176, 128:176] = three_terms(np.concatenate(mats, axis=0))
+    block[BLOCK:] = np.concatenate(parts_of(big, 2), axis=0)
+    p3 = np.concatenate(parts_of(proj, 2), axis=0)
     ph, pm = parts_of(phi.T, 2)
     block[0:BLOCK, 0:24] = np.concatenate([ph, ph, pm], axis=1)
     own = np.zeros((PEERS, 16, 16))
     for j in range(PEERS):
         for u in range(2):
             own[j, 8 * u : 8 * u + 8, :K] = cmat[2 * j + u].T
-    own = np.concatenate([six_terms(own), np.zeros((PEERS, 16, 32), bf16)], axis=2)
+    own = np.concatenate([three_terms(own), np.zeros((PEERS, 16, 80), bf16)], axis=2)
     return block, p3, own
 
 
-def six_terms(x):
-    h, m, low = parts_of(x, 3)
-    return np.concatenate([h, h, h, m, m, low], axis=-1)
+def three_terms(x):
+    h, m = parts_of(x, 2)
+    return np.concatenate([h, h, m], axis=-1)
 
 
 BASES = (1, 3, 9)
@@ -141,12 +141,10 @@
     return lax.broadcasted_iota(jnp.int32, shape, 0)
 
 
-def stack6(f):
+def split3(f):
     h = f.astype(bf16)
-    rest = f - h.astype(f32)
-    m = rest.astype(bf16)
-    low = (rest - m.astype(f32)).astype(bf16)
-    return jnp.concatenate([h, m, low, h, m, h], axis=0)
+    m = (f - h.astype(f32)).astype(bf16)
+    return jnp.concatenate([h, m, h], axis=0)
 
 
 def relax_of(rate, flags):
@@ -176,11 +174,18 @@
     return made
 
 
+CHUNKS = 8
+
+
+def chunks_of(source, target):
+    rows = [pl.ds(n * (ROWS // CHUNKS), ROWS // CHUNKS) for n in range(CHUNKS)]
+    return [(source.at[row, :], target.at[row, :]) for row in rows]
+
+
 def sums_kernel(dist_in, p3_in, start_in, packed, edges, dist, p3, start, padded, sems):
     positive = lax.axis_index("vel") >= PEERS // 2
     halves = [pl.ds(u * BLOCK, BLOCK) for u in range(2)]
-    pairs = [(p3_in, p3), (start_in, start)]
-    pairs += [(dist_in.at[half, :], dist.at[half, :]) for half in halves]
+    pairs = [(p3_in, p3), (start_in, start)] + chunks_of(dist_in, dist)
     waits = copies_of(pairs, sems)
     waits[0].wait()
     waits[1].wait()
@@ -190,9 +195,10 @@
     for j in range(PEERS):
         packed[j, 32:40, :] = owned
     for u in range(2):
-        waits[2 + u].wait()
+        for n in range(CHUNKS // 2):
+            waits[2 + u * (CHUNKS // 2) + n].wait()
         y = jnp.dot(p3[...], dist[halves[u], :], preferred_element_type=f32)
-        w = y[0:8] + y[8:16] + y[16:24]
+        w = y[0:8] + y[8:16]
         for j in range(PEERS):
             packed[j, 8 * u : 8 * u + 8, :] = w[:, 0:128]
             packed[j, 16 + 8 * u : 24 + 8 * u, :] = w[:, 128:256]
@@ -266,8 +272,8 @@
         return x - down(x)
 
     def times(first, last, inputs):
-        stacked = stack6(jnp.concatenate(inputs, axis=1) if len(inputs) > 1 else inputs[0])
-        y = jnp.dot(block[16 * first : 16 * last, 128:224], stacked, preferred_element_type=f32)
+        stacked = split3(jnp.concatenate(inputs, axis=1) if len(inputs) > 1 else inputs[0])
+        y = jnp.dot(block[16 * first : 16 * last, 128:176], stacked, preferred_element_type=f32)
         out = []
         for n in range(len(inputs)):
             cut = y[:, n * width : (n + 1) * width]
@@ -384,13 +390,10 @@
     wide = (16, CELLS)
     w = jnp.concatenate([got[:, 16 * t : 16 * t + 16, :].reshape(PEERS * 16, 128) for t in range(2)], axis=1)
     wh = w.astype(bf16)
-    w_rest = w - wh.astype(f32)
-    wm = w_rest.astype(bf16)
-    wl = (w_rest - wm.astype(f32)).astype(bf16)
-    y = jnp.dot(block[BLOCK : BLOCK + 336, :], wh, preferred_element_type=f32)
-    z = jnp.dot(block[BLOCK : BLOCK + 224, :], wm, preferred_element_type=f32)
-    t = jnp.dot(block[BLOCK : BLOCK + 112, :], wl, preferred_element_type=f32)
-    mu = ((y[224:336] + z[112:224]) + (y[112:224] + z[0:112])) + t + y[0:112]
+    wm = (w - wh.astype(f32)).astype(bf16)
+    y = jnp.dot(block[BLOCK : BLOCK + 224, :], wh, preferred_element_type=f32)
+    z = jnp.dot(block[BLOCK : BLOCK + 112, :], wm, preferred_element_type=f32)
+    mu = (y[112:224] + z) + y[0:112]
     mu = [mu[16 * g : 16 * g + 16] for g in range(7)]
 
     lane8 = lanes_of((8, 128))
@@ -517,19 +520,18 @@
     table[0:K, 0:K] = coupling_raw[...]
     c = table[0:16, 0:128]
     ch = c.astype(bf16).astype(f32)
-    cm = (c - ch).astype(bf16).astype(f32)
-    pieces = [ch, ch, ch, cm, cm, c - ch - cm]
-    six = pieces[0]
-    for n in range(1, 6):
-        six = six + pltpu.roll(pieces[n], 16 * n, 1)
-    block[0:16, 128:256] = six.astype(bf16)
+    pieces = [ch, ch, c - ch]
+    terms = pieces[0]
+    for n in range(1, 3):
+        terms = terms + pltpu.roll(pieces[n], 16 * n, 1)
+    block[0:16, 128:256] = terms.astype(bf16)
     block[176:192, 128:256] = own6[...]
     shape = (16, K)
     chosen = jnp.where(lanes_of(shape) == rows_of(shape), jnp.broadcast_to(diff_raw[...], shape), 0.0)
     table[0:16, 128:256] = jnp.broadcast_to(jnp.sum(chosen, axis=1, keepdims=True), (16, 128))
 
 
-UPDATE_ROWS = 512
+UPDATE_ROWS = 256
 
 
 def strips_of(n_space, sent):
@@ -697,7 +699,7 @@
     macro_copy = pltpu.make_async_copy(macro_part, macro, sems.at[ROWS // UPDATE_ROWS])
     macro_copy.start()
     y = jnp.dot(
-        block[176:192, 128:224], stack6(jnp.concatenate([f1, f2, f3], axis=1)), preferred_element_type=f32
+        block[176:192, 128:176], split3(jnp.concatenate([f1, f2, f3], axis=1)), preferred_element_type=f32
     )
     y1, y2, y3 = (y[:, n * WIDE : (n + 1) * WIDE] for n in range(3))
     a = speeds_of((16, WIDE))
@@ -793,10 +795,10 @@
             out_specs=(vmem(), vmem()),
             scratch_shapes=[
                 pltpu.VMEM((ROWS, CELLS), bf16),
-                pltpu.VMEM((32, BLOCK), bf16),
+                pltpu.VMEM((16, BLOCK), bf16),
                 pltpu.VMEM((K, 16), f32),
                 pltpu.VMEM((16, 128), f32),
-                pltpu.SemaphoreType.DMA((4,)),
+                pltpu.SemaphoreType.DMA((2 + CHUNKS,)),
             ],
             compiler_params=limit(8),
             name="sums",

time: 45.7 us -> 45.6 us (level)
  no operation moved by 1% of the time
where the time goes in v7:
time: 45.6 us; the launch traced here: 45.3 us
  blocking collectives  18.4 us (40%)
  Pallas kernels  12.1 us (27%)
  starting transfers between devices  9.49 us (21%)
  waiting for transfers between devices  4.61 us (10%)
  between operations  0.66 us (1%)
    all_to_all x1, blocking collectives, per_device(): lax.all_to_all(sent, 'space', split_axis=0, concat_axis=0, tiled=True)  18.4 us
    all_to_all x1, starting transfers between devices, per_device(): got = lax.all_to_all(packed, 'vel', split_axis=0, concat_axis=0, tiled=True)  6.15 us
    pallas_call x1, Pallas kernels, per_device(): pl.pallas_call(lambda *refs: update_kernel(n_space, *refs), out_shape=(st...  5.49 us
    all_to_all x1, waiting for transfers between devices, per_device(): got = lax.all_to_all(packed, 'vel', split_axis=0, concat_axis=0, tiled=True)  3.6 us
    ppermute x1, starting transfers between devices, per_device(): edges = lax.ppermute(edges, ('space', 'vel'), downwind)  3.34 us
    pallas_call x1, Pallas kernels, per_device(): pl.pallas_call(sums_kernel, out_shape=(shaped((PEERS, 40, 128)), shaped((...  2.47 us
    pallas_call x1, Pallas kernels, per_device(): pl.pallas_call(stream_kernel, out_shape=(shaped((ROWS, CELLS)), shaped((5...  2.25 us
    pallas_call x1, Pallas kernels, per_device(): pl.pallas_call(lambda *refs: fields_kernel(n_space, *refs), out_shape=(sh...  1.89 us
  transfers between devices with their start and end apart: 2, of which 2 were waited for; matrix products, arithmetic and copies ran while one was open for 0% of the time, Pallas kernels for 5%

profile of v7, /device:TPU:2, one launch (start us, length us, event | category | flops | bytes accessed | tf_op | source)
XLA Modules:
  0.0 45.3 jit_solution(1696125554661691296)
XLA Ops:
  0.6 2.5 %sums.1 = (f32[16,40,128]{2,1,0:T(8,128)}, f32[48,128]{1,0:T(8,128)S(1)}) custom-call(bf16[2048,256]{1,0:T(8,128)(2,1)} %dist_in.3, bf16[16,1024]{1,0:T(8,128)(2,1)} %constant.8.clone.p3_in, f32[13,16]{1,0:T(8,128)} %start_in.1), custom_call_target="tpu_custom_call" | custom-call | tf_op jit(solution)/shard_map/sums/pallas_call | solution.py:791
  3.1 6.1 %all-to-all-start = ((f32[16,40,128]{2,1,0:T(8,128)}), f32[16,40,128]{2,1,0:T(8,128)S(1)}, u32[]{:S(2)}, u32[]{:S(2)}) async-start(f32[16,40,128]{2,1,0:T(8,128)} %get-tuple-element.12), calls=%async_computation | async-start | bytes 655360 | tf_op jit(solution)/shard_map/all_to_all | solution.py:806
  9.3 3.3 %collective-permute-start = (f32[48,128]{1,0:T(8,128)S(1)}, f32[48,128]{1,0:T(8,128)S(1)}, u32[]{:S(2)}, u32[]{:S(2)}) collective-permute-start(f32[48,128]{1,0:T(8,128)S(1)} %get-tuple-element.14), channel_id=1, source_target_pairs={{8,24},{9,25},{10,26},{11,27},{12,28},{13,29},{14,30},{15,31},{24,... | collective-permute-start | bytes 73736 | tf_op jit(solution)/shard_map/ppermute | solution.py:811
  12.6 2.3 %stream.1 = (f32[2048,256]{1,0:T(8,128)S(1)}, f32[56,384]{1,0:T(8,128)S(1)}, bf16[1248,256]{1,0:T(8,128)(2,1)S(1)}) custom-call(bf16[2048,256]{1,0:T(8,128)(2,1)} %dist_in.3, bf16[1248,256]{1,0:T(8,128)(2,1)} %constant.9.clone.block_in, f32[32,128]{1,0:T(8,128)} %constant.10.clone.pairs_in, bf16[16,16,128]{2,1,0:T(8,128)(2,1)} %constant.11.clone.own_in, ...), custom_call_target="tpu_custom_call" | custom-call | flops 600000000 | bytes 4000000 | tf_op jit(solution)/shard_map/stream/pallas_call | solution.py:812
  14.9 1.0 %collective-permute-done.refs_5_ = f32[48,128]{1,0:T(8,128)S(1)} collective-permute-done((f32[48,128]{1,0:T(8,128)S(1)}, f32[48,128]{1,0:T(8,128)S(1)}, u32[]{:S(2)}, u32[]{:S(2)}) %collective-permute-start) | collective-permute-done | bytes 24608 | tf_op jit(solution)/shard_map/ppermute | solution.py:811
  15.9 0.0 copy-start
  15.9 3.6 %all-to-all-done.refs_0_ = f32[16,40,128]{2,1,0:T(8,128)S(1)} async-done(((f32[16,40,128]{2,1,0:T(8,128)}), f32[16,40,128]{2,1,0:T(8,128)S(1)}, u32[]{:S(2)}, u32[]{:S(2)}) %all-to-all-start) | async-done | bytes 327712 | tf_op jit(solution)/shard_map/all_to_all | solution.py:806
  19.5 1.9 %fields.1 = (f32[28,16,256]{2,1,0:T(8,128)S(1)}, f32[16,16,128]{2,1,0:T(8,128)S(1)}) custom-call(f32[16,40,128]{2,1,0:T(8,128)S(1)} %all-to-all-done.refs_0_, f32[56,384]{1,0:T(8,128)S(1)} %get-tuple-element.16.refs_1_.refs_2_, bf16[1248,256]{1,0:T(8,128)(2,1)S(1)} %get-tuple-element.17.refs_2_.refs_3_), custom_call_target="tpu_custom_call" | custom-call | tf_op jit(solution)/shard_map/fields/pallas_call | solution.py:834
  21.4 18.4 %all_to_all.10.refs_0_ = f32[16,16,128]{2,1,0:T(8,128)S(1)} all-to-all(f32[16,16,128]{2,1,0:T(8,128)S(1)} %get-tuple-element.18), channel_id=1, replica_groups=mesh['space'=16,'vel'=16] {'space'}, dimensions={0} | all-to-all | bytes 262144 | tf_op jit(solution)/shard_map/all_to_all | solution.py:843
  39.8 0.0 copy-done
  39.8 5.5 %update.1 = (bf16[2048,256]{1,0:T(8,128)(2,1)}, f32[13,16]{1,0:T(8,128)}) custom-call(f32[16,16,128]{2,1,0:T(8,128)S(1)} %all_to_all.10.refs_0_, f32[28,16,256]{2,1,0:T(8,128)S(1)} %get-tuple-element.19.refs_1_, f32[56,384]{1,0:T(8,128)S(1)} %get-tuple-element.16.refs_1_.refs_2_, bf16[1248,256]{1,0:T(8,128)(2,1)S(1)} %get-tuple-element.17.refs_2_.refs_3_, ...), custom_call_target="tpu_custom_call" | custom-call | tf_op jit(solution)/shard_map/update/pallas_call | solution.py:844
Async XLA Ops:
  3.1 16.4 %all-to-all-start = ((f32[16,40,128]{2,1,0:T(8,128)}), f32[16,40,128]{2,1,0:T(8,128)S(1)}, u32[]{:S(2)}, u32[]{:S(2)}) async-start(f32[16,40,128]{2,1,0:T(8,128)} %get-tuple-element.12), calls=%async_computation | async-start | bytes 655360 | tf_op jit(solution)/shard_map/all_to_all | solution.py:806
  9.3 6.6 %collective-permute-start = (f32[48,128]{1,0:T(8,128)S(1)}, f32[48,128]{1,0:T(8,128)S(1)}, u32[]{:S(2)}, u32[]{:S(2)}) collective-permute-start(f32[48,128]{1,0:T(8,128)S(1)} %get-tuple-element.14), channel_id=1, source_target_pairs={{8,24},{9,25},{10,26},{11,27},{12,28},{13,29},{14,30},{15,31},{24,... | collective-permute-start | bytes 73736 | tf_op jit(solution)/shard_map/ppermute | solution.py:811
  15.9 23.9 %copy-start = (f32[48,128]{1,0:T(8,128)}, f32[48,128]{1,0:T(8,128)S(1)}, u32[]{:S(2)}) copy-start(f32[48,128]{1,0:T(8,128)S(1)} %collective-permute-done.refs_5_) | copy-start | bytes 73732

commit v8 on v7

--- a/solution.py
+++ b/solution.py
@@ -194,6 +194,11 @@
     owned = padded[0:8, :] + pltpu.roll(padded[8:16, :], 16, 1)
     for j in range(PEERS):
         packed[j, 32:40, :] = owned
+    e_lane = lanes_of((16, 128))
+    e_row = rows_of((16, 128))
+    cell = jnp.where(positive, 127 - e_row, e_row)
+    pick = jnp.where((e_lane == cell) & (e_row < 3), 1.0, 0.0).astype(bf16)
+    side = pl.multiple_of(jnp.where(positive, 128, 0), 128)
     for u in range(2):
         for n in range(CHUNKS // 2):
             waits[2 + u * (CHUNKS // 2) + n].wait()
@@ -202,12 +207,8 @@
         for j in range(PEERS):
             packed[j, 8 * u : 8 * u + 8, :] = w[:, 0:128]
             packed[j, 16 + 8 * u : 24 + 8 * u, :] = w[:, 128:256]
-    e_lane = lanes_of((16, CELLS))
-    e_row = rows_of((16, CELLS))
-    cell = jnp.where(positive, CELLS - 1 - e_row, e_row)
-    pick = jnp.where((e_lane == cell) & (e_row < 3), 1.0, 0.0).astype(bf16)
-    for u in range(2):
-        e = lax.dot_general(pick, dist[halves[u], :], (((1,), (1,)), ((), ())), preferred_element_type=f32)
+        near = dist[halves[u], pl.ds(side, 128)]
+        e = lax.dot_general(pick, near, (((1,), (1,)), ((), ())), preferred_element_type=f32)
         for n in range(3):
             for k in range(8):
                 at = 16 * n + 8 * u + k
@@ -239,12 +240,19 @@
     return up, down
 
 
+STEP = (0, 0, 16, 16)
+
+
+def tile_roll(x, amount):
+    return jnp.concatenate([pltpu.roll(t, amount, 1) for t in tiles_of(x)], axis=1)
+
+
 def strip_up(x):
-    return jnp.concatenate([pltpu.roll(t, 1, 1) for t in tiles_of(x)], axis=1)
+    return tile_roll(x, 1)
 
 
 def strip_down(x):
-    return jnp.concatenate([pltpu.roll(t, 127, 1) for t in tiles_of(x)], axis=1)
+    return tile_roll(x, 127)
 
 
 def advance_three(keep, base, ups, downs, up, down):
@@ -355,9 +363,7 @@
     rights = [plain, once, again]
     if counted.shape[1] == STRIPS:
         def folded(x):
-            halves = [x[:, 0:256], x[:, 256:512]]
-            moved = [pltpu.roll(t, 16, 1) for t in tiles_of(halves[1])]
-            return halves[0] + jnp.concatenate(moved, axis=1)
+            return x[:, 0:256] + x[:, 256:512]
 
         lefts = [[[folded(x) for x in xs] for xs in xss] for xss in lefts]
         rights = lefts + [[[folded(counted * x) for x in xs] for xs in again]]
@@ -435,6 +441,7 @@
             tile = jnp.where((at >= SIDE) & (at < 16), begin, tile)
             end = pltpu.roll(mu[1 + 2 * n][:, 128:256], (32 * n + 32) % 128, 1)
             tile = jnp.where((at >= 16 + SIDE) & (at < 32), end, tile)
+    tile = pltpu.roll(tile, lax.rem(32 * lax.rem(slab, 4) + 112, 128), 1)
     row_a = jnp.broadcast_to(tops[0][0:1] + tops[1][0:1], (16, 128))
     row_b = jnp.broadcast_to(tops[2][0:1], (16, 128))
     tile = jnp.where(row1 == 14, row_a, jnp.where(row1 == 15, row_b, tile))
@@ -535,34 +542,32 @@
 
 
 def strips_of(n_space, sent):
-    quarter = lanes_of((16, 128)) // 32
     raw = []
+    lane1 = lanes_of((16, 128))
     for n in range(4):
+        which = ((lane1 + 128 - 32 * n) % 128 // 16 + 1) // 2
         tiles = []
         for t in range(4):
             tile = jnp.zeros((16, 128), f32)
-            for k in range(4):
-                j = 4 * t + k
-                if j < n_space:
-                    amount = 32 * (k - n) % 128
-                    moved = pltpu.roll(sent[j], amount, 1) if amount else sent[j]
-                    tile = jnp.where(quarter == k, moved, tile)
-            tiles.append(tile)
+            for k in range(5):
+                if 4 * t + k < n_space:
+                    tile = jnp.where(which == k, sent[4 * t + k], tile)
+            amount = (STEP[t] - 32 * n) % 128
+            tiles.append(pltpu.roll(tile, amount, 1) if amount else tile)
         raw.append(jnp.concatenate(tiles, axis=1))
     shape = (16, STRIPS)
-    lane = lanes_of(shape)
     row = rows_of(shape)
-    at = lane % 32
-    valid = (lane < 32 * (n_space - 1)) & (at < 2 * SIDE)
+    turned = jnp.concatenate([(lane1 + 128 - STEP[t]) % 128 + 128 * t for t in range(4)], axis=1)
+    at = turned % 32
+    valid = (turned < 32 * (n_space - 1)) & (at < 2 * SIDE)
     mask = jnp.where(valid, 1.0, 0.0)
     moments = jnp.where(row < K, mask, 0.0)
-    raw = [pltpu.roll(x, STRIPS - 16, 1) for x in raw]
-    closer = [pltpu.roll(x, STRIPS - 3, 1) for x in raw]
+    closer = [tile_roll(x, 128 - 3) for x in raw]
     arrays = [jnp.where(at < SIDE, x, y) for x, y in zip(raw, closer)]
     r = mask * jnp.broadcast_to(arrays[3][K : K + 1], shape)
     s1, s2, s3, start = (moments * x for x in arrays)
     ups = [jnp.where((at >= SIDE - 3) & (at < SIDE), moments * x, 0.0) for x in closer[:3]]
-    downs = [pltpu.roll(x, STRIPS - 16, 1) for x in raw[:3]]
+    downs = [tile_roll(x, 128 - 16) for x in raw[:3]]
     downs = [jnp.where((at >= SIDE) & (at < SIDE + 3), moments * x, 0.0) for x in downs]
     zero = jnp.zeros(shape, f32)
     over_up = advance_three(1.0 - r, zero, ups, [], strip_up, strip_down)
@@ -684,6 +689,7 @@
     far_right = (lane1 < 2 * has_right)
     wide = []
     for x, y in zip(own, strips):
+        y = jnp.concatenate([y[:, 0:256], tile_roll(y[:, 256:512], 112)], axis=1)
         y = pltpu.roll(y, lax.rem(STRIPS + 32 - 32 * slab, STRIPS), 1)[:, 0:128]
         from_left = pltpu.roll(y, 128 - SIDE, 1)
         from_right = pltpu.roll(y, 96 - SIDE, 1)

time: 45.6 us -> 45.5 us (level)
  no operation moved by 1% of the time
where the time goes in v8:
time: 45.5 us; the launch traced here: 45.1 us
  blocking collectives  18.4 us (40%)
  Pallas kernels  11.9 us (26%)
  starting transfers between devices  9.51 us (21%)
  waiting for transfers between devices  4.61 us (10%)
  between operations  0.66 us (1%)
    all_to_all x1, blocking collectives, per_device(): lax.all_to_all(sent, 'space', split_axis=0, concat_axis=0, tiled=True)  18.4 us
    all_to_all x1, starting transfers between devices, per_device(): got = lax.all_to_all(packed, 'vel', split_axis=0, concat_axis=0, tiled=True)  6.17 us
    pallas_call x1, Pallas kernels, per_device(): pl.pallas_call(lambda *refs: update_kernel(n_space, *refs), out_shape=(st...  5.33 us
    all_to_all x1, waiting for transfers between devices, per_device(): got = lax.all_to_all(packed, 'vel', split_axis=0, concat_axis=0, tiled=True)  3.6 us
    ppermute x1, starting transfers between devices, per_device(): edges = lax.ppermute(edges, ('space', 'vel'), downwind)  3.34 us
    pallas_call x1, Pallas kernels, per_device(): pl.pallas_call(sums_kernel, out_shape=(shaped((PEERS, 40, 128)), shaped((...  2.47 us
    pallas_call x1, Pallas kernels, per_device(): pl.pallas_call(stream_kernel, out_shape=(shaped((ROWS, CELLS)), shaped((5...  2.25 us
    pallas_call x1, Pallas kernels, per_device(): pl.pallas_call(lambda *refs: fields_kernel(n_space, *refs), out_shape=(sh...  1.89 us
  transfers between devices with their start and end apart: 2, of which 2 were waited for; matrix products, arithmetic and copies ran while one was open for 0% of the time, Pallas kernels for 5%

profile of v8, /device:TPU:2, one launch (start us, length us, event | category | flops | bytes accessed | tf_op | source)
XLA Modules:
  0.0 45.1 jit_solution(5713799208322808989)
XLA Ops:
  0.6 2.5 %sums.1 = (f32[16,40,128]{2,1,0:T(8,128)}, f32[48,128]{1,0:T(8,128)S(1)}) custom-call(bf16[2048,256]{1,0:T(8,128)(2,1)} %dist_in.3, bf16[16,1024]{1,0:T(8,128)(2,1)} %constant.8.clone.p3_in, f32[13,16]{1,0:T(8,128)} %start_in.1), custom_call_target="tpu_custom_call" | custom-call | tf_op jit(solution)/shard_map/sums/pallas_call | solution.py:797
  3.1 6.2 %all-to-all-start = ((f32[16,40,128]{2,1,0:T(8,128)}), f32[16,40,128]{2,1,0:T(8,128)S(1)}, u32[]{:S(2)}, u32[]{:S(2)}) async-start(f32[16,40,128]{2,1,0:T(8,128)} %get-tuple-element.12), calls=%async_computation | async-start | bytes 655360 | tf_op jit(solution)/shard_map/all_to_all | solution.py:812
  9.3 3.3 %collective-permute-start = (f32[48,128]{1,0:T(8,128)S(1)}, f32[48,128]{1,0:T(8,128)S(1)}, u32[]{:S(2)}, u32[]{:S(2)}) collective-permute-start(f32[48,128]{1,0:T(8,128)S(1)} %get-tuple-element.14), channel_id=1, source_target_pairs={{8,24},{9,25},{10,26},{11,27},{12,28},{13,29},{14,30},{15,31},{24,... | collective-permute-start | bytes 73736 | tf_op jit(solution)/shard_map/ppermute | solution.py:817
  12.6 2.3 %stream.1 = (f32[2048,256]{1,0:T(8,128)S(1)}, f32[56,384]{1,0:T(8,128)S(1)}, bf16[1248,256]{1,0:T(8,128)(2,1)S(1)}) custom-call(bf16[2048,256]{1,0:T(8,128)(2,1)} %dist_in.3, bf16[1248,256]{1,0:T(8,128)(2,1)} %constant.9.clone.block_in, f32[32,128]{1,0:T(8,128)} %constant.10.clone.pairs_in, bf16[16,16,128]{2,1,0:T(8,128)(2,1)} %constant.11.clone.own_in, ...), custom_call_target="tpu_custom_call" | custom-call | flops 600000000 | bytes 4000000 | tf_op jit(solution)/shard_map/stream/pallas_call | solution.py:818
  14.9 1.0 %collective-permute-done.refs_5_ = f32[48,128]{1,0:T(8,128)S(1)} collective-permute-done((f32[48,128]{1,0:T(8,128)S(1)}, f32[48,128]{1,0:T(8,128)S(1)}, u32[]{:S(2)}, u32[]{:S(2)}) %collective-permute-start) | collective-permute-done | bytes 24608 | tf_op jit(solution)/shard_map/ppermute | solution.py:817
  15.9 0.0 copy-start
  15.9 3.6 %all-to-all-done.refs_0_ = f32[16,40,128]{2,1,0:T(8,128)S(1)} async-done(((f32[16,40,128]{2,1,0:T(8,128)}), f32[16,40,128]{2,1,0:T(8,128)S(1)}, u32[]{:S(2)}, u32[]{:S(2)}) %all-to-all-start) | async-done | bytes 327712 | tf_op jit(solution)/shard_map/all_to_all | solution.py:812
  19.5 1.9 %fields.1 = (f32[28,16,256]{2,1,0:T(8,128)S(1)}, f32[16,16,128]{2,1,0:T(8,128)S(1)}) custom-call(f32[16,40,128]{2,1,0:T(8,128)S(1)} %all-to-all-done.refs_0_, f32[56,384]{1,0:T(8,128)S(1)} %get-tuple-element.16.refs_1_.refs_2_, bf16[1248,256]{1,0:T(8,128)(2,1)S(1)} %get-tuple-element.17.refs_2_.refs_3_), custom_call_target="tpu_custom_call" | custom-call | tf_op jit(solution)/shard_map/fields/pallas_call | solution.py:840
  21.4 18.4 %all_to_all.10.refs_0_ = f32[16,16,128]{2,1,0:T(8,128)S(1)} all-to-all(f32[16,16,128]{2,1,0:T(8,128)S(1)} %get-tuple-element.18), channel_id=1, replica_groups=mesh['space'=16,'vel'=16] {'space'}, dimensions={0} | all-to-all | bytes 262144 | tf_op jit(solution)/shard_map/all_to_all | solution.py:849
  39.8 0.0 copy-done
  39.8 5.3 %update.1 = (bf16[2048,256]{1,0:T(8,128)(2,1)}, f32[13,16]{1,0:T(8,128)}) custom-call(f32[16,16,128]{2,1,0:T(8,128)S(1)} %all_to_all.10.refs_0_, f32[28,16,256]{2,1,0:T(8,128)S(1)} %get-tuple-element.19.refs_1_, f32[56,384]{1,0:T(8,128)S(1)} %get-tuple-element.16.refs_1_.refs_2_, bf16[1248,256]{1,0:T(8,128)(2,1)S(1)} %get-tuple-element.17.refs_2_.refs_3_, ...), custom_call_target="tpu_custom_call" | custom-call | tf_op jit(solution)/shard_map/update/pallas_call | solution.py:850
Async XLA Ops:
  3.1 16.4 %all-to-all-start = ((f32[16,40,128]{2,1,0:T(8,128)}), f32[16,40,128]{2,1,0:T(8,128)S(1)}, u32[]{:S(2)}, u32[]{:S(2)}) async-start(f32[16,40,128]{2,1,0:T(8,128)} %get-tuple-element.12), calls=%async_computation | async-start | bytes 655360 | tf_op jit(solution)/shard_map/all_to_all | solution.py:812
  9.3 6.6 %collective-permute-start = (f32[48,128]{1,0:T(8,128)S(1)}, f32[48,128]{1,0:T(8,128)S(1)}, u32[]{:S(2)}, u32[]{:S(2)}) collective-permute-start(f32[48,128]{1,0:T(8,128)S(1)} %get-tuple-element.14), channel_id=1, source_target_pairs={{8,24},{9,25},{10,26},{11,27},{12,28},{13,29},{14,30},{15,31},{24,... | collective-permute-start | bytes 73736 | tf_op jit(solution)/shard_map/ppermute | solution.py:817
  15.9 23.9 %copy-start = (f32[48,128]{1,0:T(8,128)}, f32[48,128]{1,0:T(8,128)S(1)}, u32[]{:S(2)}) copy-start(f32[48,128]{1,0:T(8,128)S(1)} %collective-permute-done.refs_5_) | copy-start | bytes 73732

commit v9 on v8

--- a/solution.py
+++ b/solution.py
@@ -356,9 +356,12 @@
 
 
 EARLY = 4 * 1 + 4 * 6
-
-
-def inner_products(plain, once, again, counted, table):
+LATE_FROM = EARLY // 8 * 8
+EARLY_SHEETS = (EARLY + 7) // 8 * 64 + 8
+SHEETS = EARLY_SHEETS + 8 * (len(PAIRS) - LATE_FROM) + 8
+
+
+def product_operands(plain, once, again, counted):
     lefts = [[[counted * x for x in xs] for xs in xss] for xss in (plain, once)]
     rights = [plain, once, again]
     if counted.shape[1] == STRIPS:
@@ -367,31 +370,56 @@
 
         lefts = [[[folded(x) for x in xs] for xs in xss] for xss in lefts]
         rights = lefts + [[[folded(counted * x) for x in xs] for xs in again]]
-    table[EARLY:256, :] = jnp.zeros((256 - EARLY, 128), f32)
-    table[256 : 256 + EARLY, :] = jnp.zeros((EARLY, 128), f32)
-    table[len(PAIRS) + 128 : 384, :] = jnp.zeros((256 - len(PAIRS), 128), f32)
-    ones = jnp.ones((8, 128), f32)
-    tops = []
-    for n, (stage, quantity, i, j) in enumerate(PAIRS):
+    return lefts, rights
+
+
+def inner_products(operands, entries, first, sheets, table):
+    lefts, rights = operands
+    start = first // 8 * 8
+    stop = entries.stop
+    zero = jnp.zeros((8, 128), f32)
+    end = (stop + 7) // 8 * 8
+    for n in range(start, end):
+        if n not in entries:
+            sheets[8 * (n - start) : 8 * (n - start) + 8, :] = zero
+            continue
+        stage, quantity, i, j = PAIRS[n]
         x, y = ((0, 0), (0, 1), (1, 1), (1, 2))[quantity]
         product = lefts[x][stage][i] * rights[y][stage][j]
         half = product[:, 0:128] + product[:, 128:256]
-        at = n if n < EARLY else n + 128
-        table[at : at + 1, :] = jnp.sum(half[0:8] + half[8:16], axis=0, keepdims=True)
-    for n in range(3):
-        tops.append(
-            lax.dot_general(
-                ones,
-                table[128 * n : 128 * n + 128, :],
-                (((1,), (1,)), ((), ())),
-                precision=lax.Precision.HIGHEST,
-                preferred_element_type=f32,
-            )
+        sheets[8 * (n - start) : 8 * (n - start) + 8, :] = half[0:8] + half[8:16]
+    lines = (end + 127) // 128
+    if start:
+        table[0:start, :] = jnp.zeros((start, 128), f32)
+    if end < 128 * lines:
+        table[end : 128 * lines, :] = jnp.zeros((128 * lines - end, 128), f32)
+    for n in range(start, end, 8):
+        rows = [sheets[pl.ds(8 * (n - start) + k, 8, stride=8), :] for k in range(8)]
+        while len(rows) > 1:
+            rows = [p + q for p, q in zip(rows[0::2], rows[1::2])]
+        table[n : n + 8, :] = rows[0]
+    ones = jnp.ones((8, 128), f32)
+    return [
+        lax.dot_general(
+            ones,
+            table[128 * n : 128 * n + 128, :],
+            (((1,), (1,)), ((), ())),
+            precision=lax.Precision.HIGHEST,
+            preferred_element_type=f32,
         )
-    return tops
-
-
-def fields_kernel(n_space, got, known, block, fields, sent, table):
+        for n in range(lines)
+    ]
+
+
+def early_products(operands, sheets, table):
+    return inner_products(operands, range(EARLY), 0, sheets.at[0:EARLY_SHEETS, :], table.at[0:128, :])
+
+
+def late_products(operands, sheets, table):
+    return inner_products(operands, range(EARLY, len(PAIRS)), EARLY, sheets.at[EARLY_SHEETS:SHEETS, :], table.at[128:384, :])
+
+
+def fields_kernel(n_space, got, known, block, fields, sent, table, sheets):
     slab = lax.axis_index("space")
     wide = (16, CELLS)
     w = jnp.concatenate([got[:, 16 * t : 16 * t + 16, :].reshape(PEERS * 16, 128) for t in range(2)], axis=1)
@@ -424,7 +452,8 @@
     low = jnp.where(slab > 0, RIM, 0)
     high = jnp.where(slab < n_space - 1, CELLS - RIM, CELLS)
     counted = jnp.where((lane >= low) & (lane < high), 1.0, 0.0)
-    tops = inner_products(plain, once, again, counted, table)
+    operands = product_operands(plain, once, again, counted)
+    tops = early_products(operands, sheets, table) + late_products(operands, sheets, table)
 
     lane1 = lanes_of((16, 128))
     row1 = rows_of((16, 128))
@@ -591,6 +620,7 @@
     done,
     macro_part,
     products,
+    sheets,
     edges,
     ends,
     sems,
@@ -608,16 +638,13 @@
     strip_fields, plain, once, again = fields_of(
         s1, s2, s3, strip_start, strip_r, strip_mask, diffusion, block, strip_up, strip_down
     )
-    tops = inner_products(plain, once, again, counted, products)
+    operands = product_operands(plain, once, again, counted)
     gathered = sent[0, 8:16, :]
     for j in range(1, n_space):
         gathered = gathered + sent[j, 8:16, :]
     row8 = rows_of((8, 128))
-    early = jnp.where(row8 == 0, gathered[6:7] + tops[0][0:1], 0.0) * known(48)
-    line_a = gathered[6:7] + tops[1][0:1]
-    line_b = gathered[7:8] + tops[2][0:1]
-    total = jnp.where(row8 == 0, line_a, jnp.where(row8 == 1, line_b, 0.0))
-    total = total * known(48)
+    (top,) = early_products(operands, sheets, products)
+    early = jnp.where(row8 == 0, gathered[6:7] + top[0:1], 0.0) * known(48)
     cpl = table[0:16, 0:128]
     lane16 = lanes_of((16, 128))
     row16 = rows_of((16, 128))
@@ -655,6 +682,11 @@
         outer = (index >= 3).astype(jnp.int32) + (index >= 6).astype(jnp.int32)
         return choose(outer, 1.0, a2, b2) * choose(index - 3 * outer, 1.0, a1, b1)
 
+    tops = late_products(operands, sheets, products)
+    line_a = gathered[6:7] + tops[0][0:1]
+    line_b = gathered[7:8] + tops[1][0:1]
+    total = jnp.where(row8 == 0, line_a, jnp.where(row8 == 1, line_b, 0.0))
+    total = total * known(48)
     a3, b3 = weights_of(2, total * both(li) * both(ri))
 
     def last_fields(at, r):
@@ -842,7 +874,7 @@
             out_shape=(shaped((N_FIELDS, 16, CELLS)), shaped((n_space, 16, 128))),
             in_specs=[vmem()] * 3,
             out_specs=(vmem(), vmem()),
-            scratch_shapes=[pltpu.VMEM((384, 128), f32)],
+            scratch_shapes=[pltpu.VMEM((384, 128), f32), pltpu.VMEM((SHEETS, 128), f32)],
             compiler_params=limit(12),
             name="fields",
         )(*near(got, known, constants))
@@ -856,6 +888,7 @@
                 pltpu.VMEM((ROWS, CELLS), bf16),
                 pltpu.VMEM((K, 16), f32),
                 pltpu.VMEM((384, 128), f32),
+                pltpu.VMEM((SHEETS, 128), f32),
                 pltpu.VMEM((48, 128), f32),
                 pltpu.VMEM((16, ROWS), f32),
                 pltpu.SemaphoreType.DMA((ROWS // UPDATE_ROWS + 2,)),

time: 45.5 us -> 45 us (0.989)
  Pallas kernels: 11.9 us -> 11.4 us
where the time goes in v9:
time: 45 us; the launch traced here: 44.6 us
  blocking collectives  18.4 us (41%)
  Pallas kernels  11.4 us (25%)
  starting transfers between devices  9.51 us (21%)
  waiting for transfers between devices  4.61 us (10%)
  between operations  0.66 us (1%)
    all_to_all x1, blocking collectives, per_device(): lax.all_to_all(sent, 'space', split_axis=0, concat_axis=0, tiled=True)  18.4 us
    all_to_all x1, starting transfers between devices, per_device(): got = lax.all_to_all(packed, 'vel', split_axis=0, concat_axis=0, tiled=True)  6.17 us
    pallas_call x1, Pallas kernels, per_device(): pl.pallas_call(lambda *refs: update_kernel(n_space, *refs), out_shape=(st...  5 us
    all_to_all x1, waiting for transfers between devices, per_device(): got = lax.all_to_all(packed, 'vel', split_axis=0, concat_axis=0, tiled=True)  3.6 us
    ppermute x1, starting transfers between devices, per_device(): edges = lax.ppermute(edges, ('space', 'vel'), downwind)  3.34 us
    pallas_call x1, Pallas kernels, per_device(): pl.pallas_call(sums_kernel, out_shape=(shaped((PEERS, 40, 128)), shaped((...  2.47 us
    pallas_call x1, Pallas kernels, per_device(): pl.pallas_call(stream_kernel, out_shape=(shaped((ROWS, CELLS)), shaped((5...  2.25 us
    pallas_call x1, Pallas kernels, per_device(): pl.pallas_call(lambda *refs: fields_kernel(n_space, *refs), out_shape=(sh...  1.7 us
  transfers between devices with their start and end apart: 2, of which 2 were waited for; matrix products, arithmetic and copies ran while one was open for 0% of the time, Pallas kernels for 5%

profile of v9, /device:TPU:2, one launch (start us, length us, event | category | flops | bytes accessed | tf_op | source)
XLA Modules:
  0.0 44.6 jit_solution(5210282348284818537)
XLA Ops:
  0.6 2.5 %sums.1 = (f32[16,40,128]{2,1,0:T(8,128)}, f32[48,128]{1,0:T(8,128)S(1)}) custom-call(bf16[2048,256]{1,0:T(8,128)(2,1)} %dist_in.3, bf16[16,1024]{1,0:T(8,128)(2,1)} %constant.8.clone.p3_in, f32[13,16]{1,0:T(8,128)} %start_in.1), custom_call_target="tpu_custom_call" | custom-call | tf_op jit(solution)/shard_map/sums/pallas_call | solution.py:829
  3.1 6.2 %all-to-all-start = ((f32[16,40,128]{2,1,0:T(8,128)}), f32[16,40,128]{2,1,0:T(8,128)S(1)}, u32[]{:S(2)}, u32[]{:S(2)}) async-start(f32[16,40,128]{2,1,0:T(8,128)} %get-tuple-element.12), calls=%async_computation | async-start | bytes 655360 | tf_op jit(solution)/shard_map/all_to_all | solution.py:844
  9.3 3.3 %collective-permute-start = (f32[48,128]{1,0:T(8,128)S(1)}, f32[48,128]{1,0:T(8,128)S(1)}, u32[]{:S(2)}, u32[]{:S(2)}) collective-permute-start(f32[48,128]{1,0:T(8,128)S(1)} %get-tuple-element.14), channel_id=1, source_target_pairs={{8,24},{9,25},{10,26},{11,27},{12,28},{13,29},{14,30},{15,31},{24,... | collective-permute-start | bytes 73736 | tf_op jit(solution)/shard_map/ppermute | solution.py:849
  12.6 2.3 %stream.1 = (f32[2048,256]{1,0:T(8,128)S(1)}, f32[56,384]{1,0:T(8,128)S(1)}, bf16[1248,256]{1,0:T(8,128)(2,1)S(1)}) custom-call(bf16[2048,256]{1,0:T(8,128)(2,1)} %dist_in.3, bf16[1248,256]{1,0:T(8,128)(2,1)} %constant.9.clone.block_in, f32[32,128]{1,0:T(8,128)} %constant.10.clone.pairs_in, bf16[16,16,128]{2,1,0:T(8,128)(2,1)} %constant.11.clone.own_in, ...), custom_call_target="tpu_custom_call" | custom-call | flops 600000000 | bytes 4000000 | tf_op jit(solution)/shard_map/stream/pallas_call | solution.py:850
  14.9 1.0 %collective-permute-done.refs_5_ = f32[48,128]{1,0:T(8,128)S(1)} collective-permute-done((f32[48,128]{1,0:T(8,128)S(1)}, f32[48,128]{1,0:T(8,128)S(1)}, u32[]{:S(2)}, u32[]{:S(2)}) %collective-permute-start) | collective-permute-done | bytes 24608 | tf_op jit(solution)/shard_map/ppermute | solution.py:849
  15.9 0.0 copy-start
  15.9 3.6 %all-to-all-done.refs_0_ = f32[16,40,128]{2,1,0:T(8,128)S(1)} async-done(((f32[16,40,128]{2,1,0:T(8,128)}), f32[16,40,128]{2,1,0:T(8,128)S(1)}, u32[]{:S(2)}, u32[]{:S(2)}) %all-to-all-start) | async-done | bytes 327712 | tf_op jit(solution)/shard_map/all_to_all | solution.py:844
  19.5 1.7 %fields.1 = (f32[28,16,256]{2,1,0:T(8,128)S(1)}, f32[16,16,128]{2,1,0:T(8,128)S(1)}) custom-call(f32[16,40,128]{2,1,0:T(8,128)S(1)} %all-to-all-done.refs_0_, f32[56,384]{1,0:T(8,128)S(1)} %get-tuple-element.16.refs_1_.refs_2_, bf16[1248,256]{1,0:T(8,128)(2,1)S(1)} %get-tuple-element.17.refs_2_.refs_3_), custom_call_target="tpu_custom_call" | custom-call | tf_op jit(solution)/shard_map/fields/pallas_call | solution.py:872
  21.2 18.4 %all_to_all.10.refs_0_ = f32[16,16,128]{2,1,0:T(8,128)S(1)} all-to-all(f32[16,16,128]{2,1,0:T(8,128)S(1)} %get-tuple-element.18), channel_id=1, replica_groups=mesh['space'=16,'vel'=16] {'space'}, dimensions={0} | all-to-all | bytes 262144 | tf_op jit(solution)/shard_map/all_to_all | solution.py:881
  39.6 0.0 copy-done
  39.6 5.0 %update.1 = (bf16[2048,256]{1,0:T(8,128)(2,1)}, f32[13,16]{1,0:T(8,128)}) custom-call(f32[16,16,128]{2,1,0:T(8,128)S(1)} %all_to_all.10.refs_0_, f32[28,16,256]{2,1,0:T(8,128)S(1)} %get-tuple-element.19.refs_1_, f32[56,384]{1,0:T(8,128)S(1)} %get-tuple-element.16.refs_1_.refs_2_, bf16[1248,256]{1,0:T(8,128)(2,1)S(1)} %get-tuple-element.17.refs_2_.refs_3_, ...), custom_call_target="tpu_custom_call" | custom-call | tf_op jit(solution)/shard_map/update/pallas_call | solution.py:882
Async XLA Ops:
  3.1 16.4 %all-to-all-start = ((f32[16,40,128]{2,1,0:T(8,128)}), f32[16,40,128]{2,1,0:T(8,128)S(1)}, u32[]{:S(2)}, u32[]{:S(2)}) async-start(f32[16,40,128]{2,1,0:T(8,128)} %get-tuple-element.12), calls=%async_computation | async-start | bytes 655360 | tf_op jit(solution)/shard_map/all_to_all | solution.py:844
  9.3 6.6 %collective-permute-start = (f32[48,128]{1,0:T(8,128)S(1)}, f32[48,128]{1,0:T(8,128)S(1)}, u32[]{:S(2)}, u32[]{:S(2)}) collective-permute-start(f32[48,128]{1,0:T(8,128)S(1)} %get-tuple-element.14), channel_id=1, source_target_pairs={{8,24},{9,25},{10,26},{11,27},{12,28},{13,29},{14,30},{15,31},{24,... | collective-permute-start | bytes 73736 | tf_op jit(solution)/shard_map/ppermute | solution.py:849
  15.9 23.7 %copy-start = (f32[48,128]{1,0:T(8,128)}, f32[48,128]{1,0:T(8,128)S(1)}, u32[]{:S(2)}) copy-start(f32[48,128]{1,0:T(8,128)S(1)} %collective-permute-done.refs_5_) | copy-start | bytes 73732

commit v10 on v9

--- a/solution.py
+++ b/solution.py
@@ -182,7 +182,7 @@
     return [(source.at[row, :], target.at[row, :]) for row in rows]
 
 
-def sums_kernel(dist_in, p3_in, start_in, packed, edges, dist, p3, start, padded, sems):
+def sums_kernel(dist_in, p3_in, start_in, packed, edges, dist, p3, start, padded, whole, sems, sends):
     positive = lax.axis_index("vel") >= PEERS // 2
     halves = [pl.ds(u * BLOCK, BLOCK) for u in range(2)]
     pairs = [(p3_in, p3), (start_in, start)] + chunks_of(dist_in, dist)
@@ -193,26 +193,31 @@
     padded[0:K, 0:16] = start[...]
     owned = padded[0:8, :] + pltpu.roll(padded[8:16, :], 16, 1)
     for j in range(PEERS):
-        packed[j, 32:40, :] = owned
+        whole[j, 0:8, :] = owned
     e_lane = lanes_of((16, 128))
     e_row = rows_of((16, 128))
     cell = jnp.where(positive, 127 - e_row, e_row)
     pick = jnp.where((e_lane == cell) & (e_row < 3), 1.0, 0.0).astype(bf16)
     side = pl.multiple_of(jnp.where(positive, 128, 0), 128)
+    going = []
     for u in range(2):
         for n in range(CHUNKS // 2):
             waits[2 + u * (CHUNKS // 2) + n].wait()
         y = jnp.dot(p3[...], dist[halves[u], :], preferred_element_type=f32)
         w = y[0:8] + y[8:16]
         for j in range(PEERS):
-            packed[j, 8 * u : 8 * u + 8, :] = w[:, 0:128]
-            packed[j, 16 + 8 * u : 24 + 8 * u, :] = w[:, 128:256]
+            whole[j, 8 + 16 * u : 16 + 16 * u, :] = w[:, 0:128]
+            whole[j, 16 + 16 * u : 24 + 16 * u, :] = w[:, 128:256]
+        rows = pl.ds(0, 24) if u == 0 else pl.ds(24, 16)
+        going += copies_of([(whole.at[:, rows, :], packed.at[:, rows, :])], sends.at[pl.ds(u, 1)])
         near = dist[halves[u], pl.ds(side, 128)]
         e = lax.dot_general(pick, near, (((1,), (1,)), ((), ())), preferred_element_type=f32)
         for n in range(3):
             for k in range(8):
                 at = 16 * n + 8 * u + k
                 edges[at : at + 1, :] = e[n : n + 1, 128 * k : 128 * k + 128]
+    for copy in going:
+        copy.wait()
 
 
 N_FIELDS = 28
@@ -422,7 +427,11 @@
 def fields_kernel(n_space, got, known, block, fields, sent, table, sheets):
     slab = lax.axis_index("space")
     wide = (16, CELLS)
-    w = jnp.concatenate([got[:, 16 * t : 16 * t + 16, :].reshape(PEERS * 16, 128) for t in range(2)], axis=1)
+    w = [
+        jnp.concatenate([got[:, 8 + 8 * t : 16 + 8 * t, :], got[:, 24 + 8 * t : 32 + 8 * t, :]], axis=1)
+        for t in range(2)
+    ]
+    w = jnp.concatenate([x.reshape(PEERS * 16, 128) for x in w], axis=1)
     wh = w.astype(bf16)
     wm = (w - wh.astype(f32)).astype(bf16)
     y = jnp.dot(block[BLOCK : BLOCK + 224, :], wh, preferred_element_type=f32)
@@ -433,7 +442,7 @@
     lane8 = lanes_of((8, 128))
     parts = [[jnp.zeros((8, 128), f32)] * 2 for _ in range(2)]
     for j in range(PEERS):
-        tile = got[j, 32:40, :]
+        tile = got[j, 0:8, :]
         here = lane8 // 16 == j % 8
         for half in range(2):
             amount = (16 * j - 16 * half) % 128
@@ -828,15 +837,17 @@
         flags = wall_flags.reshape(1, CELLS)
         packed, edges = pl.pallas_call(
             sums_kernel,
-            out_shape=(shaped((PEERS, 40, 128)), shaped((48, 128))),
+            out_shape=(stored((PEERS, 40, 128)), shaped((48, 128))),
             in_specs=[hbm()] * 3,
-            out_specs=(vmem(), vmem()),
+            out_specs=(hbm(), vmem()),
             scratch_shapes=[
                 pltpu.VMEM((ROWS, CELLS), bf16),
                 pltpu.VMEM((16, BLOCK), bf16),
                 pltpu.VMEM((K, 16), f32),
                 pltpu.VMEM((16, 128), f32),
+                pltpu.VMEM((PEERS, 40, 128), f32),
                 pltpu.SemaphoreType.DMA((2 + CHUNKS,)),
+                pltpu.SemaphoreType.DMA((2,)),
             ],
             compiler_params=limit(8),
             name="sums",

time: 45 us -> 44.9 us (level)
  no operation moved by 1% of the time
where the time goes in v10:
time: 44.9 us; the launch traced here: 44.6 us
  blocking collectives  18.4 us (41%)
  Pallas kernels  11.4 us (25%)
  starting transfers between devices  9.51 us (21%)
  waiting for transfers between devices  4.61 us (10%)
  between operations  0.66 us (1%)
    all_to_all x1, blocking collectives, per_device(): lax.all_to_all(sent, 'space', split_axis=0, concat_axis=0, tiled=True)  18.4 us
    all_to_all x1, starting transfers between devices, per_device(): got = lax.all_to_all(packed, 'vel', split_axis=0, concat_axis=0, tiled=True)  6.17 us
    pallas_call x1, Pallas kernels, per_device(): pl.pallas_call(lambda *refs: update_kernel(n_space, *refs), out_shape=(st...  5.01 us
    all_to_all x1, waiting for transfers between devices, per_device(): got = lax.all_to_all(packed, 'vel', split_axis=0, concat_axis=0, tiled=True)  3.6 us
    ppermute x1, starting transfers between devices, per_device(): edges = lax.ppermute(edges, ('space', 'vel'), downwind)  3.34 us
    pallas_call x1, Pallas kernels, per_device(): pl.pallas_call(sums_kernel, out_shape=(stored((PEERS, 40, 128)), shaped((...  2.42 us
    pallas_call x1, Pallas kernels, per_device(): pl.pallas_call(stream_kernel, out_shape=(shaped((ROWS, CELLS)), shaped((5...  2.26 us
    pallas_call x1, Pallas kernels, per_device(): pl.pallas_call(lambda *refs: fields_kernel(n_space, *refs), out_shape=(sh...  1.69 us
  transfers between devices with their start and end apart: 2, of which 2 were waited for; matrix products, arithmetic and copies ran while one was open for 0% of the time, Pallas kernels for 5%

profile of v10, /device:TPU:2, one launch (start us, length us, event | category | flops | bytes accessed | tf_op | source)
XLA Modules:
  0.0 44.6 jit_solution(11873224528304583365)
XLA Ops:
  0.6 2.4 %sums.1 = (f32[16,40,128]{2,1,0:T(8,128)}, f32[48,128]{1,0:T(8,128)S(1)}) custom-call(bf16[2048,256]{1,0:T(8,128)(2,1)} %dist_in.3, bf16[16,1024]{1,0:T(8,128)(2,1)} %constant.8.clone.p3_in, f32[13,16]{1,0:T(8,128)} %start_in.1), custom_call_target="tpu_custom_call" | custom-call | tf_op jit(solution)/shard_map/sums/pallas_call | solution.py:838
  3.1 6.2 %all-to-all-start = ((f32[16,40,128]{2,1,0:T(8,128)}), f32[16,40,128]{2,1,0:T(8,128)S(1)}, u32[]{:S(2)}, u32[]{:S(2)}) async-start(f32[16,40,128]{2,1,0:T(8,128)} %get-tuple-element.12), calls=%async_computation | async-start | bytes 655360 | tf_op jit(solution)/shard_map/all_to_all | solution.py:855
  9.2 3.3 %collective-permute-start = (f32[48,128]{1,0:T(8,128)S(1)}, f32[48,128]{1,0:T(8,128)S(1)}, u32[]{:S(2)}, u32[]{:S(2)}) collective-permute-start(f32[48,128]{1,0:T(8,128)S(1)} %get-tuple-element.14), channel_id=1, source_target_pairs={{8,24},{9,25},{10,26},{11,27},{12,28},{13,29},{14,30},{15,31},{24,... | collective-permute-start | bytes 73736 | tf_op jit(solution)/shard_map/ppermute | solution.py:860
  12.6 2.3 %stream.1 = (f32[2048,256]{1,0:T(8,128)S(1)}, f32[56,384]{1,0:T(8,128)S(1)}, bf16[1248,256]{1,0:T(8,128)(2,1)S(1)}) custom-call(bf16[2048,256]{1,0:T(8,128)(2,1)} %dist_in.3, bf16[1248,256]{1,0:T(8,128)(2,1)} %constant.9.clone.block_in, f32[32,128]{1,0:T(8,128)} %constant.10.clone.pairs_in, bf16[16,16,128]{2,1,0:T(8,128)(2,1)} %constant.11.clone.own_in, ...), custom_call_target="tpu_custom_call" | custom-call | flops 600000000 | bytes 4000000 | tf_op jit(solution)/shard_map/stream/pallas_call | solution.py:861
  14.8 1.0 %collective-permute-done.refs_5_ = f32[48,128]{1,0:T(8,128)S(1)} collective-permute-done((f32[48,128]{1,0:T(8,128)S(1)}, f32[48,128]{1,0:T(8,128)S(1)}, u32[]{:S(2)}, u32[]{:S(2)}) %collective-permute-start) | collective-permute-done | bytes 24608 | tf_op jit(solution)/shard_map/ppermute | solution.py:860
  15.8 0.0 copy-start
  15.9 3.6 %all-to-all-done.refs_0_ = f32[16,40,128]{2,1,0:T(8,128)S(1)} async-done(((f32[16,40,128]{2,1,0:T(8,128)}), f32[16,40,128]{2,1,0:T(8,128)S(1)}, u32[]{:S(2)}, u32[]{:S(2)}) %all-to-all-start) | async-done | bytes 327712 | tf_op jit(solution)/shard_map/all_to_all | solution.py:855
  19.5 1.7 %fields.1 = (f32[28,16,256]{2,1,0:T(8,128)S(1)}, f32[16,16,128]{2,1,0:T(8,128)S(1)}) custom-call(f32[16,40,128]{2,1,0:T(8,128)S(1)} %all-to-all-done.refs_0_, f32[56,384]{1,0:T(8,128)S(1)} %get-tuple-element.16.refs_1_.refs_2_, bf16[1248,256]{1,0:T(8,128)(2,1)S(1)} %get-tuple-element.17.refs_2_.refs_3_), custom_call_target="tpu_custom_call" | custom-call | tf_op jit(solution)/shard_map/fields/pallas_call | solution.py:883
  21.1 18.4 %all_to_all.10.refs_0_ = f32[16,16,128]{2,1,0:T(8,128)S(1)} all-to-all(f32[16,16,128]{2,1,0:T(8,128)S(1)} %get-tuple-element.18), channel_id=1, replica_groups=mesh['space'=16,'vel'=16] {'space'}, dimensions={0} | all-to-all | bytes 262144 | tf_op jit(solution)/shard_map/all_to_all | solution.py:892
  39.6 0.0 copy-done
  39.6 5.0 %update.1 = (bf16[2048,256]{1,0:T(8,128)(2,1)}, f32[13,16]{1,0:T(8,128)}) custom-call(f32[16,16,128]{2,1,0:T(8,128)S(1)} %all_to_all.10.refs_0_, f32[28,16,256]{2,1,0:T(8,128)S(1)} %get-tuple-element.19.refs_1_, f32[56,384]{1,0:T(8,128)S(1)} %get-tuple-element.16.refs_1_.refs_2_, bf16[1248,256]{1,0:T(8,128)(2,1)S(1)} %get-tuple-element.17.refs_2_.refs_3_, ...), custom_call_target="tpu_custom_call" | custom-call | tf_op jit(solution)/shard_map/update/pallas_call | solution.py:893
Async XLA Ops:
  3.1 16.4 %all-to-all-start = ((f32[16,40,128]{2,1,0:T(8,128)}), f32[16,40,128]{2,1,0:T(8,128)S(1)}, u32[]{:S(2)}, u32[]{:S(2)}) async-start(f32[16,40,128]{2,1,0:T(8,128)} %get-tuple-element.12), calls=%async_computation | async-start | bytes 655360 | tf_op jit(solution)/shard_map/all_to_all | solution.py:855
  9.2 6.6 %collective-permute-start = (f32[48,128]{1,0:T(8,128)S(1)}, f32[48,128]{1,0:T(8,128)S(1)}, u32[]{:S(2)}, u32[]{:S(2)}) collective-permute-start(f32[48,128]{1,0:T(8,128)S(1)} %get-tuple-element.14), channel_id=1, source_target_pairs={{8,24},{9,25},{10,26},{11,27},{12,28},{13,29},{14,30},{15,31},{24,... | collective-permute-start | bytes 73736 | tf_op jit(solution)/shard_map/ppermute | solution.py:860
  15.8 23.7 %copy-start = (f32[48,128]{1,0:T(8,128)}, f32[48,128]{1,0:T(8,128)S(1)}, u32[]{:S(2)}) copy-start(f32[48,128]{1,0:T(8,128)S(1)} %collective-permute-done.refs_5_) | copy-start | bytes 73732

commit v11 on v10

--- a/solution.py
+++ b/solution.py
@@ -403,17 +403,17 @@
         while len(rows) > 1:
             rows = [p + q for p, q in zip(rows[0::2], rows[1::2])]
         table[n : n + 8, :] = rows[0]
-    ones = jnp.ones((8, 128), f32)
-    return [
-        lax.dot_general(
-            ones,
-            table[128 * n : 128 * n + 128, :],
-            (((1,), (1,)), ((), ())),
-            precision=lax.Precision.HIGHEST,
-            preferred_element_type=f32,
-        )
-        for n in range(lines)
-    ]
+    ones = jnp.ones((8, 3 * 128), bf16)
+    out = []
+    for n in range(lines):
+        x = table[128 * n : 128 * n + 128, :]
+        h = x.astype(bf16)
+        rest = x - h.astype(f32)
+        m = rest.astype(bf16)
+        low = (rest - m.astype(f32)).astype(bf16)
+        x = jnp.concatenate([h, m, low], axis=1)
+        out.append(lax.dot_general(ones, x, (((1,), (1,)), ((), ())), preferred_element_type=f32))
+    return out
 
 
 def early_products(operands, sheets, table):

time: 44.9 us -> 45 us (level)
  no operation moved by 1% of the time
where the time goes in v11:
time: 45 us; the launch traced here: 44.7 us
  blocking collectives  18.4 us (41%)
  Pallas kernels  11.5 us (26%)
  starting transfers between devices  9.51 us (21%)
  waiting for transfers between devices  4.61 us (10%)
  between operations  0.66 us (1%)
    all_to_all x1, blocking collectives, per_device(): lax.all_to_all(sent, 'space', split_axis=0, concat_axis=0, tiled=True)  18.4 us
    all_to_all x1, starting transfers between devices, per_device(): got = lax.all_to_all(packed, 'vel', split_axis=0, concat_axis=0, tiled=True)  6.17 us
    pallas_call x1, Pallas kernels, per_device(): pl.pallas_call(lambda *refs: update_kernel(n_space, *refs), out_shape=(st...  5.15 us
    all_to_all x1, waiting for transfers between devices, per_device(): got = lax.all_to_all(packed, 'vel', split_axis=0, concat_axis=0, tiled=True)  3.6 us
    ppermute x1, starting transfers between devices, per_device(): edges = lax.ppermute(edges, ('space', 'vel'), downwind)  3.34 us
    pallas_call x1, Pallas kernels, per_device(): pl.pallas_call(sums_kernel, out_shape=(stored((PEERS, 40, 128)), shaped((...  2.42 us
    pallas_call x1, Pallas kernels, per_device(): pl.pallas_call(stream_kernel, out_shape=(shaped((ROWS, CELLS)), shaped((5...  2.26 us
    pallas_call x1, Pallas kernels, per_device(): pl.pallas_call(lambda *refs: fields_kernel(n_space, *refs), out_shape=(sh...  1.65 us
  transfers between devices with their start and end apart: 2, of which 2 were waited for; matrix products, arithmetic and copies ran while one was open for 0% of the time, Pallas kernels for 5%

profile of v11, /device:TPU:2, one launch (start us, length us, event | category | flops | bytes accessed | tf_op | source)
XLA Modules:
  0.0 44.7 jit_solution(7277303082056871362)
XLA Ops:
  0.6 2.4 %sums.1 = (f32[16,40,128]{2,1,0:T(8,128)}, f32[48,128]{1,0:T(8,128)S(1)}) custom-call(bf16[2048,256]{1,0:T(8,128)(2,1)} %dist_in.3, bf16[16,1024]{1,0:T(8,128)(2,1)} %constant.8.clone.p3_in, f32[13,16]{1,0:T(8,128)} %start_in.1), custom_call_target="tpu_custom_call" | custom-call | tf_op jit(solution)/shard_map/sums/pallas_call | solution.py:838
  3.1 6.2 %all-to-all-start = ((f32[16,40,128]{2,1,0:T(8,128)}), f32[16,40,128]{2,1,0:T(8,128)S(1)}, u32[]{:S(2)}, u32[]{:S(2)}) async-start(f32[16,40,128]{2,1,0:T(8,128)} %get-tuple-element.12), calls=%async_computation | async-start | bytes 655360 | tf_op jit(solution)/shard_map/all_to_all | solution.py:855
  9.2 3.3 %collective-permute-start = (f32[48,128]{1,0:T(8,128)S(1)}, f32[48,128]{1,0:T(8,128)S(1)}, u32[]{:S(2)}, u32[]{:S(2)}) collective-permute-start(f32[48,128]{1,0:T(8,128)S(1)} %get-tuple-element.14), channel_id=1, source_target_pairs={{8,24},{9,25},{10,26},{11,27},{12,28},{13,29},{14,30},{15,31},{24,... | collective-permute-start | bytes 73736 | tf_op jit(solution)/shard_map/ppermute | solution.py:860
  12.6 2.3 %stream.1 = (f32[2048,256]{1,0:T(8,128)S(1)}, f32[56,384]{1,0:T(8,128)S(1)}, bf16[1248,256]{1,0:T(8,128)(2,1)S(1)}) custom-call(bf16[2048,256]{1,0:T(8,128)(2,1)} %dist_in.3, bf16[1248,256]{1,0:T(8,128)(2,1)} %constant.9.clone.block_in, f32[32,128]{1,0:T(8,128)} %constant.10.clone.pairs_in, bf16[16,16,128]{2,1,0:T(8,128)(2,1)} %constant.11.clone.own_in, ...), custom_call_target="tpu_custom_call" | custom-call | flops 600000000 | bytes 4000000 | tf_op jit(solution)/shard_map/stream/pallas_call | solution.py:861
  14.8 1.0 %collective-permute-done.refs_5_ = f32[48,128]{1,0:T(8,128)S(1)} collective-permute-done((f32[48,128]{1,0:T(8,128)S(1)}, f32[48,128]{1,0:T(8,128)S(1)}, u32[]{:S(2)}, u32[]{:S(2)}) %collective-permute-start) | collective-permute-done | bytes 24608 | tf_op jit(solution)/shard_map/ppermute | solution.py:860
  15.8 0.0 copy-start
  15.9 3.6 %all-to-all-done.refs_0_ = f32[16,40,128]{2,1,0:T(8,128)S(1)} async-done(((f32[16,40,128]{2,1,0:T(8,128)}), f32[16,40,128]{2,1,0:T(8,128)S(1)}, u32[]{:S(2)}, u32[]{:S(2)}) %all-to-all-start) | async-done | bytes 327712 | tf_op jit(solution)/shard_map/all_to_all | solution.py:855
  19.5 1.7 %fields.1 = (f32[28,16,256]{2,1,0:T(8,128)S(1)}, f32[16,16,128]{2,1,0:T(8,128)S(1)}) custom-call(f32[16,40,128]{2,1,0:T(8,128)S(1)} %all-to-all-done.refs_0_, f32[56,384]{1,0:T(8,128)S(1)} %get-tuple-element.16.refs_1_.refs_2_, bf16[1248,256]{1,0:T(8,128)(2,1)S(1)} %get-tuple-element.17.refs_2_.refs_3_), custom_call_target="tpu_custom_call" | custom-call | tf_op jit(solution)/shard_map/fields/pallas_call | solution.py:883
  21.1 18.4 %all_to_all.10.refs_0_ = f32[16,16,128]{2,1,0:T(8,128)S(1)} all-to-all(f32[16,16,128]{2,1,0:T(8,128)S(1)} %get-tuple-element.18), channel_id=1, replica_groups=mesh['space'=16,'vel'=16] {'space'}, dimensions={0} | all-to-all | bytes 262144 | tf_op jit(solution)/shard_map/all_to_all | solution.py:892
  39.5 0.0 copy-done
  39.5 5.2 %update.1 = (bf16[2048,256]{1,0:T(8,128)(2,1)}, f32[13,16]{1,0:T(8,128)}) custom-call(f32[16,16,128]{2,1,0:T(8,128)S(1)} %all_to_all.10.refs_0_, f32[28,16,256]{2,1,0:T(8,128)S(1)} %get-tuple-element.19.refs_1_, f32[56,384]{1,0:T(8,128)S(1)} %get-tuple-element.16.refs_1_.refs_2_, bf16[1248,256]{1,0:T(8,128)(2,1)S(1)} %get-tuple-element.17.refs_2_.refs_3_, ...), custom_call_target="tpu_custom_call" | custom-call | tf_op jit(solution)/shard_map/update/pallas_call | solution.py:893
Async XLA Ops:
  3.1 16.4 %all-to-all-start = ((f32[16,40,128]{2,1,0:T(8,128)}), f32[16,40,128]{2,1,0:T(8,128)S(1)}, u32[]{:S(2)}, u32[]{:S(2)}) async-start(f32[16,40,128]{2,1,0:T(8,128)} %get-tuple-element.12), calls=%async_computation | async-start | bytes 655360 | tf_op jit(solution)/shard_map/all_to_all | solution.py:855
  9.2 6.6 %collective-permute-start = (f32[48,128]{1,0:T(8,128)S(1)}, f32[48,128]{1,0:T(8,128)S(1)}, u32[]{:S(2)}, u32[]{:S(2)}) collective-permute-start(f32[48,128]{1,0:T(8,128)S(1)} %get-tuple-element.14), channel_id=1, source_target_pairs={{8,24},{9,25},{10,26},{11,27},{12,28},{13,29},{14,30},{15,31},{24,... | collective-permute-start | bytes 73736 | tf_op jit(solution)/shard_map/ppermute | solution.py:860
  15.8 23.7 %copy-start = (f32[48,128]{1,0:T(8,128)}, f32[48,128]{1,0:T(8,128)S(1)}, u32[]{:S(2)}) copy-start(f32[48,128]{1,0:T(8,128)S(1)} %collective-permute-done.refs_5_) | copy-start | bytes 73732
